TPU v7x, 32 devices: a whole 2x2x4 slice. The times are simulated.
32 devices in a mesh: fsdp: 4 (over y, x), ctx: 4 (over z), tp: 2 (over core).
Axes of the slice: x: 2, y: 2, z: 4, core: 2. Of those that a mesh axis runs over, the one named last changes fastest.
Arguments:
- tokens: bfloat16 [2, 2048, 1536], P(None, ('fsdp', 'ctx')), may hold values from -6 to 6
- gain_attn: bfloat16 [1536], P('fsdp'), may hold values from 0.5 to 1.5
- w_query: bfloat16 [1536, 1536], P('fsdp', 'tp'), may hold values from -0.15625 to 0.15625
- key_projection_weight: bfloat16 [1536, 256], P('fsdp', 'tp'), may hold values from -0.15625 to 0.15625
- value_projection_weight: bfloat16 [1536, 256], P('fsdp', 'tp'), may hold values from -0.15625 to 0.15625
- w_output: bfloat16 [1536, 1536], P('tp', 'fsdp'), may hold values from -1.25 to 1.25
- gain_mlp: bfloat16 [1536], P('fsdp'), may hold values from 0.5 to 1.5
- w_router: bfloat16 [1536, 8], P('fsdp'), may hold values from -0.078125 to 0.078125
- w_gate: bfloat16 [8, 1536, 768], P(None, 'fsdp', 'tp'), may hold values from -0.15625 to 0.15625
- w_up: bfloat16 [8, 1536, 768], P(None, 'fsdp', 'tp'), may hold values from -0.15625 to 0.15625
- w_down: bfloat16 [8, 768, 1536], P(None, 'tp', 'fsdp'), may hold values from -0.875 to 0.875
- lineage: int32 [2, 3, 2048], replicated, may hold values from -1 to 13, as said below
- expert_ids: int32 [2, 2048, 4], P(None, ('fsdp', 'ctx')), may hold values from 0 to 7, all different within a row; in each aligned block of 128 rows (0 to 127, 128 to 255, ..., all dimensions but the last counted through in order) at most 96 rows name the same one
- cotangent: bfloat16 [2, 2048, 1536], P(None, ('fsdp', 'ctx')), may hold values from -6 to 6
Outputs:
- output: bfloat16 [2, 2048, 1536], P(None, ('fsdp', 'ctx'))
- input_grad: float32 [2, 2048, 1536], P(None, ('fsdp', 'ctx'))
- grad_gain_attn: float32 [1536], P('fsdp')
- grad_w_query: float32 [1536, 1536], P('fsdp', 'tp')
- grad_w_key: float32 [1536, 256], P('fsdp', 'tp')
- grad_w_value: float32 [1536, 256], P('fsdp', 'tp')
- grad_w_output: float32 [1536, 1536], P('tp', 'fsdp')
- grad_gain_mlp: float32 [1536], P('fsdp')
- grad_w_router: float32 [1536, 8], P('fsdp')
- grad_w_gate: float32 [8, 1536, 768], P(None, 'fsdp', 'tp')
- grad_w_up: float32 [8, 1536, 768], P(None, 'fsdp', 'tp')
- grad_w_down: float32 [8, 768, 1536], P(None, 'tp', 'fsdp')
Inputs may be any that keep to these rules, and one draw needn't show every extreme that they name: `lineage`: in each micro-batch row 0 gives each slot's segment, rows 1 and 2 the segments of its parent and grandparent, -1 where there is none. Segments are contiguous runs of slots; a parent's slots precede its children's. A micro-batch holds a tree of a trunk, four branches and two leaves on each branch, and a tree that is only a trunk. `expert_ids`: among the 128 tokens of one device (aligned blocks of the slots of a micro-batch), no expert is named by more than 96 tokens, a bound that some block reaches.
All inputs are finite; a program needn't handle non-finite values.
Results may differ from a plain program's by a relative error of at most 0.024.
Values may be sent and summed in bfloat16 or wider, within the bound.
No kernel may reach another device: no remote copies, remote signals or barrier semaphores. Data moves between devices by JAX's collectives and lax.ppermute only.
A program may use at most 136 MiB of HBM per device.

v0:
```python
import jax
import jax.numpy as jnp
from jax import lax
from jax.sharding import PartitionSpec as P

HEAD_SIZE = 128
CAP = 96
KEY_BLOCK = 1024


EPSILON = 1e-06
ROPE_BASE = 1000000.0
NEG_FILL = -1e30


def normed(values, gain):
    return values * lax.rsqrt(jnp.mean(values * values, -1, keepdims=True) + EPSILON) * gain


def rotary_embedding(values, tree_positions):
    half_dim = values.shape[-1] // 2
    frequency = ROPE_BASE ** (-jnp.arange(half_dim, dtype=jnp.float32) / half_dim)
    angles = tree_positions[:, None] * frequency[None, :]
    cosine = jnp.cos(angles)[:, None, :]
    sine_val = jnp.sin(angles)[:, None, :]
    first_half = values[..., :half_dim]
    second_half = values[..., half_dim:]
    return jnp.concatenate(
        [
            first_half * cosine - second_half * sine_val,
            second_half * cosine + first_half * sine_val,
        ],
        -1,
    )


def allowed(query_lin, query_index, key_owner, key_index):
    same_seg = (key_owner[None, :] == query_lin[0][:, None]) & (
        key_index[None, :] <= query_index[:, None]
    )
    return (
        same_seg
        | (key_owner[None, :] == query_lin[1][:, None])
        | (key_owner[None, :] == query_lin[2][:, None])
    )


def micro_step(gathered, tokens_mb, lineage_mb, route_ids, cotangent_mb, first_row):
    (
        g_attn,
        query_mat,
        key_mat,
        value_mat,
        output_mat,
        g_mlp,
        router_mat,
        gate_mats,
        up_mats,
        down_mats,
    ) = gathered
    f32 = jnp.float32
    bf16 = jnp.bfloat16
    tok_rows = tokens_mb.shape[0]
    expert_slot_total = lineage_mb.shape[1]
    block_count = expert_slot_total // KEY_BLOCK
    scale_factor = HEAD_SIZE ** (-0.5)
    query_index = first_row + jnp.arange(tok_rows, dtype=jnp.int32)
    key_index = jnp.arange(expert_slot_total, dtype=jnp.int32)
    query_lin = lax.dynamic_slice_in_dim(lineage_mb, first_row, tok_rows, 1)
    key_owner = lineage_mb[0]
    tree_positions = (
        jnp.sum(allowed(query_lin, query_index, key_owner, key_index).astype(jnp.int32), -1) - 1
    ).astype(f32)
    tokens_in = tokens_mb.astype(f32)
    gain_one = g_attn.astype(f32)
    normalized_input = normed(tokens_in, gain_one).astype(bf16)
    head_count = query_mat.shape[1] // HEAD_SIZE
    query_pre = jnp.dot(normalized_input, query_mat, preferred_element_type=f32).reshape(
        tok_rows, head_count, HEAD_SIZE
    )
    key_before_rotation = jnp.dot(normalized_input, key_mat, preferred_element_type=f32).reshape(
        tok_rows, 1, HEAD_SIZE
    )
    value_own = jnp.dot(normalized_input, value_mat, preferred_element_type=f32).astype(bf16)
    query_rows = rotary_embedding(query_pre, tree_positions).astype(bf16)
    keys_own = (
        rotary_embedding(key_before_rotation, tree_positions)
        .reshape(tok_rows, HEAD_SIZE)
        .astype(bf16)
    )
    keys_all, values_all = (
        lax.all_gather(keys_own, ("fsdp", "ctx"), axis=0, tiled=True),
        lax.all_gather(value_own, ("fsdp", "ctx"), axis=0, tiled=True),
    )
    key_blocks = keys_all.reshape(block_count, KEY_BLOCK, HEAD_SIZE)
    value_blocks = values_all.reshape(block_count, KEY_BLOCK, HEAD_SIZE)
    owner_blocks = key_owner.reshape(block_count, KEY_BLOCK)
    index_blocks = key_index.reshape(block_count, KEY_BLOCK)

    def scores_of(key_piece, owner_piece, index_piece):
        raw_scores = (
            jnp.einsum("qhd,kd->qhk", query_rows, key_piece, preferred_element_type=f32)
            * scale_factor
        )
        visible = allowed(query_lin, query_index, owner_piece, index_piece)
        return jnp.where(visible[:, None, :], raw_scores, NEG_FILL)

    def online_step(carried, pieces):
        run_max, run_sum, run_acc = carried
        key_piece, value_piece, owner_piece, index_piece = pieces
        scores = scores_of(key_piece, owner_piece, index_piece)
        new_max = jnp.maximum(run_max, jnp.max(scores, -1))
        rescale = jnp.exp(run_max - new_max)
        exp_scores = jnp.exp(scores - new_max[..., None])
        run_sum = run_sum * rescale + jnp.sum(exp_scores, -1)
        run_acc = run_acc * rescale[..., None] + jnp.einsum(
            "qhk,kd->qhd", exp_scores.astype(bf16), value_piece, preferred_element_type=f32
        )
        return ((new_max, run_sum, run_acc), None)

    initial = (
        jnp.full((tok_rows, head_count), NEG_FILL, f32),
        jnp.zeros((tok_rows, head_count), f32),
        jnp.zeros((tok_rows, head_count, HEAD_SIZE), f32),
    )
    (row_max, row_sum, run_acc), unused = lax.scan(
        online_step, initial, (key_blocks, value_blocks, owner_blocks, index_blocks)
    )
    log_total = row_max + jnp.log(row_sum)
    attended = run_acc / row_sum[..., None]

    def probs_of(key_piece, owner_piece, index_piece):
        return jnp.exp(scores_of(key_piece, owner_piece, index_piece) - log_total[..., None])

    attended_low = attended.reshape(tok_rows, head_count * HEAD_SIZE).astype(bf16)
    branch = lax.psum(
        jnp.dot(attended_low, output_mat, preferred_element_type=f32).astype(jnp.bfloat16), "tp"
    ).astype(jnp.float32)
    middle = tokens_in + branch
    gain_two = g_mlp.astype(f32)
    mixed_in = normed(middle, gain_two).astype(bf16)
    logits = jnp.dot(mixed_in, router_mat, preferred_element_type=f32)
    router_exp = jnp.exp(logits - jnp.max(logits, -1, keepdims=True))
    router_probs = router_exp / jnp.sum(router_exp, -1, keepdims=True)
    expert_count = router_mat.shape[1]
    topk_count = route_ids.shape[1]
    chosen = (
        route_ids[:, :, None] == jnp.arange(expert_count, dtype=jnp.int32)[None, None, :]
    ).astype(f32)
    gate_share = jnp.sum(chosen * router_probs[:, None, :], -1)
    flat_ids = route_ids.reshape(-1)
    route_count = flat_ids.shape[0]
    picked = (flat_ids[:, None] == jnp.arange(expert_count, dtype=jnp.int32)[None, :]).astype(
        jnp.int32
    )
    before = jnp.cumsum(picked, 0) - picked
    slot_of = flat_ids * CAP + jnp.sum(before * picked, 1)
    slot_total = expert_count * CAP
    matches = (slot_of[None, :] == jnp.arange(slot_total, dtype=jnp.int32)[:, None]).astype(
        jnp.int32
    )
    source = jnp.sum(matches * jnp.arange(route_count, dtype=jnp.int32)[None, :], 1)
    filled = jnp.sum(matches, 1) > 0
    source_tok = source // topk_count
    slot_in = jnp.where(filled[:, None], mixed_in[source_tok], 0).reshape(expert_count, CAP, -1)
    gate_val = jnp.einsum("ecd,edf->ecf", slot_in, gate_mats, preferred_element_type=f32)
    up_val = jnp.einsum("ecd,edf->ecf", slot_in, up_mats, preferred_element_type=f32)
    activated, gelu_back = jax.vjp(jax.nn.gelu, gate_val)
    hidden = (activated * up_val).astype(bf16)
    slot_out = jnp.einsum("ecf,efd->ecd", hidden, down_mats, preferred_element_type=f32).reshape(
        slot_total, -1
    )
    route_out = slot_out[slot_of].reshape(tok_rows, topk_count, -1)
    expert_part = jnp.sum(gate_share[..., None] * route_out, 1)
    expert_mix = lax.psum(expert_part.astype(jnp.bfloat16), "tp").astype(jnp.float32)
    result = (middle + expert_mix).astype(bf16)
    grad_out = cotangent_mb.astype(f32)
    route_grad = (
        (gate_share[..., None] * grad_out[:, None, :]).astype(bf16).reshape(route_count, -1)
    )
    slot_grad = jnp.where(filled[:, None], route_grad[source], 0).reshape(expert_count, CAP, -1)
    gate_part = jnp.sum(grad_out[:, None, :] * route_out, -1)
    grad_down = jnp.einsum("ecf,ecd->efd", hidden, slot_grad, preferred_element_type=f32)
    hidden_grad = jnp.einsum("ecd,efd->ecf", slot_grad, down_mats, preferred_element_type=f32)
    gate_grad = gelu_back(hidden_grad * up_val)[0].astype(bf16)
    up_grad = (hidden_grad * activated).astype(bf16)
    grad_gate = jnp.einsum("ecd,ecf->edf", slot_in, gate_grad, preferred_element_type=f32)
    grad_up = jnp.einsum("ecd,ecf->edf", slot_in, up_grad, preferred_element_type=f32)
    slot_back = jnp.einsum("ecf,edf->ecd", gate_grad, gate_mats, preferred_element_type=f32)
    slot_back = (
        slot_back + jnp.einsum("ecf,edf->ecd", up_grad, up_mats, preferred_element_type=f32)
    ).reshape(slot_total, -1)
    route_back = jnp.sum(slot_back[slot_of].reshape(tok_rows, topk_count, -1), 1)
    mixed_grad, share_grad = (
        lax.psum(route_back.astype(jnp.bfloat16), "tp").astype(jnp.float32),
        lax.psum(gate_part.astype(jnp.bfloat16), "tp").astype(jnp.float32),
    )
    prob_grad = jnp.sum(chosen * share_grad[..., None], 1)
    logit_grad = router_probs * (prob_grad - jnp.sum(router_probs * prob_grad, -1, keepdims=True))
    grad_router = jnp.einsum(
        "td,te->de", mixed_in.astype(f32), logit_grad, precision=lax.Precision.HIGHEST
    )
    mixed_grad = mixed_grad + jnp.einsum(
        "te,de->td", logit_grad, router_mat.astype(f32), precision=lax.Precision.HIGHEST
    )
    unused_two, norm_two_back = jax.vjp(normed, middle, gain_two)
    middle_norm_grad, grad_gain_two = norm_two_back(mixed_grad)
    middle_grad = grad_out + middle_norm_grad
    branch_grad = middle_grad.astype(bf16)
    grad_output = jnp.einsum("tf,td->fd", attended_low, branch_grad, preferred_element_type=f32)
    attended_grad = (
        jnp.einsum("td,fd->tf", branch_grad, output_mat, preferred_element_type=f32)
        .astype(bf16)
        .reshape(tok_rows, head_count, HEAD_SIZE)
    )
    delta_sum = jnp.sum(attended_grad.astype(f32) * attended, -1)

    def grad_step(carried, pieces):
        key_piece, value_piece, owner_piece, index_piece = pieces
        soft_probs = probs_of(key_piece, owner_piece, index_piece)
        dot_grad = jnp.einsum("qhd,kd->qhk", attended_grad, value_piece, preferred_element_type=f32)
        score_grad = (soft_probs * (dot_grad - delta_sum[..., None])).astype(bf16)
        query_grad = (
            carried
            + jnp.einsum("qhk,kd->qhd", score_grad, key_piece, preferred_element_type=f32)
            * scale_factor
        )
        key_grad = (
            jnp.einsum("qhk,qhd->kd", score_grad, query_rows, preferred_element_type=f32)
            * scale_factor
        )
        value_grad = jnp.einsum(
            "qhk,qhd->kd", soft_probs.astype(bf16), attended_grad, preferred_element_type=f32
        )
        return (query_grad, (key_grad, value_grad))

    query_grad, (key_grads, value_grads) = lax.scan(
        grad_step,
        jnp.zeros((tok_rows, head_count, HEAD_SIZE), f32),
        (key_blocks, value_blocks, owner_blocks, index_blocks),
    )
    key_sum, value_sum = (
        lax.psum_scatter(
            key_grads.reshape(expert_slot_total, HEAD_SIZE),
            ("fsdp", "ctx"),
            scatter_dimension=0,
            tiled=True,
        ),
        lax.psum_scatter(
            value_grads.reshape(expert_slot_total, HEAD_SIZE),
            ("fsdp", "ctx"),
            scatter_dimension=0,
            tiled=True,
        ),
    )
    unused_query, rope_query_back = jax.vjp(
        lambda values: rotary_embedding(values, tree_positions), query_pre
    )
    unused_key, rope_key_back = jax.vjp(
        lambda values: rotary_embedding(values, tree_positions), key_before_rotation
    )
    query_pre_grad = (
        rope_query_back(query_grad)[0].reshape(tok_rows, head_count * HEAD_SIZE).astype(bf16)
    )
    key_pre_grad = (
        rope_key_back(key_sum.reshape(tok_rows, 1, HEAD_SIZE))[0]
        .reshape(tok_rows, HEAD_SIZE)
        .astype(bf16)
    )
    value_pre_grad = value_sum.astype(bf16)
    grad_query = jnp.einsum(
        "td,tf->df", normalized_input, query_pre_grad, preferred_element_type=f32
    )
    grad_key = jnp.einsum("td,tf->df", normalized_input, key_pre_grad, preferred_element_type=f32)
    grad_value = jnp.einsum(
        "td,tf->df", normalized_input, value_pre_grad, preferred_element_type=f32
    )
    normed_part = jnp.einsum("tf,df->td", query_pre_grad, query_mat, preferred_element_type=f32)
    normed_part = normed_part + jnp.einsum(
        "tf,df->td", key_pre_grad, key_mat, preferred_element_type=f32
    )
    normed_part = normed_part + jnp.einsum(
        "tf,df->td", value_pre_grad, value_mat, preferred_element_type=f32
    )
    normed_grad = lax.psum(normed_part.astype(jnp.bfloat16), "tp").astype(jnp.float32)
    unused_one, norm_one_back = jax.vjp(normed, tokens_in, gain_one)
    token_norm_grad, grad_gain_one = norm_one_back(normed_grad)
    input_grad = middle_grad + token_norm_grad
    grad_list = (
        grad_gain_one,
        grad_query,
        grad_key,
        grad_value,
        grad_output,
        grad_gain_two,
        grad_router,
        grad_gate,
        grad_up,
        grad_down,
    )
    return (result, input_grad, grad_list)


def local(
    tokens,
    gain_attn,
    w_query,
    key_projection_weight,
    value_projection_weight,
    w_output,
    gain_mlp,
    w_router,
    w_gate,
    w_up,
    w_down,
    lineage,
    expert_ids,
    cotangent,
):
    micro_count = tokens.shape[0]
    tok_rows = tokens.shape[1]
    first_row = lax.axis_index(("fsdp", "ctx")) * tok_rows
    outputs = []
    input_grads = []
    running = None
    for batch_index in range(micro_count):
        gathered = (
            lax.all_gather(gain_attn, "fsdp", axis=0, tiled=True),
            lax.all_gather(w_query, "fsdp", axis=0, tiled=True),
            lax.all_gather(key_projection_weight, "fsdp", axis=0, tiled=True),
            lax.all_gather(value_projection_weight, "fsdp", axis=0, tiled=True),
            lax.all_gather(w_output, "fsdp", axis=1, tiled=True),
            lax.all_gather(gain_mlp, "fsdp", axis=0, tiled=True),
            lax.all_gather(w_router, "fsdp", axis=0, tiled=True),
            lax.all_gather(w_gate, "fsdp", axis=1, tiled=True),
            lax.all_gather(w_up, "fsdp", axis=1, tiled=True),
            lax.all_gather(w_down, "fsdp", axis=2, tiled=True),
        )
        result, input_grad, grad_list = micro_step(
            gathered,
            tokens[batch_index],
            lineage[batch_index],
            expert_ids[batch_index],
            cotangent[batch_index],
            first_row,
        )
        outputs.append(result)
        input_grads.append(input_grad)
        running = (
            grad_list
            if running is None
            else tuple((before_sum + added for before_sum, added in zip(running, grad_list)))
        )
    (
        sum_gain_one,
        sum_query,
        sum_key,
        sum_value,
        sum_output,
        sum_gain_two,
        sum_router,
        sum_gate,
        sum_up,
        sum_down,
    ) = (
        lax.psum_scatter(
            running[0].astype(jnp.bfloat16), "fsdp", scatter_dimension=0, tiled=True
        ).astype(jnp.float32),
        lax.psum_scatter(
            running[1].astype(jnp.bfloat16), "fsdp", scatter_dimension=0, tiled=True
        ).astype(jnp.float32),
        lax.psum_scatter(
            running[2].astype(jnp.bfloat16), "fsdp", scatter_dimension=0, tiled=True
        ).astype(jnp.float32),
        lax.psum_scatter(
            running[3].astype(jnp.bfloat16), "fsdp", scatter_dimension=0, tiled=True
        ).astype(jnp.float32),
        lax.psum_scatter(
            running[4].astype(jnp.bfloat16), "fsdp", scatter_dimension=1, tiled=True
        ).astype(jnp.float32),
        lax.psum_scatter(
            running[5].astype(jnp.bfloat16), "fsdp", scatter_dimension=0, tiled=True
        ).astype(jnp.float32),
        lax.psum_scatter(
            running[6].astype(jnp.bfloat16), "fsdp", scatter_dimension=0, tiled=True
        ).astype(jnp.float32),
        lax.psum_scatter(
            running[7].astype(jnp.bfloat16), "fsdp", scatter_dimension=1, tiled=True
        ).astype(jnp.float32),
        lax.psum_scatter(
            running[8].astype(jnp.bfloat16), "fsdp", scatter_dimension=1, tiled=True
        ).astype(jnp.float32),
        lax.psum_scatter(
            running[9].astype(jnp.bfloat16), "fsdp", scatter_dimension=2, tiled=True
        ).astype(jnp.float32),
    )
    running = (
        lax.psum(sum_gain_one.astype(jnp.bfloat16), "ctx").astype(jnp.float32),
        lax.psum(sum_query.astype(jnp.bfloat16), "ctx").astype(jnp.float32),
        lax.psum(sum_key.astype(jnp.bfloat16), "ctx").astype(jnp.float32),
        lax.psum(sum_value.astype(jnp.bfloat16), "ctx").astype(jnp.float32),
        lax.psum(sum_output.astype(jnp.bfloat16), "ctx").astype(jnp.float32),
        lax.psum(sum_gain_two.astype(jnp.bfloat16), "ctx").astype(jnp.float32),
        lax.psum(sum_router.astype(jnp.bfloat16), "ctx").astype(jnp.float32),
        lax.psum(sum_gate.astype(jnp.bfloat16), "ctx").astype(jnp.float32),
        lax.psum(sum_up.astype(jnp.bfloat16), "ctx").astype(jnp.float32),
        lax.psum(sum_down.astype(jnp.bfloat16), "ctx").astype(jnp.float32),
    )
    return (
        jnp.stack(outputs),
        jnp.stack(input_grads),
        running[0],
        running[1],
        running[2],
        running[3],
        running[4],
        running[5],
        running[6],
        running[7],
        running[8],
        running[9],
    )


def solution(mesh):
    placed = (
        P(None, ("fsdp", "ctx"), None),
        P("fsdp"),
        P("fsdp", "tp"),
        P("fsdp", "tp"),
        P("fsdp", "tp"),
        P("tp", "fsdp"),
        P("fsdp"),
        P("fsdp", None),
        P(None, "fsdp", "tp"),
        P(None, "fsdp", "tp"),
        P(None, "tp", "fsdp"),
        P(),
        P(None, ("fsdp", "ctx"), None),
        P(None, ("fsdp", "ctx"), None),
    )
    return jax.shard_map(
        local,
        mesh=mesh,
        in_specs=placed,
        out_specs=(
            P(None, ("fsdp", "ctx"), None),
            P(None, ("fsdp", "ctx"), None),
            P("fsdp"),
            P("fsdp", "tp"),
            P("fsdp", "tp"),
            P("fsdp", "tp"),
            P("tp", "fsdp"),
            P("fsdp"),
            P("fsdp", None),
            P(None, "fsdp", "tp"),
            P(None, "fsdp", "tp"),
            P(None, "tp", "fsdp"),
        ),
        check_vma=False,
    )
```

profile of v0, /device:TPU:8, one launch (start us, length us, event | category | flops | bytes accessed | tf_op | source)
XLA Modules:
  0.0 1887.9 jit_solution(16610538779154753706)
XLA Ops:
  10.6 9.9 all_gather.53
  21.2 7.7 all-gather.2
  30.5 11.9 all_gather.56
  47.1 40.5 %all-gather.1 = bf16[2048,1,128]{0,2,1:T(8,128)(2,1)S(1)} all-gather(bf16[128,1,128]{0,2,1:T(8,128)(2,1)S(1)} %pad_maximum_fusion.5), channel_id=3, replica_groups=mesh['fsdp'=4,'ctx'=4,'tp'=2] {'fsdp','ctx'}, dimensions={0}, use_global_device_ids=true | all-gather | bytes 557056 | tf_op jit(solution)/shard_map/all_gather | solution.py:92
  88.6 47.8 %all_gather.65 = bf16[2048,128]{1,0:T(8,128)(2,1)} all-gather(bf16[128,128]{1,0:T(8,128)(2,1)S(1)} %convolution_convert_fusion.4), channel_id=1, replica_groups=mesh['fsdp'=4,'ctx'=4,'tp'=2] {'fsdp','ctx'}, dimensions={0}, use_global_device_ids=true | all-gather | bytes 557056 | tf_op jit(solution)/shard_map/all_gather | solution.py:93
  137.5 40.0 %all-gather = bf16[2048,1,128]{0,2,1:T(8,128)(2,1)S(1)} all-gather(bf16[128,1,128]{0,2,1:T(8,128)(2,1)S(1)} %pad_maximum_fusion.4), channel_id=2, replica_groups=mesh['fsdp'=4,'ctx'=4,'tp'=2] {'fsdp','ctx'}, dimensions={0}, use_global_device_ids=true | all-gather | bytes 557056 | tf_op jit(solution)/shard_map/all_gather | solution.py:92
  178.6 45.2 %all_gather.57 = bf16[2048,128]{1,0:T(8,128)(2,1)} all-gather(bf16[128,128]{1,0:T(8,128)(2,1)S(1)} %convolution_convert_fusion.5), channel_id=1, replica_groups=mesh['fsdp'=4,'ctx'=4,'tp'=2] {'fsdp','ctx'}, dimensions={0}, use_global_device_ids=true | all-gather | bytes 557056 | tf_op jit(solution)/shard_map/all_gather | solution.py:93
  229.4 12.9 while.61
  245.5 16.7 while.60
  272.3 7.9 all-gather.3
  286.2 4.9 mul.995
  294.4 5.0 mul.952
  299.4 7.6 all_gather.60
  332.1 54.4 %all-gather.14.cloned.1.call-done = bf16[8,1536,384]{2,1,0:T(8,128)(2,1)} async-done(((bf16[8,384,384]{2,1,0:T(8,128)(2,1)}), bf16[8,1536,384]{2,1,0:T(8,128)(2,1)}) %all-gather.14.cloned.1.call-update) | async-done | bytes 9437200 | tf_op jit(solution)/shard_map/all_gather | solution.py:335
  386.5 7.2 fusion.117
  393.6 91.0 %all-gather.16.cloned.1.call-done = bf16[8,1536,384]{2,1,0:T(8,128)(2,1)} async-done(((bf16[8,384,384]{2,1,0:T(8,128)(2,1)}), bf16[8,1536,384]{2,1,0:T(8,128)(2,1)}) %all-gather.16.cloned.1.call-update) | async-done | bytes 9437200 | tf_op jit(solution)/shard_map/all_gather | solution.py:336
  484.7 7.2 fusion.116
  491.9 90.9 %all-gather.18.cloned.1.call-done = bf16[8,384,1536]{2,1,0:T(8,128)(2,1)} async-done(((bf16[8,384,384]{2,1,0:T(8,128)(2,1)}), bf16[8,384,1536]{2,1,0:T(8,128)(2,1)}) %all-gather.18.cloned.1.call-update) | async-done | bytes 9437200 | tf_op jit(solution)/shard_map/all_gather | solution.py:337
  582.7 8.9 multiply_convert_fusion.2
  591.6 7.2 fusion.300
  598.8 5.2 convolution_add_fusion
  604.0 6.9 gather_fusion.7
  610.9 5.1 reshape.1324
  616.0 7.3 fusion.115
  623.4 6.7 fusion.114
  630.1 8.7 multiply_convert_fusion.3
  642.9 8.9 convolution_add_fusion.1
  651.8 6.9 gather_fusion.5
  658.7 5.0 reshape.1318
  663.8 7.8 fusion.297
  671.5 6.9 gather_fusion.3
  678.4 4.8 reshape.1316
  683.3 5.0 multiply_reduce_fusion
  688.3 7.8 fusion.296
  696.1 6.9 gather_fusion.1
  703.0 5.0 reshape.1310
  708.0 4.5 reduce_sum.427
  712.5 4.6 reduce_sum.420
  717.2 5.0 multiply_reduce_fusion.1
  724.9 12.0 all-reduce.26.cloned.1.call-done
  755.6 13.1 while.62
  774.4 12.8 while.63
  799.8 10.8 fusion.109
  810.6 13.4 add_convert_fusion
  824.0 12.9 copy.242
  836.9 9.6 copy.248
  847.5 77.8 %reduce-scatter.23.cloned.1.call-done = f32[128,128]{0,1:T(8,128)} async-done(((f32[2048,128]{0,1:T(8,128)}), f32[128,128]{0,1:T(8,128)}) %reduce-scatter.23.cloned.1.call-update) | async-done | bytes 65552 | tf_op jit(solution)/shard_map/reduce_scatter | solution.py:243
  928.3 74.8 %reduce-scatter.21.cloned.1.call-done = f32[128,128]{1,0:T(8,128)} async-done(((f32[2048,128]{1,0:T(8,128)}), f32[128,128]{1,0:T(8,128)}) %reduce-scatter.21.cloned.1.call-update) | async-done | bytes 65552 | tf_op jit(solution)/shard_map/reduce_scatter | solution.py:249
  1004.4 77.0 %reduce-scatter.25.cloned.1.call-done = f32[128,128]{1,0:T(8,128)} async-done(((f32[2048,128]{1,0:T(8,128)}), f32[128,128]{1,0:T(8,128)}) %reduce-scatter.25.cloned.1.call-update) | async-done | bytes 65552 | tf_op jit(solution)/shard_map/reduce_scatter | solution.py:249
  1087.7 11.3 fusion.113
  1098.9 14.0 add_convert_fusion.2
  1114.0 10.9 fusion.112
  1124.9 13.5 add_convert_fusion.1
  1151.7 69.9 %reduce-scatter.41.cloned.1.call-done = bf16[384,3072]{1,0:T(8,128)(2,1)} async-done(((bf16[1536,3072]{1,0:T(8,128)(2,1)}), bf16[384,3072]{1,0:T(8,128)(2,1)}) %reduce-scatter.41.cloned.1.call-update) | async-done | bytes 2359312
  1229.6 19.0 %reduce-scatter.29.cloned.1.call-done = bf16[384,128]{1,0:T(8,128)(2,1)} async-done(((bf16[1536,128]{1,0:T(8,128)(2,1)}), bf16[384,128]{1,0:T(8,128)(2,1)}) %reduce-scatter.29.cloned.1.call-update) | async-done | bytes 98320 | tf_op jit(solution)/shard_map/reduce_scatter | solution.py:372
  1248.7 27.1 %reduce-scatter.31.cloned.1.call-done = bf16[384,128]{1,0:T(8,128)(2,1)} async-done(((bf16[1536,128]{1,0:T(8,128)(2,1)}), bf16[384,128]{1,0:T(8,128)(2,1)}) %reduce-scatter.31.cloned.1.call-update) | async-done | bytes 98320 | tf_op jit(solution)/shard_map/reduce_scatter | solution.py:375
  1275.8 40.9 %reduce-scatter.27.cloned.1.call-done = bf16[384,768]{1,0:T(8,128)(2,1)} async-done(((bf16[1536,768]{1,0:T(8,128)(2,1)}), bf16[384,768]{1,0:T(8,128)(2,1)}) %reduce-scatter.27.cloned.1.call-update) | async-done | bytes 589840 | tf_op jit(solution)/shard_map/reduce_scatter | solution.py:369
  1316.7 98.0 %reduce-scatter.33.cloned.1.call-done = bf16[8,384,384]{2,1,0:T(8,128)(2,1)} async-done(((bf16[8,1536,384]{2,1,0:T(8,128)(2,1)}), bf16[8,384,384]{2,1,0:T(8,128)(2,1)}) %reduce-scatter.33.cloned.1.call-update) | async-done | bytes 2359312 | tf_op jit(solution)/shard_map/reduce_scatter | solution.py:387
  1414.7 98.0 %reduce-scatter.35.cloned.1.call-done = bf16[8,384,384]{2,1,0:T(8,128)(2,1)} async-done(((bf16[8,1536,384]{2,1,0:T(8,128)(2,1)}), bf16[8,384,384]{2,1,0:T(8,128)(2,1)}) %reduce-scatter.35.cloned.1.call-update) | async-done | bytes 2359312 | tf_op jit(solution)/shard_map/reduce_scatter | solution.py:390
  1514.6 25.9 %reduce-scatter.39.cloned.1.call-done = bf16[384,8]{1,0:T(8,128)(2,1)} async-done(((bf16[1536,8]{1,0:T(8,128)(2,1)}), bf16[384,8]{1,0:T(8,128)(2,1)}) %reduce-scatter.39.cloned.1.call-update) | async-done | bytes 6160
  1541.5 22.9 %all-reduce.24.cloned.1.call-done = (bf16[128,1536]{1,0:T(8,128)(2,1)}, bf16[128,1536]{1,0:T(8,128)(2,1)}, bf16[128,1536]{1,0:T(8,128)(2,1)}, bf16[128,1536]{1,0:T(8,128)(2,1)}) async-done(((bf16[128,1536]{1,0:T(8,128)(2,1)}, bf16[128,1536]{1,0:T(8,128)(2,1)}, bf16[128,1536]{1,0:T(8,128)(2,1)}, bf16[128,1536]{1,0:T(8,128)(2,1)}), (bf16[128,1536]{1,0:T(8,128)(2,1)}, bf16[128,1536]{1,0:T(8,128)(2,1)}, ...) | async-done | bytes 1572880 | tf_op jit(solution)/shard_map/psum | solution.py:175
  1566.2 10.0 all-reduce.12
  1576.4 9.3 all-reduce.10
  1591.8 273.6 %all-reduce.22.cloned.1.call-done = (bf16[384,768]{1,0:T(8,128)(2,1)}, bf16[384,128]{1,0:T(8,128)(2,1)}, bf16[384,128]{1,0:T(8,128)(2,1)}, bf16[768,384]{1,0:T(8...) async-done(((bf16[384,768]{1,0:T(8,128)(2,1)}, bf16[384,128]{1,0:T(8,128)(2,1)}, bf16[384,128]{1,0:T(8,128)(2,1)}, ...) | async-done | bytes 8454160 | tf_op jit(solution)/shard_map/psum | solution.py:399
  (689 shorter events, 223.0 us)
Async XLA Ops:
  7.2 21.7 %copy-start.4 = (bf16[2,128,1536]{2,1,0:T(8,128)(2,1)S(1)}, bf16[2,128,1536]{2,1,0:T(8,128)(2,1)}, u32[]{:S(2)}) copy-start(bf16[2,128,1536]{2,1,0:T(8,128)(2,1)} %param.22) | copy-start | bytes 2359300
  7.2 23.3 %copy-start.109 = (bf16[384,128]{1,0:T(8,128)(2,1)S(1)}, bf16[384,128]{1,0:T(8,128)(2,1)}, u32[]{:S(2)}) copy-start(bf16[384,128]{1,0:T(8,128)(2,1)} %param.26) | copy-start | bytes 294916
  7.2 216.6 %all-gather.10.cloned.1.call-start = ((), (), s32[]{:S(2)}) async-start(), calls=%async_computation.12 | async-start | bytes 2949120 | tf_op jit(solution)/shard_map/all_gather | solution.py:329
  7.9 257.4 %all-gather.12.cloned.1.call-start = ((), (), s32[]{:S(2)}) async-start(), calls=%async_computation.13 | async-start | bytes 2949120 | tf_op jit(solution)/shard_map/all_gather | solution.py:332
  8.7 299.7 %all-reduce.28.cloned.1.call-start = ((), (), s32[]{:S(2)}) async-start(), calls=%async_computation.32 | async-start | bytes 1572864 | tf_op jit(solution)/shard_map/psum | solution.py:136
  10.6 36.2 %copy-start.123 = (f32[64]{0:T(128)}, f32[64]{0:T(128)S(1)}, u32[]{:S(2)}) copy-start(f32[64]{0:T(128)S(1)} %multiply_power_fusion) | copy-start | bytes 772
  20.5 22.3 %copy-start.48 = (bf16[1536,128]{1,0:T(8,128)(2,1)}, bf16[1536,128]{1,0:T(8,128)(2,1)S(1)}, u32[]{:S(2)}) copy-start(bf16[1536,128]{1,0:T(8,128)(2,1)S(1)} %all_gather.53) | copy-start | bytes 1179652
  28.9 198.6 %copy-start.72 = (f32[1536]{0:T(1024)}, f32[1536]{0:T(1024)S(1)}, u32[]{:S(2)}) copy-start(f32[1536]{0:T(1024)S(1)} %reshape.1405) | copy-start | bytes 18436
  29.2 13.2 copy-start.138
  29.7 13.8 copy-start.114
  29.7 13.8 copy-start.117
  45.8 177.9 %copy-start.125 = (f32[128]{0:T(128)}, f32[128]{0:T(128)S(1)}, u32[]{:S(2)}) copy-start(f32[128]{0:T(128)S(1)} %add_convert_fusion.16) | copy-start | bytes 1540
  45.8 177.9 %copy-start.127 = (f32[128]{0:T(128)}, f32[128]{0:T(128)S(1)}, u32[]{:S(2)}) copy-start(f32[128]{0:T(128)S(1)} %add_convert_fusion.15) | copy-start | bytes 1540
  46.8 182.3 %copy-start.86 = (f32[128,64]{0,1:T(8,128)}, f32[128,64]{0,1:T(8,128)S(1)}, u32[]{:S(2)}) copy-start(f32[128,64]{0,1:T(8,128)S(1)} %get-tuple-element.1000) | copy-start | bytes 98308
  46.8 182.3 %copy-start.88 = (f32[128,64]{0,1:T(8,128)}, f32[128,64]{0,1:T(8,128)S(1)}, u32[]{:S(2)}) copy-start(f32[128,64]{0,1:T(8,128)S(1)} %get-tuple-element.1001) | copy-start | bytes 98308
  269.7 116.7 %all-gather.14.cloned.1.call-start = ((), (), s32[]{:S(2)}) async-start(), calls=%async_computation.14 | async-start | bytes 11796480 | tf_op jit(solution)/shard_map/all_gather | solution.py:335
  270.3 13.4 copy-start.54
  270.3 214.3 %all-gather.16.cloned.1.call-start = ((), (), s32[]{:S(2)}) async-start(), calls=%async_computation.15 | async-start | bytes 11796480 | tf_op jit(solution)/shard_map/all_gather | solution.py:336
  270.9 311.8 %all-gather.18.cloned.1.call-start = ((), (), s32[]{:S(2)}) async-start(), calls=%async_computation.16 | async-start | bytes 11796480 | tf_op jit(solution)/shard_map/all_gather | solution.py:337
  271.5 465.3 %all-reduce.26.cloned.1.call-start = ((), (), s32[]{:S(2)}) async-start(), calls=%async_computation.31 | async-start | bytes 1572864 | tf_op jit(solution)/shard_map/psum | solution.py:195
  283.8 299.0 %copy-start.107 = (pred[8,96]{1,0:T(8,128)(4,1)}, pred[8,96]{1,0:T(8,128)(4,1)S(1)}, u32[]{:S(2)}) copy-start(pred[8,96]{1,0:T(8,128)(4,1)S(1)} %gt.23) | copy-start | bytes 2308
  292.2 337.9 %copy-start.99 = (pred[8,96]{1,0:T(8,128)(4,1)}, pred[8,96]{1,0:T(8,128)(4,1)S(1)}, u32[]{:S(2)}) copy-start(pred[8,96]{1,0:T(8,128)(4,1)S(1)} %gt.21) | copy-start | bytes 2308
  294.4 12.8 copy-start.96
  294.4 13.4 copy-start.92
  294.4 14.0 copy-start.5
  319.7 418.7 %copy-start.110 = (f32[128,8]{0,1:T(8,128)}, f32[128,8]{0,1:T(8,128)S(1)}, u32[]{:S(2)}) copy-start(f32[128,8]{0,1:T(8,128)S(1)} %fusion.246) | copy-start | bytes 12292
  582.7 16.1 slice-start.3
  582.7 16.1 slice-start.4
  623.4 15.4 slice-start
  623.4 15.4 slice-start.1
  717.1 21.3 %copy-start.32 = (bf16[128,1536]{1,0:T(8,128)(2,1)S(1)}, bf16[128,1536]{1,0:T(8,128)(2,1)}, u32[]{:S(2)}) copy-start(bf16[128,1536]{1,0:T(8,128)(2,1)} %get-tuple-element.916) | copy-start | bytes 1179652
  717.2 21.3 %copy-start.34 = (bf16[128,1536]{1,0:T(8,128)(2,1)S(1)}, bf16[128,1536]{1,0:T(8,128)(2,1)}, u32[]{:S(2)}) copy-start(bf16[128,1536]{1,0:T(8,128)(2,1)} %get-tuple-element.917) | copy-start | bytes 1179652
  717.2 130.3 %reduce-scatter.19.cloned.1.call-start = ((), (), s32[]{:S(2)}) async-start(), calls=%async_computation.17 | async-start | bytes 1114112 | tf_op jit(solution)/shard_map/reduce_scatter | solution.py:243
  724.8 16.4 copy-start.112
  724.8 16.4 copy-start.129
  724.9 16.4 copy-start.135
  772.2 153.1 %reduce-scatter.23.cloned.1.call-start = ((), (), s32[]{:S(2)}) async-start(), calls=%async_computation.19 | async-start | bytes 1114112 | tf_op jit(solution)/shard_map/reduce_scatter | solution.py:243
  789.8 213.4 %reduce-scatter.21.cloned.1.call-start = ((), (), s32[]{:S(2)}) async-start(), calls=%async_computation.18 | async-start | bytes 1114112 | tf_op jit(solution)/shard_map/reduce_scatter | solution.py:249
  790.4 290.9 %reduce-scatter.25.cloned.1.call-start = ((), (), s32[]{:S(2)}) async-start(), calls=%async_computation.20 | async-start | bytes 1114112 | tf_op jit(solution)/shard_map/reduce_scatter | solution.py:249
  791.1 358.4 %reduce-scatter.37.cloned.1.call-start = ((), (), s32[]{:S(2)}) async-start(), calls=%async_computation.26 | async-start | bytes 2949120
  798.8 422.8 %reduce-scatter.41.cloned.1.call-start = ((), (), s32[]{:S(2)}) async-start(), calls=%async_computation.28 | async-start | bytes 11796480
  846.6 78.7 %copy-start.124 = (f32[64]{0:T(128)S(1)}, f32[64]{0:T(128)}, u32[]{:S(2)}) copy-start(f32[64]{0:T(128)} %copy-done.123) | copy-start | bytes 772
  846.6 78.7 %copy-start.126 = (f32[128]{0:T(128)S(1)}, f32[128]{0:T(128)}, u32[]{:S(2)}) copy-start(f32[128]{0:T(128)} %copy-done.125) | copy-start | bytes 1540
  846.6 78.7 %copy-start.128 = (f32[128]{0:T(128)S(1)}, f32[128]{0:T(128)}, u32[]{:S(2)}) copy-start(f32[128]{0:T(128)} %copy-done.127) | copy-start | bytes 1540
  846.6 79.8 %copy-start.73 = (f32[1536]{0:T(1024)S(1)}, f32[1536]{0:T(1024)}, u32[]{:S(2)}) copy-start(f32[1536]{0:T(1024)} %copy-done.72) | copy-start | bytes 18436
  846.6 79.8 %copy-start.116 = (f32[128]{0:T(128)S(1)}, f32[128]{0:T(128)}, u32[]{:S(2)}) copy-start(f32[128]{0:T(128)} %copy-done.114) | copy-start | bytes 1540
  846.7 80.2 %copy-start.119 = (f32[128]{0:T(128)S(1)}, f32[128]{0:T(128)}, u32[]{:S(2)}) copy-start(f32[128]{0:T(128)} %copy-done.117) | copy-start | bytes 1540
  846.7 402.0 %reduce-scatter.29.cloned.1.call-start = ((), (), s32[]{:S(2)}) async-start(), calls=%async_computation.22 | async-start | bytes 491520 | tf_op jit(solution)/shard_map/reduce_scatter | solution.py:372
  847.4 80.7 %copy-start.22 = (f32[128,6,128]{2,0,1:T(8,128)S(1)}, f32[128,6,128]{2,0,1:T(8,128)}, u32[]{:S(2)}) copy-start(f32[128,6,128]{2,0,1:T(8,128)} %copy-done.21) | copy-start | bytes 1179652
  928.0 347.8 %reduce-scatter.31.cloned.1.call-start = ((), (), s32[]{:S(2)}) async-start(), calls=%async_computation.23 | async-start | bytes 491520 | tf_op jit(solution)/shard_map/reduce_scatter | solution.py:375
  1083.3 233.4 %reduce-scatter.27.cloned.1.call-start = ((), (), s32[]{:S(2)}) async-start(), calls=%async_computation.21 | async-start | bytes 2949120 | tf_op jit(solution)/shard_map/reduce_scatter | solution.py:369
  1086.6 12.3 copy-start.67
  1086.6 328.1 %reduce-scatter.33.cloned.1.call-start = ((), (), s32[]{:S(2)}) async-start(), calls=%async_computation.24 | async-start | bytes 11796480 | tf_op jit(solution)/shard_map/reduce_scatter | solution.py:387
  1113.0 399.8 %reduce-scatter.35.cloned.1.call-start = ((), (), s32[]{:S(2)}) async-start(), calls=%async_computation.25 | async-start | bytes 11796480 | tf_op jit(solution)/shard_map/reduce_scatter | solution.py:390
  1138.5 402.1 %reduce-scatter.39.cloned.1.call-start = ((), (), s32[]{:S(2)}) async-start(), calls=%async_computation.27 | async-start | bytes 491520
  1140.9 423.5 %all-reduce.24.cloned.1.call-start = ((), (), s32[]{:S(2)}) async-start(), calls=%async_computation.30 | async-start | bytes 3145728 | tf_op jit(solution)/shard_map/psum | solution.py:175
  1149.5 715.9 %all-reduce.22.cloned.1.call-start = ((), (), s32[]{:S(2)}) async-start(), calls=%async_computation.29 | async-start | bytes 16908288 | tf_op jit(solution)/shard_map/psum | solution.py:399
  1512.7 28.8 %copy-start.120 = (f32[1536]{0:T(1024)S(1)}, f32[1536]{0:T(1024)}, u32[]{:S(2)}) copy-start(f32[1536]{0:T(1024)} %get-tuple-element.770) | copy-start | bytes 18436
  1512.7 28.8 %copy-start.121 = (f32[1536]{0:T(1024)S(1)}, f32[1536]{0:T(1024)}, u32[]{:S(2)}) copy-start(f32[1536]{0:T(1024)} %get-tuple-element.779) | copy-start | bytes 18436
  1512.7 74.8 %copy-start.141 = (f32[128]{0:T(128)S(1)}, f32[128]{0:T(128)}, u32[]{:S(2)}) copy-start(f32[128]{0:T(128)} %copy-done.140) | copy-start | bytes 1540
  1512.7 74.8 %copy-start.139 = (f32[128]{0:T(128)S(1)}, f32[128]{0:T(128)}, u32[]{:S(2)}) copy-start(f32[128]{0:T(128)} %copy-done.138) | copy-start | bytes 1540
  1512.8 74.8 %copy-start.33 = (bf16[128,1536]{1,0:T(8,128)(2,1)S(1)}, bf16[128,1536]{1,0:T(8,128)(2,1)}, u32[]{:S(2)}) copy-start(bf16[128,1536]{1,0:T(8,128)(2,1)} %get-tuple-element.916) | copy-start | bytes 1179652
  1512.8 74.8 %copy-start.36 = (bf16[128,1536]{1,0:T(8,128)(2,1)S(1)}, bf16[128,1536]{1,0:T(8,128)(2,1)}, u32[]{:S(2)}) copy-start(bf16[128,1536]{1,0:T(8,128)(2,1)} %get-tuple-element.917) | copy-start | bytes 1179652
  1512.8 74.8 %copy-start.27 = (f32[128,1536]{1,0:T(8,128)S(1)}, f32[128,1536]{1,0:T(8,128)}, u32[]{:S(2)}) copy-start(f32[128,1536]{1,0:T(8,128)} %copy-done.25) | copy-start | bytes 2359300
  (138 other events, 408.7 us)
Sparse Core Ops, SparseCore 0:
  9.9 39.9 all-gather.9
  51.7 39.6 all-gather.11
  269.9 17.4 all-reduce.27
  289.1 97.2 all-gather.13
  388.3 96.3 all-gather.15
  486.5 96.1 all-gather.17
  717.3 19.5 all-reduce.25
  772.3 75.0 reduce-scatter.18
  849.8 75.4 reduce-scatter.22
  928.0 75.1 reduce-scatter.20
  1006.1 75.1 reduce-scatter.24
  1084.8 38.5 reduce-scatter.36
  1126.5 95.0 reduce-scatter.40
  1224.2 24.4 reduce-scatter.28
  1251.3 24.4 reduce-scatter.30
  1279.3 37.3 reduce-scatter.26
  1319.6 95.0 reduce-scatter.32
  1417.7 95.0 reduce-scatter.34
  1516.1 24.4 reduce-scatter.38
  1543.5 20.8 all-reduce.23
  1569.4 295.9 all-reduce.21
where the time goes:
time: 1900 us; the launch traced here: 1890 us
  waiting for transfers between devices  1160 us (61%)
  blocking collectives  240 us (13%)
  matrix products  227 us (12%)
  local copies, waits for them, and re-layouts  171 us (9%)
  other arithmetic  72.6 us (4%)
    psum x1, waiting for transfers between devices, local(): lax.psum(sum_query.astype(jnp.bfloat16), 'ctx').astype(jnp.float32)  274 us
    reduce_scatter x2, waiting for transfers between devices, micro_step(): lax.psum_scatter(value_grads.reshape(expert_slot_total, HEAD_SIZE), ('fsd...  152 us
    unnamed x24, waiting for transfers between devices  100 us
    reduce_scatter x1, waiting for transfers between devices, local(): lax.psum_scatter(running[8].astype(jnp.bfloat16), 'fsdp', scatter_dimensi...  98 us
    reduce_scatter x1, waiting for transfers between devices, local(): lax.psum_scatter(running[7].astype(jnp.bfloat16), 'fsdp', scatter_dimensi...  98 us
    all_gather x2, blocking collectives, micro_step(): lax.all_gather(value_own, ('fsdp', 'ctx'), axis=0, tiled=True)  93 us
    all_gather x1, waiting for transfers between devices, local(): lax.all_gather(w_up, 'fsdp', axis=1, tiled=True)  91 us
    all_gather x1, waiting for transfers between devices, local(): lax.all_gather(w_down, 'fsdp', axis=2, tiled=True)  90.9 us
  transfers between devices with their start and end apart: 21, of which 16 were waited for; matrix products, arithmetic and copies ran while one was open for 14% of the time, Pallas kernels for 0%

commit v1 on v0

v1 whole, which is shorter than its diff:
```python
import jax
import jax.numpy as jnp
from jax import lax
from jax.experimental import pallas as pl
from jax.experimental.pallas import tpu as pltpu
from jax.sharding import PartitionSpec as P

HEAD = 128
LANES = 128
EPSILON = 1e-06
ROPE_BASE = 1000000.0
NEG_FILL = -1e30
KEY_STEP = 256
MOE_ROWS = 512
VMEM_BYTES = 60 * 2**20

f32 = jnp.float32
bf16 = jnp.bfloat16
EXACT = lax.Precision.HIGHEST
NN = (((1,), (0,)), ((), ()))
NT = (((1,), (1,)), ((), ()))
TN = (((0,), (0,)), ((), ()))


def mm(left, right, dims=NN, precision=None):
    return lax.dot_general(left, right, dims, precision=precision, preferred_element_type=f32)


def vmem(count):
    return [pl.BlockSpec(memory_space=pltpu.VMEM)] * count


def anywhere(count):
    return [pl.BlockSpec(memory_space=pl.ANY)] * count


def scalars():
    return [pl.BlockSpec(memory_space=pltpu.SMEM)]


def shape(dims, kind):
    return jax.ShapeDtypeStruct(dims, kind)


def cost(flops, moved):
    return pl.CostEstimate(flops=int(flops), bytes_accessed=int(moved), transcendentals=0)


def params():
    return pltpu.CompilerParams(vmem_limit_bytes=VMEM_BYTES)


def swap(value, axis, size, bit):
    return lax.ppermute(value, axis, [(i, i ^ bit) for i in range(size)])


def low_bit(number):
    return number & -number


def high_bit(number):
    return 1 << (number.bit_length() - 1)


def gather_relative(own, axis, size, high):
    pick = high_bit if high else low_bit
    got = [own] + [None] * (size - 1)
    for j in range(1, size):
        bit = pick(j)
        got[j] = swap(got[j ^ bit], axis, size, bit)
    return got


def add_low(left, right):
    return (left.astype(f32) + right.astype(f32)).astype(bf16)


def scatter_relative(blocks, axis, size, high):
    current = dict(enumerate(blocks))
    bits = [1 << k for k in range(size.bit_length() - 1)]
    for bit in reversed(bits) if high else bits:
        current = {
            j: add_low(current[j], swap(current[j | bit], axis, size, bit))
            for j in current
            if not j & bit
        }
    return current[0]


def exchange_direct(blocks, axis, size):
    return [blocks[0]] + [swap(blocks[j], axis, size, j) for j in range(1, size)]


def ordered(blocks, index):
    count = len(blocks)
    bit = 1
    while bit < count:
        flag = (index & bit) != 0
        blocks = [jnp.where(flag, blocks[i ^ bit], blocks[i]) for i in range(count)]
        bit *= 2
    return blocks


def axis_relative(value, dim, index):
    count, bit, dims = value.shape[dim], 1, value.shape
    while bit < count:
        split = value.reshape(*dims[:dim], count // (2 * bit), 2, bit, *dims[dim + 1 :])
        value = jnp.where((index & bit) != 0, jnp.flip(split, dim + 1), split).reshape(dims)
        bit *= 2
    return value


def lanes_relative(value, index, count):
    width = value.shape[-1] // count
    return jnp.concatenate(
        [
            lax.dynamic_slice_in_dim(value, (index ^ j) * width, width, value.ndim - 1)
            for j in range(count)
        ],
        -1,
    )


def rotated(values, cosine, sine):
    return values * cosine + pltpu.roll(values, HEAD // 2, 1) * sine


def norm_scale(values):
    return lax.rsqrt(jnp.mean(values * values, -1, keepdims=True) + EPSILON)


def fetch(sources, targets, sems):
    copies = [
        pltpu.make_async_copy(source, target, sems.at[number])
        for number, (source, target) in enumerate(zip(sources, targets))
    ]
    for copy in copies:
        copy.start()
    return copies


def project_in(x, gain, cosine, sine, weights, micro, rows):
    total, width = x.shape
    parts = len(weights)
    depth, half = weights[0].shape
    heads = (2 * half - 2 * HEAD) // HEAD

    def body(x_ref, gain_ref, cos_ref, sin_ref, *rest):
        w_refs, (a_ref, q_ref, kv_ref, all_ref, sems) = rest[:parts], rest[parts:]
        copies = fetch(
            w_refs,
            [
                all_ref.at[pl.ds(n // 2 * depth, depth), pl.ds(n % 2 * half, half)]
                for n in range(parts)
            ],
            sems,
        )
        values = x_ref[...].astype(f32)
        a_ref[...] = (values * norm_scale(values) * gain_ref[...]).astype(bf16)
        for copy in copies:
            copy.wait()
        for m in range(micro):
            span = slice(m * rows, (m + 1) * rows)
            mixed = mm(a_ref[span, :], all_ref[...])
            cosine_m, sine_m = cos_ref[span, :], sin_ref[span, :]
            for h in range(heads):
                q_ref[m, h * rows : (h + 1) * rows, :] = rotated(
                    mixed[:, h * HEAD : (h + 1) * HEAD], cosine_m, sine_m
                ).astype(bf16)
            kv_ref[m, :, :HEAD] = rotated(
                mixed[:, heads * HEAD : (heads + 1) * HEAD], cosine_m, sine_m
            ).astype(bf16)
            kv_ref[m, :, HEAD:] = mixed[:, (heads + 1) * HEAD :].astype(bf16)

    return pl.pallas_call(
        body,
        name="project_in",
        out_shape=(
            shape((total, width), bf16),
            shape((micro, heads * rows, HEAD), bf16),
            shape((micro, rows, 2 * HEAD), bf16),
            shape((width, 2 * half), bf16),
        ),
        in_specs=vmem(4) + anywhere(parts),
        out_specs=tuple(vmem(4)),
        scratch_shapes=[pltpu.SemaphoreType.DMA((parts,))],
        compiler_params=params(),
        cost_estimate=cost(2 * total * width * 2 * half, 2 * 2 * width * 2 * half),
    )(x, gain, cosine, sine, *weights)


def attend(seen, q, mask, kv, weights):
    micro, stacked, _ = q.shape
    keys, rows = mask.shape[1], mask.shape[2]
    heads = stacked // rows
    blocks, parts = len(kv), len(weights)
    per_block = keys // blocks
    depth, half = weights[0].shape
    width = depth * parts // 2
    steps = keys // KEY_STEP
    scale = HEAD ** (-0.5)

    def body(seen_ref, q_ref, mask_ref, *rest):
        kv_refs, w_refs = rest[:blocks], rest[blocks : blocks + parts]
        branch_ref, o_ref, lse_ref, wo_ref, kv_all, top, total, acc, kv_sems, w_sems = rest[
            blocks + parts :
        ]
        kv_copies = fetch(
            kv_refs, [kv_all.at[:, pl.ds(j * per_block, per_block), :] for j in range(blocks)], kv_sems
        )
        w_copies = fetch(
            w_refs,
            [
                wo_ref.at[pl.ds(n // 2 * depth, depth), pl.ds(n % 2 * half, half)]
                for n in range(parts)
            ],
            w_sems,
        )
        for copy in kv_copies:
            copy.wait()
        for m in range(micro):
            top[...] = jnp.full_like(top, NEG_FILL)
            total[...] = jnp.zeros_like(total)
            acc[...] = jnp.zeros_like(acc)
            queries = q_ref[m]

            def step(n, carry, m=m, queries=queries):
                @pl.when(seen_ref[m * steps + n] > 0)
                def _():
                    start = pl.multiple_of(n * KEY_STEP, KEY_STEP)
                    keys_n = kv_all[m, pl.ds(start, KEY_STEP), :HEAD]
                    values_n = kv_all[m, pl.ds(start, KEY_STEP), HEAD:]
                    bias = mask_ref[m, pl.ds(start, KEY_STEP), :].astype(f32)
                    scores = mm(keys_n, queries, NT) * scale + jnp.concatenate([bias] * heads, 1)
                    peak = jnp.maximum(top[...], jnp.max(scores, 0, keepdims=True))
                    rescale = jnp.exp(top[...] - peak)
                    weights_n = jnp.exp(scores - peak)
                    total[...] = total[...] * rescale + jnp.sum(weights_n, 0, keepdims=True)
                    acc[...] = acc[...] * rescale + mm(values_n, weights_n.astype(bf16), TN)
                    top[...] = peak

                return carry

            lax.fori_loop(0, steps, step, 0)
            lse_ref[m] = top[...] + jnp.log(total[...])
            mixed = acc[...] / total[...]
            for h in range(heads):
                o_ref[m, :, h * HEAD : (h + 1) * HEAD] = mixed[
                    :, h * rows : (h + 1) * rows
                ].T.astype(bf16)
        for copy in w_copies:
            copy.wait()
        for m in range(micro):
            branch_ref[m] = mm(o_ref[m], wo_ref[...], NT).astype(bf16)

    return pl.pallas_call(
        body,
        name="attend",
        out_shape=(
            shape((micro, rows, width), bf16),
            shape((micro, rows, heads * HEAD), bf16),
            shape((micro, 1, stacked), f32),
            shape((width, heads * HEAD), bf16),
        ),
        in_specs=scalars() + vmem(2) + anywhere(blocks + parts),
        out_specs=tuple(vmem(4)),
        scratch_shapes=[
            pltpu.VMEM((micro, keys, 2 * HEAD), bf16),
            pltpu.VMEM((1, stacked), f32),
            pltpu.VMEM((1, stacked), f32),
            pltpu.VMEM((HEAD, stacked), f32),
            pltpu.SemaphoreType.DMA((blocks,)),
            pltpu.SemaphoreType.DMA((parts,)),
        ],
        compiler_params=params(),
        cost_estimate=cost(
            2 * micro * stacked * keys * HEAD * 2 + 2 * micro * rows * width * heads * HEAD,
            2 * micro * keys * 2 * HEAD + 2 * width * heads * HEAD * 2,
        ),
    )(seen, q, mask, *kv, *weights)


def second_norm(place, x, branch, other, gain):
    rows, width = other.shape

    def body(place_ref, x_ref, branch_ref, other_ref, gain_ref, middle_ref, b_ref):
        t = place_ref[2]
        middle = (
            x_ref[t].astype(f32) + branch_ref[t].astype(f32) + other_ref[...].astype(f32)
        )
        middle_ref[...] = middle
        b_ref[...] = (middle * norm_scale(middle) * gain_ref[...]).astype(bf16)

    return pl.pallas_call(
        body,
        name="second_norm",
        out_shape=(shape((rows, width), f32), shape((rows, width), bf16)),
        in_specs=scalars() + vmem(4),
        out_specs=tuple(vmem(2)),
        compiler_params=params(),
        cost_estimate=cost(10 * rows * width, 20 * rows * width),
    )(place, x, branch, other, gain)


def routing(b, router, experts):
    logits = mm(b, router)
    lane = lax.broadcasted_iota(jnp.int32, logits.shape, 1)
    logits = jnp.where(lane < experts, logits, NEG_FILL)
    powers = jnp.exp(logits - jnp.max(logits, -1, keepdims=True))
    return powers / jnp.sum(powers, -1, keepdims=True), lane


def experts_step(place, b, cx, router, weights, experts):
    chunks, rows, width = b.shape
    local = len(weights)
    parts = len(weights[0])
    _, depth, hidden = weights[0][0].shape
    k0 = 0.7978845608028654
    k1 = 0.044715

    def body(place_ref, b_ref, cx_ref, router_ref, *rest):
        w_refs = rest[: local * parts]
        rest = rest[local * parts :]
        out_ref, back_ref = rest[:2]
        grad_refs = rest[2 : 2 + local * parts]
        w_all, b_turned, c_turned, gate_all, out_acc, back_acc, share_acc, grad_acc, stage, w_sems, g_sems = rest[
            2 + local * parts :
        ]
        chunk, e = pl.program_id(0), pl.program_id(1)

        def weight_copies(number):
            return [
                pltpu.make_async_copy(
                    w_refs[number * parts + j],
                    w_all.at[number, :, pl.ds(j * depth, depth), :],
                    w_sems.at[number * parts + j],
                )
                for j in range(parts)
            ]

        def grad_copies(number):
            return [
                pltpu.make_async_copy(
                    stage.at[:, pl.ds(j * depth, depth), :],
                    grad_refs[number * parts + j],
                    g_sems.at[number * parts + j],
                )
                for j in range(parts)
            ]

        @pl.when((chunk == 0) & (e == 0))
        def _():
            for number in range(local):
                for copy in weight_copies(number):
                    copy.start()

        @pl.when(e == 0)
        def _():
            probs, _ = routing(b_ref[0], router_ref[...], experts)
            gate_all[...] = probs * cx_ref[0, :, width:].astype(f32)
            b_turned[...] = b_ref[0].T
            c_turned[...] = cx_ref[0, :, :width].T

        for number in range(local):

            @pl.when((chunk == 0) & (e == number))
            def _(number=number):
                for copy in weight_copies(number):
                    copy.wait()

        b_rows = b_ref[0]
        c_rows = cx_ref[0, :, :width]
        w_gate, w_up, w_down = w_all[e, 0], w_all[e, 1], w_all[e, 2]
        lane = lax.broadcasted_iota(jnp.int32, (rows, LANES), 1)
        mine = lane == place_ref[1] * local + e
        gate = jnp.sum(jnp.where(mine, gate_all[...], 0.0), -1, keepdims=True)
        z = mm(b_rows, w_gate)
        up = mm(b_rows, w_up)
        down_back = mm(c_rows, w_down)
        square = z * z
        bend = jnp.tanh(k0 * z * (1.0 + k1 * square))
        half = 0.5 * (1.0 + bend)
        active = z * half
        slope = half + 0.5 * z * (1.0 - bend * bend) * (k0 * (1.0 + 3.0 * k1 * square))
        hidden_rows = active * up
        share = jnp.sum(hidden_rows * down_back, -1, keepdims=True)
        scaled = (gate * hidden_rows).astype(bf16)
        hidden_back = gate * down_back
        gate_back = (hidden_back * up * slope).astype(bf16)
        up_back = (hidden_back * active).astype(bf16)
        def sum_up(acc, new):
            @pl.when(e == 0)
            def _():
                acc[...] = new

            @pl.when(e > 0)
            def _():
                acc[...] += new

        sum_up(share_acc, jnp.where(mine, share, 0.0))
        sum_up(out_acc, mm(scaled, w_down, NT))
        sum_up(back_acc, mm(gate_back, w_gate, NT) + mm(up_back, w_up, NT))

        @pl.when(e == local - 1)
        def _():
            out_ref[0] = out_acc[...].astype(bf16)
            back_ref[0, :, :width] = back_acc[...].astype(bf16)
            back_ref[0, :, width:] = share_acc[...].astype(bf16)

        for number in range(1, local):

            @pl.when((chunk == chunks - 1) & (e == number))
            def _(number=number):
                for copy in grad_copies(number - 1):
                    copy.wait()

        for n, (turned, back) in enumerate(
            ((b_turned, gate_back), (b_turned, up_back), (c_turned, scaled))
        ):
            new = mm(turned[...], back)

            @pl.when(chunk == 0)
            def _(n=n, new=new):
                grad_acc[e, n] = new

            @pl.when((chunk > 0) & (chunk < chunks - 1))
            def _(n=n, new=new):
                grad_acc[e, n] += new

            @pl.when(chunk == chunks - 1)
            def _(n=n, new=new):
                stage[n] = (grad_acc[e, n] + new).astype(bf16)

        for number in range(local):

            @pl.when((chunk == chunks - 1) & (e == number))
            def _(number=number):
                for copy in grad_copies(number):
                    copy.start()
                if number == local - 1:
                    for copy in grad_copies(number):
                        copy.wait()

    block = lambda lanes: pl.BlockSpec((1, rows, lanes), lambda i, j: (i, 0, 0))
    return pl.pallas_call(
        body,
        name="experts_step",
        grid=(chunks, local),
        out_shape=(
            shape((chunks, rows, width), bf16),
            shape((chunks, rows, width + LANES), bf16),
            *[shape((3, depth, hidden), bf16)] * (local * parts),
        ),
        in_specs=scalars()
        + [
            block(width),
            block(width + LANES),
            pl.BlockSpec((width, LANES), lambda i, j: (0, 0), pipeline_mode=pl.Buffered(1)),
        ]
        + anywhere(local * parts),
        out_specs=(block(width), block(width + LANES), *anywhere(local * parts)),
        scratch_shapes=[
            pltpu.VMEM((local, 3, width, hidden), bf16),
            pltpu.VMEM((width, rows), bf16),
            pltpu.VMEM((width, rows), bf16),
            pltpu.VMEM((rows, LANES), f32),
            pltpu.VMEM((rows, width), f32),
            pltpu.VMEM((rows, width), f32),
            pltpu.VMEM((rows, LANES), f32),
            pltpu.VMEM((local, 3, width, hidden), f32),
            pltpu.VMEM((3, width, hidden), bf16),
            pltpu.SemaphoreType.DMA((local * parts,)),
            pltpu.SemaphoreType.DMA((local * parts,)),
        ],
        compiler_params=params(),
        cost_estimate=cost(
            18 * chunks * rows * width * hidden * local,
            2 * (4 * chunks * rows * width + 6 * local * width * hidden),
        ),
    )(place, b, cx, router, *[block_j for one in weights for block_j in one])


def second_norm_back(sums, middle, b, cx, gain, router, experts):
    rows, width = middle.shape
    count = len(sums)

    def body(*refs):
        middle_ref, b_ref, cx_ref, gain_ref, router_ref = refs[count : count + 5]
        dmiddle_ref, go_ref, small_ref = refs[count + 5 :]
        total = refs[0][...].astype(f32)
        for ref in refs[1:count]:
            total += ref[...].astype(f32)
        share = total[:, width:] * cx_ref[:, width:].astype(f32)
        probs, lane = routing(b_ref[...], router_ref[...], experts)
        dl = probs * (share - jnp.sum(probs * share, -1, keepdims=True))
        db = total[:, :width] + mm(dl, router_ref[...].astype(f32), NT, EXACT)
        values = middle_ref[...]
        scale = norm_scale(values)
        normal = values * scale
        dn = db * gain_ref[...]
        dmiddle = cx_ref[:, :width].astype(f32) + scale * (
            dn - normal * jnp.mean(dn * normal, -1, keepdims=True)
        )
        dmiddle_ref[...] = dmiddle
        go_ref[...] = dmiddle.astype(bf16)
        small_ref[...] = mm(b_ref[...].astype(f32), dl, TN, EXACT) + mm(
            db * normal, (lane == experts).astype(f32), TN, EXACT
        )

    return pl.pallas_call(
        body,
        name="second_norm_back",
        out_shape=(
            shape((rows, width), f32),
            shape((rows, width), bf16),
            shape((width, LANES), f32),
        ),
        in_specs=vmem(count + 5),
        out_specs=tuple(vmem(3)),
        compiler_params=params(),
        cost_estimate=cost(2 * 20 * rows * width * LANES, 24 * rows * width),
    )(*sums, middle, b, cx, gain, router)


def attend_back(place, seen, go_own, go_other, q, o, lse, mask, cosine, sine, wo, kv):
    micro, stacked, _ = q.shape
    keys, rows = mask.shape[1], mask.shape[2]
    heads = stacked // rows
    blocks = len(kv)
    per_block = keys // blocks
    width = wo.shape[0]
    steps = keys // KEY_STEP
    scale = HEAD ** (-0.5)

    def body(place_ref, seen_ref, own_ref, other_ref, q_ref, o_ref, lse_ref, mask_ref, cos_ref, sin_ref, wo_ref, *rest):
        kv_refs = rest[:blocks]
        go_ref, dq_ref = rest[blocks : blocks + 2]
        dkv_refs = rest[blocks + 2 : 2 * blocks + 2]
        kv_all, dkv_all, acc, do_all, kv_sems, d_sems = rest[2 * blocks + 2 :]
        kv_copies = fetch(
            kv_refs, [kv_all.at[:, pl.ds(j * per_block, per_block), :] for j in range(blocks)], kv_sems
        )
        t = place_ref[2]
        go_ref[t] = own_ref[...]
        go_ref[1 - t] = other_ref[...]
        for copy in kv_copies:
            copy.wait()
        for m in range(micro):
            do = mm(go_ref[m], wo_ref[...]).astype(bf16)
            pieces = []
            for h in range(heads):
                do_h = do[:, h * HEAD : (h + 1) * HEAD]
                do_all[h * rows : (h + 1) * rows, :] = do_h
                product = do_h.astype(f32) * o_ref[m, :, h * HEAD : (h + 1) * HEAD].astype(f32)
                pieces.append(jnp.sum(product.T, 0, keepdims=True))
            delta = jnp.concatenate(pieces, 1)
            acc[...] = jnp.zeros_like(acc)
            queries, outs, total = q_ref[m], do_all[...], lse_ref[m]

            def step(n, carry, m=m, queries=queries, outs=outs, total=total, delta=delta):
                start = pl.multiple_of(n * KEY_STEP, KEY_STEP)
                span = pl.ds(start, KEY_STEP)

                @pl.when(seen_ref[m * steps + n] > 0)
                def _():
                    keys_n = kv_all[m, span, :HEAD]
                    values_n = kv_all[m, span, HEAD:]
                    bias = mask_ref[m, span, :].astype(f32)
                    scores = mm(keys_n, queries, NT) * scale + jnp.concatenate([bias] * heads, 1)
                    probs = jnp.exp(scores - total)
                    ds = (probs * (mm(values_n, outs, NT) - delta)).astype(bf16)
                    acc[...] += mm(keys_n, ds, TN)
                    dkv_all[m, span, :HEAD] = (mm(ds, queries) * scale).astype(bf16)
                    dkv_all[m, span, HEAD:] = mm(probs.astype(bf16), outs).astype(bf16)

                @pl.when(seen_ref[m * steps + n] == 0)
                def _():
                    dkv_all[m, span, :] = jnp.zeros((KEY_STEP, 2 * HEAD), bf16)

                return carry

            lax.fori_loop(0, steps, step, 0)
            for h in range(heads):
                back = acc[:, h * rows : (h + 1) * rows].T * scale
                part = slice(m * rows, (m + 1) * rows)
                dq_ref[part, h * HEAD : (h + 1) * HEAD] = rotated(
                    back, cos_ref[part, :], -sin_ref[part, :]
                ).astype(bf16)
        d_copies = fetch(
            [dkv_all.at[:, pl.ds(j * per_block, per_block), :] for j in range(blocks)], dkv_refs, d_sems
        )
        for copy in d_copies:
            copy.wait()

    return pl.pallas_call(
        body,
        name="attend_back",
        out_shape=(
            shape((micro, rows, width), bf16),
            shape((micro * rows, heads * HEAD), bf16),
            *[shape((micro, per_block, 2 * HEAD), bf16)] * blocks,
        ),
        in_specs=scalars() * 2 + vmem(9) + anywhere(blocks),
        out_specs=(*vmem(2), *anywhere(blocks)),
        scratch_shapes=[
            pltpu.VMEM((micro, keys, 2 * HEAD), bf16),
            pltpu.VMEM((micro, keys, 2 * HEAD), bf16),
            pltpu.VMEM((HEAD, stacked), f32),
            pltpu.VMEM((stacked, HEAD), bf16),
            pltpu.SemaphoreType.DMA((blocks,)),
            pltpu.SemaphoreType.DMA((blocks,)),
        ],
        compiler_params=params(),
        cost_estimate=cost(
            2 * micro * stacked * keys * HEAD * 5,
            2 * micro * keys * 4 * HEAD + 2 * width * heads * HEAD,
        ),
    )(place, seen, go_own, go_other, q, o, lse, mask, cosine, sine, wo, *kv)


def project_back(dkv, dq, cosine, sine, w):
    count = len(dkv)
    micro, rows, _ = dkv[0].shape
    width, columns = w.shape
    wide = columns - 2 * HEAD

    def body(*refs):
        dq_ref, cos_ref, sin_ref, w_ref, dkv_ref, da_ref = refs[count:]
        for m in range(micro):
            part = slice(m * rows, (m + 1) * rows)
            total = refs[0][m].astype(f32)
            for ref in refs[1:count]:
                total += ref[m].astype(f32)
            dkv_ref[part, :HEAD] = rotated(
                total[:, :HEAD], cos_ref[part, :], -sin_ref[part, :]
            ).astype(bf16)
            dkv_ref[part, HEAD:] = total[:, HEAD:].astype(bf16)
            da_ref[m] = (
                mm(dq_ref[part, :], w_ref[:, :wide], NT) + mm(dkv_ref[part, :], w_ref[:, wide:], NT)
            ).astype(bf16)

    return pl.pallas_call(
        body,
        name="project_back",
        out_shape=(shape((micro * rows, 2 * HEAD), bf16), shape((micro, rows, width), bf16)),
        in_specs=vmem(count + 4),
        out_specs=tuple(vmem(2)),
        compiler_params=params(),
        cost_estimate=cost(2 * micro * rows * width * columns, 2 * width * columns),
    )(*dkv, dq, cosine, sine, w)


def first_norm_back(place, da, other, x, gain, dmiddle, lane_at):
    rows, width = dmiddle.shape

    def body(place_ref, da_ref, other_ref, x_ref, gain_ref, dmiddle_ref, ig_ref, small_ref):
        t = place_ref[2]
        total = da_ref[t].astype(f32) + other_ref[...].astype(f32)
        values = x_ref[t].astype(f32)
        scale = norm_scale(values)
        normal = values * scale
        dn = total * gain_ref[...]
        ig_ref[...] = dmiddle_ref[...] + scale * (
            dn - normal * jnp.mean(dn * normal, -1, keepdims=True)
        )
        lane = lax.broadcasted_iota(jnp.int32, (rows, LANES), 1)
        small_ref[...] = mm(total * normal, (lane == lane_at).astype(f32), TN, EXACT)

    return pl.pallas_call(
        body,
        name="first_norm_back",
        out_shape=(shape((rows, width), f32), shape((width, LANES), f32)),
        in_specs=scalars() + vmem(5),
        out_specs=tuple(vmem(2)),
        compiler_params=params(),
        cost_estimate=cost(2 * 6 * rows * width * LANES, 20 * rows * width),
    )(place, da, other, x, gain, dmiddle)


def solution(mesh):
    F, C, T = mesh.shape["fsdp"], mesh.shape["ctx"], mesh.shape["tp"]

    def local(
        tokens,
        gain_attn,
        w_query,
        w_key,
        w_value,
        w_output,
        gain_mlp,
        w_router,
        w_gate,
        w_up,
        w_down,
        lineage,
        expert_ids,
        cotangent,
    ):
        micro, rows, width = tokens.shape
        depth = width // F
        experts = w_router.shape[1]
        local_experts = experts // C
        slots = lineage.shape[2]
        f, c, t = lax.axis_index("fsdp"), lax.axis_index("ctx"), lax.axis_index("tp")
        place = jnp.stack([f, c, t]).astype(jnp.int32)

        def pick(pair, index):
            return jnp.where(index == 0, pair[0], pair[1])

        def core(value):
            return swap(value, "tp", T, 1)

        small = jnp.concatenate(
            [gain_attn[None, :], gain_mlp[None, :], w_router.T, jnp.zeros((6, depth), bf16)], 0
        )
        small = exchange_direct([small] * F, "fsdp", F)
        in_cols = jnp.concatenate([w_query, w_key, w_value], 1)
        half = in_cols.shape[1] // 2
        in_a = gather_relative(in_cols[:, :half], "fsdp", F, True)
        in_b = gather_relative(in_cols[:, half:], "fsdp", F, False)
        in_weights = [block for pair in zip(in_a, in_b) for block in pair]
        out_rows = w_output.T
        half = out_rows.shape[1] // 2
        out_a = gather_relative(out_rows[:, :half], "fsdp", F, True)
        out_b = gather_relative(out_rows[:, half:], "fsdp", F, False)
        out_weights = [block for pair in zip(out_a, out_b) for block in pair]
        first = c * local_experts
        mine = [lax.dynamic_slice_in_dim(w, first, local_experts, 0) for w in (w_gate, w_up, w_down)]
        expert_weights = []
        for e in range(local_experts):
            own = jnp.stack([mine[0][e], mine[1][e], mine[2][e].T])
            expert_weights.append(gather_relative(own, "fsdp", F, e % 2 == 0))
        gains = jnp.concatenate(small, 1)
        gain_one, gain_two = gains[0:1].astype(f32), gains[1:2].astype(f32)
        router = jnp.pad(gains[2 : 2 + experts].T, ((0, 0), (0, LANES - experts)))

        x = lanes_relative(tokens, f, F)
        c_mine = lanes_relative(pick(cotangent, t), f, F)
        ids_mine = pick(expert_ids, t)
        chosen = jnp.sum(
            (ids_mine[:, :, None] == jnp.arange(LANES, dtype=jnp.int32)[None, None, :]).astype(f32), 1
        ).astype(bf16)
        cx_mine = jnp.concatenate([c_mine, chosen], 1)

        def to_rows(mine_value):
            got = jnp.stack(exchange_direct([mine_value] * C, "ctx", C))
            both = jnp.stack([got, core(got)])
            return both.reshape(T * C * rows // MOE_ROWS, MOE_ROWS, mine_value.shape[-1])

        cx_rows = to_rows(cx_mine)

        f_order = f ^ jnp.arange(F, dtype=jnp.int32)
        c_order = c ^ jnp.arange(C, dtype=jnp.int32)
        block_order = (f_order[:, None] * C + c_order[None, :]).reshape(-1)
        key_index = (block_order[:, None] * rows + jnp.arange(rows, dtype=jnp.int32)).reshape(-1)
        key_owner = lineage[:, 0].reshape(micro, F, C, rows)
        key_owner = axis_relative(axis_relative(key_owner, 1, f), 2, c).reshape(micro, slots)
        first_row = (f * C + c) * rows
        query_lin = lax.dynamic_slice_in_dim(lineage, first_row, rows, 2)
        query_index = first_row + jnp.arange(rows, dtype=jnp.int32)
        owner = key_owner[:, :, None]
        visible = (
            ((owner == query_lin[:, 0, None, :]) & (key_index[None, :, None] <= query_index))
            | (owner == query_lin[:, 1, None, :])
            | (owner == query_lin[:, 2, None, :])
        )
        mask = jnp.where(visible, 0.0, NEG_FILL).astype(bf16)
        counts = jnp.sum(visible.astype(f32).reshape(micro, slots // KEY_STEP, KEY_STEP, rows), 2)
        positions = (jnp.sum(counts, 1) - 1.0).reshape(micro * rows)
        seen = (jnp.max(counts, -1) > 0).astype(jnp.int32).reshape(-1)
        frequency = ROPE_BASE ** (-jnp.arange(HEAD // 2, dtype=f32) / (HEAD // 2))
        angles = positions[:, None] * frequency[None, :]
        cosine, sine = jnp.cos(angles), jnp.sin(angles)
        cosine = jnp.concatenate([cosine, cosine], 1)
        sine = jnp.concatenate([-sine, sine], 1)

        a, q, kv_own, in_all = project_in(
            x.reshape(micro * rows, width), gain_one, cosine, sine, in_weights, micro, rows
        )
        kv_ctx = jnp.concatenate(exchange_direct([kv_own] * C, "ctx", C), 1)
        kv = exchange_direct([kv_ctx] * F, "fsdp", F)
        branch, o, lse, wo_all = attend(seen, q, mask, kv, out_weights)
        middle, b = second_norm(place, x, branch, core(pick(branch, 1 - t)), gain_two)

        b_rows = to_rows(b)
        out_parts, back_parts, *grads = experts_step(
            place, b_rows, cx_rows, router, expert_weights, experts
        )

        def to_owner(parts):
            parts = parts.reshape(T, C, rows, parts.shape[-1])
            got = core(parts[1])
            return exchange_direct([add_low(parts[0, k], got[k]) for k in range(C)], "ctx", C)

        dmiddle, go, small_grad = second_norm_back(
            to_owner(back_parts), middle, b, cx_mine, gain_two, router, experts
        )
        out_sums = to_owner(out_parts)
        result = middle
        for part in out_sums:
            result = result + part.astype(f32)
        result = result.astype(bf16)

        expert_grads = []
        for e in range(local_experts):
            expert_grads.append(
                scatter_relative(grads[e * F : (e + 1) * F], "fsdp", F, e % 2 == 0)
            )
        expert_grads = lax.all_gather(jnp.stack(expert_grads), "ctx", axis=0, tiled=True)

        go_all, dq, *dkv = attend_back(
            place, seen, go, core(go), q, o, lse, mask, cosine, sine, wo_all, kv
        )
        go_flat, o_flat = go_all.reshape(micro * rows, width), o.reshape(micro * rows, -1)

        def grad_blocks(left, right):
            return [
                mm(left[:, j * depth : (j + 1) * depth], right, TN).astype(bf16) for j in range(F)
            ]

        def over_ctx(part):
            step = part.shape[0] // C
            pieces = [lax.dynamic_slice_in_dim(part, (c ^ k) * step, step, 0) for k in range(C)]
            got = exchange_direct(pieces, "ctx", C)
            total = got[0].astype(f32)
            for piece in got[1:]:
                total = total + piece.astype(f32)
            total = total.astype(bf16)
            return jnp.concatenate(ordered(exchange_direct([total] * C, "ctx", C), c), 0)

        grad_out = over_ctx(scatter_relative(grad_blocks(go_flat, o_flat), "fsdp", F, True))
        dkv = exchange_direct(dkv, "fsdp", F)
        total = dkv[0].astype(f32)
        for part in dkv[1:]:
            total = total + part.astype(f32)
        total = total.astype(bf16).reshape(micro, C, rows, 2 * HEAD)
        dkv = exchange_direct([total[:, k] for k in range(C)], "ctx", C)
        dkv, da = project_back(dkv, dq, cosine, sine, in_all)
        grad_q = over_ctx(scatter_relative(grad_blocks(a, dq), "fsdp", F, False))
        input_grad, small_more = first_norm_back(
            place, da, core(pick(da, 1 - t)), x, gain_one, dmiddle, experts + 1
        )
        small_grad = small_grad + small_more
        small_grad = (small_grad + core(small_grad)).astype(bf16)
        tail = [
            jnp.concatenate([block, small_grad[j * depth : (j + 1) * depth]], 1)
            for j, block in enumerate(grad_blocks(a, dkv))
        ]
        grad_tail = over_ctx(scatter_relative(tail, "fsdp", F, True)).astype(f32)

        def whole(mine_value):
            other = core(mine_value)
            both = jnp.stack([pick((mine_value, other), t), pick((other, mine_value), t)])
            return lanes_relative(both, f, F)

        return (
            whole(result),
            whole(input_grad),
            grad_tail[:, 2 * HEAD + experts + 1],
            grad_q.astype(f32),
            grad_tail[:, :HEAD],
            grad_tail[:, HEAD : 2 * HEAD],
            grad_out.astype(f32).T,
            grad_tail[:, 2 * HEAD + experts],
            grad_tail[:, 2 * HEAD : 2 * HEAD + experts],
            expert_grads[:, 0].astype(f32),
            expert_grads[:, 1].astype(f32),
            jnp.swapaxes(expert_grads[:, 2].astype(f32), 1, 2),
        )

    rows_of = P(None, ("fsdp", "ctx"), None)
    weights = (
        P("fsdp"),
        P("fsdp", "tp"),
        P("fsdp", "tp"),
        P("fsdp", "tp"),
        P("tp", "fsdp"),
        P("fsdp"),
        P("fsdp", None),
        P(None, "fsdp", "tp"),
        P(None, "fsdp", "tp"),
        P(None, "tp", "fsdp"),
    )
    return jax.shard_map(
        local,
        mesh=mesh,
        in_specs=(rows_of, *weights, P(), rows_of, rows_of),
        out_specs=(rows_of, rows_of, *weights),
        check_vma=False,
    )
```

time: 1900 us -> 673 us (0.35)
  waiting for transfers between devices: 1160 us -> 345 us
  blocking collectives: 240 us -> 0 us
  matrix products: 227 us -> 12.8 us
  local copies, waits for them, and re-layouts: 171 us -> 34.4 us
  starting transfers between devices: 1.48 us -> 111 us
  Pallas kernels: 0 us -> 89.1 us
  other arithmetic: 72.6 us -> 52.7 us
    reduce_scatter x9 -> x0, waiting for transfers between devices: 513 us -> none  [the longest x2 152 us: micro_step(): lax.psum_scatter(value_grads.reshape(expert_slot_total, HEAD_SIZE), ('fsd...]
    ppermute x0 -> x88, waiting for transfers between devices: none -> 345 us  [swap(): return lax.ppermute(value, axis, [(i, i ^ bit) for i in range(size)])]
    psum x4 -> x0, waiting for transfers between devices: 308 us -> none  [the longest x1 274 us: local(): lax.psum(sum_query.astype(jnp.bfloat16), 'ctx').astype(jnp.float32)]
    all_gather x5 -> x1, waiting for transfers between devices: 236 us -> 0.01 us  [local(): lax.all_gather(jnp.stack(expert_grads), 'ctx', axis=0, tiled=True)]
    all_gather x9 -> x0, blocking collectives: 218 us -> none  [the longest x2 93 us: micro_step(): lax.all_gather(value_own, ('fsdp', 'ctx'), axis=0, tiled=True)]
    dot_general x76 -> x12, matrix products: 227 us -> 12.8 us  [mm(): lax.dot_general(left, right, dims, precision=precision, preferred_element...]
    ppermute x0 -> x88, starting transfers between devices: none -> 111 us  [swap(): return lax.ppermute(value, axis, [(i, i ^ bit) for i in range(size)])]
    unnamed x24 -> x1, waiting for transfers between devices: 100 us -> 0.02 us
  transfers between devices with their start and end apart: 21 -> 89, of which waited for: 16 -> 45; matrix products, arithmetic and copies ran while one was open for 14% -> 11% of each run, Pallas kernels for 0% -> 6%
where the time goes in v1:
time: 673 us; the launch traced here: 661 us
  waiting for transfers between devices  345 us (51%)
  starting transfers between devices  111 us (16%)
  Pallas kernels  89.1 us (13%)
  other arithmetic  52.7 us (8%)
  local copies, waits for them, and re-layouts  34.4 us (5%)
  between operations  15.3 us (2%)
  matrix products  12.8 us (2%)
    ppermute x88, waiting for transfers between devices, swap(): return lax.ppermute(value, axis, [(i, i ^ bit) for i in range(size)])  345 us
    ppermute x88, starting transfers between devices, swap(): return lax.ppermute(value, axis, [(i, i ^ bit) for i in range(size)])  111 us
    pallas_call x1, Pallas kernels, experts_step(): pl.pallas_call(body, name='experts_step', grid=(chunks, local), out_shape...  48.6 us
    unnamed x145, local copies, waits for them, and re-layouts  19.6 us
  transfers between devices with their start and end apart: 89, of which 45 were waited for; matrix products, arithmetic and copies ran while one was open for 11% of the time, Pallas kernels for 6%

profile of v1, /device:TPU:8, one launch (start us, length us, event | category | flops | bytes accessed | tf_op | source)
XLA Modules:
  0.0 660.5 jit_solution(5783287283059159024)
XLA Ops:
  25.5 2.9 select_convert_fusion.mask_ref
  36.7 7.2 %collective-permute-done = bf16[16,384]{1,0:T(8,128)(2,1)S(1)} collective-permute-done((bf16[16,384]{1,0:T(8,128)(2,1)}, bf16[16,384]{1,0:T(8,128)(2,1)S(1)}, u32[]{:S(2)}, u32[]{:S(2)}) %collective-permute-start) | collective-permute-done | bytes 12320 | tf_op jit(solution)/shard_map/ppermute | solution.py:54
  47.9 3.0 collective-permute-done.7.rest_6_
  51.8 5.2 project_in.1
  58.2 2.6 collective-permute-start.10
  69.2 2.9 collective-permute-start.14
  72.7 8.5 %collective-permute-done.18.rest_9_ = bf16[384,384]{1,0:T(8,128)(2,1)S(1)} collective-permute-done((bf16[384,384]{1,0:T(8,128)(2,1)}, bf16[384,384]{1,0:T(8,128)(2,1)S(1)}, u32[]{:S(2)}, u32[]{:S(2)}) %collective-permute-start.18) | collective-permute-done | bytes 294944 | tf_op jit(solution)/shard_map/ppermute | solution.py:54
  81.7 15.0 %collective-permute-done.19.rest_10_ = bf16[384,384]{1,0:T(8,128)(2,1)S(1)} collective-permute-done((bf16[384,384]{1,0:T(8,128)(2,1)}, bf16[384,384]{1,0:T(8,128)(2,1)S(1)}, u32[]{:S(2)}, u32[]{:S(2)}) %collective-permute-start.19) | collective-permute-done | bytes 294944 | tf_op jit(solution)/shard_map/ppermute | solution.py:54
  98.5 3.7 collective-permute-start.27
  103.9 8.0 %attend.1 = (bf16[2,128,1536]{2,1,0:T(8,128)(2,1)}, bf16[2,128,768]{2,1,0:T(8,128)(2,1)}, f32[2,1,768]{2,1,0:T(1,128)}, bf16[1536,768]{1,0:T(8,128)(2,1)}) custom-call(s32[16]{0:T(128)} %reshape.242.seen_ref, bf16[2,768,128]{2,1,0:T(8,128)(2,1)} %get-tuple-element.45.q_ref, bf16[2,2048,128]{2,1,0:T(8,128)(2,1)} %select_convert_fusion.mask_ref, ...), custom_call_target="tpu_custom_call" | custom-call | flops 2214592512 | bytes 6815744 | tf_op jit(solution)/shard_map/attend/pallas_call | solution.py:256
  113.8 4.7 collective-permute-done.28
  118.6 7.2 %collective-permute-done.27 = bf16[128,1664]{1,0:T(8,128)(2,1)S(1)} collective-permute-done((bf16[128,1664]{1,0:T(8,128)(2,1)S(1)}, bf16[128,1664]{1,0:T(8,128)(2,1)S(1)}, u32[]{:S(2)}, u32[]{:S(2)}) %collective-permute-start.27) | collective-permute-done | bytes 426016 | tf_op jit(solution)/shard_map/ppermute | solution.py:54
  127.5 2.7 second_norm.1
  130.5 4.3 collective-permute-start.23
  140.2 3.9 collective-permute-start.30
  145.0 14.2 %collective-permute-done.24 = bf16[128,1536]{1,0:T(8,128)(2,1)S(1)} collective-permute-done((bf16[128,1536]{1,0:T(8,128)(2,1)}, bf16[128,1536]{1,0:T(8,128)(2,1)S(1)}, u32[]{:S(2)}, u32[]{:S(2)}) %collective-permute-start.24) | collective-permute-done | bytes 393248 | tf_op jit(solution)/shard_map/ppermute | solution.py:54
  159.2 5.9 collective-permute-done.23
  170.0 3.9 collective-permute-start.33
  173.9 16.8 %collective-permute-done.34.rest_6_ = bf16[3,384,384]{2,1,0:T(8,128)(2,1)} collective-permute-done((bf16[3,384,384]{2,1,0:T(8,128)(2,1)}, bf16[3,384,384]{2,1,0:T(8,128)(2,1)}, u32[]{:S(2)}, u32[]{:S(2)}) %collective-permute-start.34) | collective-permute-done | bytes 884768 | tf_op jit(solution)/shard_map/ppermute | solution.py:54
  190.8 4.4 collective-permute-start.35
  198.7 3.5 pad_maximum_fusion.cx_ref
  202.2 3.4 pad_maximum_fusion.1.b_ref
  205.6 4.1 collective-permute-done.31.rest_2_
  209.7 18.5 %collective-permute-done.32.rest_3_ = bf16[3,384,384]{2,1,0:T(8,128)(2,1)} collective-permute-done((bf16[3,384,384]{2,1,0:T(8,128)(2,1)}, bf16[3,384,384]{2,1,0:T(8,128)(2,1)}, u32[]{:S(2)}, u32[]{:S(2)}) %collective-permute-start.32) | collective-permute-done | bytes 884768 | tf_op jit(solution)/shard_map/ppermute | solution.py:54
  228.2 48.6 %experts_step.1 = (bf16[2,512,1536]{2,1,0:T(8,128)(2,1)}, bf16[2,512,1664]{2,1,0:T(8,128)(2,1)}, bf16[3,384,384]{2,1,0:T(8,128)(2,1)}, bf16[3,384,384]{2,1,0:T(8...) custom-call(s32[3]{0:T(128)} %pad_add_fusion.place_ref, ...), custom_call_target="tpu_custom_call" | custom-call | flops 21743271936 | bytes 26738688 | tf_op jit(solution)/shard_map/experts_step/pallas_call | solution.py:445
  278.6 4.0 collective-permute-start.86
  285.3 17.7 %collective-permute-done.86 = bf16[3,384,384]{2,1,0:T(8,128)(2,1)S(1)} collective-permute-done((bf16[3,384,384]{2,1,0:T(8,128)(2,1)S(1)}, bf16[3,384,384]{2,1,0:T(8,128)(2,1)S(1)}, u32[]{:S(2)}, u32[]{:S(2)}) %collective-permute-start.86) | collective-permute-done | bytes 884768 | tf_op jit(solution)/shard_map/ppermute | solution.py:54
  303.8 3.2 collective-permute-done.83
  308.2 13.8 %collective-permute-done.85 = bf16[3,384,384]{2,1,0:T(8,128)(2,1)S(1)} collective-permute-done((bf16[3,384,384]{2,1,0:T(8,128)(2,1)S(1)}, bf16[3,384,384]{2,1,0:T(8,128)(2,1)S(1)}, u32[]{:S(2)}, u32[]{:S(2)}) %collective-permute-start.85) | collective-permute-done | bytes 884768 | tf_op jit(solution)/shard_map/ppermute | solution.py:54
  323.8 4.3 collective-permute-start.38
  331.1 19.8 %collective-permute-done.39 = bf16[128,1536]{1,0:T(8,128)(2,1)S(1)} collective-permute-done((bf16[128,1536]{1,0:T(8,128)(2,1)S(1)}, bf16[128,1536]{1,0:T(8,128)(2,1)S(1)}, u32[]{:S(2)}, u32[]{:S(2)}) %collective-permute-start.39) | collective-permute-done | bytes 393248 | tf_op jit(solution)/shard_map/ppermute | solution.py:54
  350.9 6.3 collective-permute-done.38
  357.2 3.4 collective-permute-start.43
  363.9 4.1 collective-permute-done.42.refs_1_
  368.0 47.2 %collective-permute-done.43.refs_2_ = bf16[128,1664]{1,0:T(8,128)(2,1)S(1)} collective-permute-done((bf16[128,1664]{1,0:T(8,128)(2,1)S(1)}, bf16[128,1664]{1,0:T(8,128)(2,1)S(1)}, u32[]{:S(2)}, u32[]{:S(2)}) %collective-permute-start.43) | collective-permute-done | bytes 426016 | tf_op jit(solution)/shard_map/ppermute | solution.py:54
  415.2 35.7 %collective-permute-done.44.refs_3_ = bf16[128,1664]{1,0:T(8,128)(2,1)S(1)} collective-permute-done((bf16[128,1664]{1,0:T(8,128)(2,1)S(1)}, bf16[128,1664]{1,0:T(8,128)(2,1)S(1)}, u32[]{:S(2)}, u32[]{:S(2)}) %collective-permute-start.44) | collective-permute-done | bytes 426016 | tf_op jit(solution)/shard_map/ppermute | solution.py:54
  451.6 5.7 second_norm_back.1
  460.0 9.8 %attend_back.1 = (bf16[2,128,1536]{2,1,0:T(8,128)(2,1)}, bf16[256,768]{1,0:T(8,128)(2,1)}, bf16[2,512,256]{2,1,0:T(8,128)(2,1)}, bf16[2,512,256]{2,1,0:T(8,128)(...) custom-call(s32[3]{0:T(128)} %pad_add_fusion.place_ref, s32[16]{0:T(128)} %reshape.242.seen_ref, ...), custom_call_target="tpu_custom_call" | custom-call | flops 4026531840 | bytes 6553600 | tf_op jit(solution)/shard_map/attend_back/pallas_call | solution.py:595
  469.9 2.8 collective-permute-start.47
  481.3 4.5 collective-permute-done.48
  485.8 2.8 collective-permute-start.74
  488.6 8.0 %collective-permute-done.47 = bf16[2,512,256]{2,1,0:T(8,128)(2,1)S(1)} collective-permute-done((bf16[2,512,256]{2,1,0:T(8,128)(2,1)}, bf16[2,512,256]{2,1,0:T(8,128)(2,1)S(1)}, u32[]{:S(2)}, u32[]{:S(2)}) %collective-permute-start.47) | collective-permute-done | bytes 524320 | tf_op jit(solution)/shard_map/ppermute | solution.py:54
  499.9 11.1 %collective-permute-done.65 = bf16[384,768]{1,0:T(8,128)(2,1)S(1)} collective-permute-done((bf16[384,768]{1,0:T(8,128)(2,1)S(1)}, bf16[384,768]{1,0:T(8,128)(2,1)S(1)}, u32[]{:S(2)}, u32[]{:S(2)}) %collective-permute-start.65) | collective-permute-done | bytes 589856 | tf_op jit(solution)/shard_map/ppermute | solution.py:54
  512.2 5.9 collective-permute-start.51
  519.8 5.5 collective-permute-done.51.refs_3_
  525.9 5.4 project_back.1
  536.6 3.7 first_norm_back.1
  549.2 7.8 %collective-permute-done.69 = bf16[96,768]{1,0:T(8,128)(2,1)S(1)} collective-permute-done((bf16[96,768]{1,0:T(8,128)(2,1)S(1)}, bf16[96,768]{1,0:T(8,128)(2,1)S(1)}, u32[]{:S(2)}, u32[]{:S(2)}) %collective-permute-start.69) | collective-permute-done | bytes 147488 | tf_op jit(solution)/shard_map/ppermute | solution.py:54
  558.2 3.0 collective-permute-done.68
  561.2 3.4 collective-permute-start.77
  564.8 4.7 collective-permute-done.78
  569.5 4.3 collective-permute-done.77
  573.8 3.4 collective-permute-start.71
  577.3 4.8 collective-permute-done.70
  582.1 4.3 collective-permute-done.71
  586.4 3.4 collective-permute-start.80
  589.9 4.8 collective-permute-done.79
  602.6 5.2 collective-permute-done.56
  612.4 3.2 collective-permute-done.57
  617.1 3.7 collective-permute-start.59
  621.0 2.8 collective-permute-done.60
  626.9 3.5 collective-permute-start.62
  638.9 8.6 %convert_bitcast_fusion = (f32[8,384,384]{1,2,0:T(8,128)}, f32[8,384,384]{2,1,0:T(8,128)}, f32[8,384,384]{2,1,0:T(8,128)}) fusion(bf16[8,3,384,384]{3,2,1,0:T(8,128)(2,1)} %all-gather.2.cloned.1.call-done), kind=kLoop, calls=%fused_computation | loop fusion | flops 3538944 | bytes 21233664 | tf_op jit(solution)/shard_map/transpose | solution.py:868
  647.4 6.0 copy.92
  (390 shorter events, 138.6 us)
Async XLA Ops:
  7.2 631.7 %all-gather.2.cloned.1.call-start = ((), (), s32[]{:S(2)}) async-start(), calls=%async_computation | async-start | bytes 8847360 | tf_op jit(solution)/shard_map/all_gather | solution.py:809
  9.9 20.5 %collective-permute-start.2 = (bf16[16,384]{1,0:T(8,128)(2,1)}, bf16[16,384]{1,0:T(8,128)(2,1)}, u32[]{:S(2)}, u32[]{:S(2)}) collective-permute-start(bf16[16,384]{1,0:T(8,128)(2,1)} %pad_maximum_fusion.22), channel_id=1, source_target_pairs={{0,24},{8,16},{16,8},{24,0},{1,25},{9,17},{17,9},{25,1},{2,26},{10... | collective-permute-start | bytes 36872 | tf_op jit(solution)/shard_map/ppermute | solution.py:54
  12.4 22.8 %collective-permute-start.1 = (bf16[16,384]{1,0:T(8,128)(2,1)}, bf16[16,384]{1,0:T(8,128)(2,1)}, u32[]{:S(2)}, u32[]{:S(2)}) collective-permute-start(bf16[16,384]{1,0:T(8,128)(2,1)} %pad_maximum_fusion.22), channel_id=1, source_target_pairs={{0,16},{8,24},{16,0},{24,8},{1,17},{9,25},{17,1},{25,9},{2,18},{10... | collective-permute-start | bytes 36872 | tf_op jit(solution)/shard_map/ppermute | solution.py:54
  14.2 31.7 %collective-permute-start.4 = (bf16[384,512]{1,0:T(8,128)(2,1)S(1)}, bf16[384,512]{1,0:T(8,128)(2,1)S(1)}, u32[]{:S(2)}, u32[]{:S(2)}) collective-permute-start(bf16[384,512]{1,0:T(8,128)(2,1)S(1)} %get-tuple-element.180.rest_1_), channel_id=1, source_target_pairs={{0,8},{8,0},{16,24},{24,16},{1,9},{9,1},{17,25},{25,17},{2,10},{10... | collective-permute-start | bytes 1179656 | tf_op jit(solution)/shard_map/ppermute | solution.py:54
  14.8 19.8 %collective-permute-start.6 = (bf16[384,512]{1,0:T(8,128)(2,1)S(1)}, bf16[384,512]{1,0:T(8,128)(2,1)S(1)}, u32[]{:S(2)}, u32[]{:S(2)}) collective-permute-start(bf16[384,512]{1,0:T(8,128)(2,1)S(1)} %get-tuple-element.180.rest_1_), channel_id=1, source_target_pairs={{0,16},{8,24},{16,0},{24,8},{1,17},{9,25},{17,1},{25,9},{2,18},{10... | collective-permute-start | bytes 1179656 | tf_op jit(solution)/shard_map/ppermute | solution.py:54
  16.3 16.8 %collective-permute-start.3 = (bf16[384,512]{1,0:T(8,128)(2,1)S(1)}, bf16[384,512]{1,0:T(8,128)(2,1)}, u32[]{:S(2)}, u32[]{:S(2)}) collective-permute-start(bf16[384,512]{1,0:T(8,128)(2,1)S(1)} %get-tuple-element.181.rest_0_), channel_id=1, source_target_pairs={{0,8},{8,0},{16,24},{24,16},{1,9},{9,1},{17,25},{25,17},{2,10},{10... | collective-permute-start | bytes 1179656 | tf_op jit(solution)/shard_map/ppermute | solution.py:54
  30.4 16.0 %collective-permute-start.5 = (bf16[384,512]{1,0:T(8,128)(2,1)S(1)}, bf16[384,512]{1,0:T(8,128)(2,1)S(1)}, u32[]{:S(2)}, u32[]{:S(2)}) collective-permute-start(bf16[384,512]{1,0:T(8,128)(2,1)S(1)} %get-tuple-element.181.rest_0_), channel_id=1, source_target_pairs={{0,16},{8,24},{16,0},{24,8},{1,17},{9,25},{17,1},{25,9},{2,18},{10... | collective-permute-start | bytes 1179656 | tf_op jit(solution)/shard_map/ppermute | solution.py:54
  33.1 17.9 %collective-permute-start.7 = (bf16[384,512]{1,0:T(8,128)(2,1)}, bf16[384,512]{1,0:T(8,128)(2,1)S(1)}, u32[]{:S(2)}, u32[]{:S(2)}) collective-permute-start(bf16[384,512]{1,0:T(8,128)(2,1)} %collective-permute-done.3.rest_2_), channel_id=1, source_target_pairs={{0,16},{8,24},{16,0},{24,8},{1,17},{9,25},{17,1},{25,9},{2,18},{10... | collective-permute-start | bytes 1179656 | tf_op jit(solution)/shard_map/ppermute | solution.py:54
  34.6 16.3 %collective-permute-start.8 = (bf16[384,512]{1,0:T(8,128)(2,1)S(1)}, bf16[384,512]{1,0:T(8,128)(2,1)S(1)}, u32[]{:S(2)}, u32[]{:S(2)}) collective-permute-start(bf16[384,512]{1,0:T(8,128)(2,1)S(1)} %collective-permute-done.6.rest_5_), channel_id=1, source_target_pairs={{0,8},{8,0},{16,24},{24,16},{1,9},{9,1},{17,25},{25,17},{2,10},{10... | collective-permute-start | bytes 1179656 | tf_op jit(solution)/shard_map/ppermute | solution.py:54
  43.9 24.7 %collective-permute-start.15 = (bf16[384,384]{1,0:T(8,128)(2,1)}, bf16[384,384]{1,0:T(8,128)(2,1)}, u32[]{:S(2)}, u32[]{:S(2)}) collective-permute-start(bf16[384,384]{1,0:T(8,128)(2,1)} %get-tuple-element.179.rest_4_), channel_id=1, source_target_pairs={{0,8},{8,0},{16,24},{24,16},{1,9},{9,1},{17,25},{25,17},{2,10},{10... | collective-permute-start | bytes 884744 | tf_op jit(solution)/shard_map/ppermute | solution.py:54
  45.9 26.2 %collective-permute-start.17 = (bf16[384,384]{1,0:T(8,128)(2,1)}, bf16[384,384]{1,0:T(8,128)(2,1)S(1)}, u32[]{:S(2)}, u32[]{:S(2)}) collective-permute-start(bf16[384,384]{1,0:T(8,128)(2,1)} %get-tuple-element.179.rest_4_), channel_id=1, source_target_pairs={{0,16},{8,24},{16,0},{24,8},{1,17},{9,25},{17,1},{25,9},{2,18},{10... | collective-permute-start | bytes 884744 | tf_op jit(solution)/shard_map/ppermute | solution.py:54
  46.4 22.7 %collective-permute-start.16 = (bf16[384,384]{1,0:T(8,128)(2,1)}, bf16[384,384]{1,0:T(8,128)(2,1)}, u32[]{:S(2)}, u32[]{:S(2)}) collective-permute-start(bf16[384,384]{1,0:T(8,128)(2,1)} %get-tuple-element.178.rest_5_), channel_id=1, source_target_pairs={{0,8},{8,0},{16,24},{24,16},{1,9},{9,1},{17,25},{25,17},{2,10},{10... | collective-permute-start | bytes 884744 | tf_op jit(solution)/shard_map/ppermute | solution.py:54
  65.4 15.8 %collective-permute-start.18 = (bf16[384,384]{1,0:T(8,128)(2,1)}, bf16[384,384]{1,0:T(8,128)(2,1)S(1)}, u32[]{:S(2)}, u32[]{:S(2)}) collective-permute-start(bf16[384,384]{1,0:T(8,128)(2,1)} %get-tuple-element.178.rest_5_), channel_id=1, source_target_pairs={{0,16},{8,24},{16,0},{24,8},{1,17},{9,25},{17,1},{25,9},{2,18},{10... | collective-permute-start | bytes 884744 | tf_op jit(solution)/shard_map/ppermute | solution.py:54
  68.5 33.6 %collective-permute-start.12 = (bf16[2,512,256]{2,1,0:T(8,128)(2,1)S(1)}, bf16[2,512,256]{2,1,0:T(8,128)(2,1)S(1)}, u32[]{:S(2)}, u32[]{:S(2)}) collective-permute-start(bf16[2,512,256]{2,1,0:T(8,128)(2,1)S(1)} %constant_dynamic-update-slice_fusion.rest_0_), channel_id=1, source_target_pairs={{0,8},{8,0},{16,24},{24,16},{1,9},{9,1},{17,25},{25,17},{2,10},{10... | collective-permute-start | bytes 1572872 | tf_op jit(solution)/shard_map/ppermute | solution.py:54
  68.6 33.6 %collective-permute-start.13 = (bf16[2,512,256]{2,1,0:T(8,128)(2,1)S(1)}, bf16[2,512,256]{2,1,0:T(8,128)(2,1)S(1)}, u32[]{:S(2)}, u32[]{:S(2)}) collective-permute-start(bf16[2,512,256]{2,1,0:T(8,128)(2,1)S(1)} %constant_dynamic-update-slice_fusion.rest_0_), channel_id=1, source_target_pairs={{0,16},{8,24},{16,0},{24,8},{1,17},{9,25},{17,1},{25,9},{2,18},{10... | collective-permute-start | bytes 1572872 | tf_op jit(solution)/shard_map/ppermute | solution.py:54
  69.2 33.1 %collective-permute-start.14 = (bf16[2,512,256]{2,1,0:T(8,128)(2,1)S(1)}, bf16[2,512,256]{2,1,0:T(8,128)(2,1)S(1)}, u32[]{:S(2)}, u32[]{:S(2)}) collective-permute-start(bf16[2,512,256]{2,1,0:T(8,128)(2,1)S(1)} %constant_dynamic-update-slice_fusion.rest_0_), channel_id=1, source_target_pairs={{0,24},{8,16},{16,8},{24,0},{1,25},{9,17},{17,9},{25,1},{2,26},{10... | collective-permute-start | bytes 1572872 | tf_op jit(solution)/shard_map/ppermute | solution.py:54
  72.1 24.6 %collective-permute-start.19 = (bf16[384,384]{1,0:T(8,128)(2,1)}, bf16[384,384]{1,0:T(8,128)(2,1)S(1)}, u32[]{:S(2)}, u32[]{:S(2)}) collective-permute-start(bf16[384,384]{1,0:T(8,128)(2,1)} %collective-permute-done.15.rest_6_), channel_id=1, source_target_pairs={{0,16},{8,24},{16,0},{24,8},{1,17},{9,25},{17,1},{25,9},{2,18},{10... | collective-permute-start | bytes 884744 | tf_op jit(solution)/shard_map/ppermute | solution.py:54
  81.2 17.3 %collective-permute-start.20 = (bf16[384,384]{1,0:T(8,128)(2,1)S(1)}, bf16[384,384]{1,0:T(8,128)(2,1)}, u32[]{:S(2)}, u32[]{:S(2)}) collective-permute-start(bf16[384,384]{1,0:T(8,128)(2,1)S(1)} %collective-permute-done.18.rest_9_), channel_id=1, source_target_pairs={{0,8},{8,0},{16,24},{24,16},{1,9},{9,1},{17,25},{25,17},{2,10},{10... | collective-permute-start | bytes 884744 | tf_op jit(solution)/shard_map/ppermute | solution.py:54
  96.7 21.9 %collective-permute-start.28 = (bf16[128,1664]{1,0:T(8,128)(2,1)S(1)}, bf16[128,1664]{1,0:T(8,128)(2,1)S(1)}, u32[]{:S(2)}, u32[]{:S(2)}) collective-permute-start(bf16[128,1664]{1,0:T(8,128)(2,1)S(1)} %convert_dynamic-update-slice_fusion.refs_6_), channel_id=1, source_target_pairs={{0,6},{2,4},{4,2},{6,0},{1,7},{3,5},{5,3},{7,1},{8,14},{10,12},{12... | collective-permute-start | bytes 1277960 | tf_op jit(solution)/shard_map/ppermute | solution.py:54
  98.5 27.3 %collective-permute-start.27 = (bf16[128,1664]{1,0:T(8,128)(2,1)S(1)}, bf16[128,1664]{1,0:T(8,128)(2,1)S(1)}, u32[]{:S(2)}, u32[]{:S(2)}) collective-permute-start(bf16[128,1664]{1,0:T(8,128)(2,1)S(1)} %convert_dynamic-update-slice_fusion.refs_6_), channel_id=1, source_target_pairs={{0,4},{2,6},{4,0},{6,2},{1,5},{3,7},{5,1},{7,3},{8,12},{10,14},{12... | collective-permute-start | bytes 1277960 | tf_op jit(solution)/shard_map/ppermute | solution.py:54
  102.1 23.6 %collective-permute-start.26 = (bf16[128,1664]{1,0:T(8,128)(2,1)S(1)}, bf16[128,1664]{1,0:T(8,128)(2,1)S(1)}, u32[]{:S(2)}, u32[]{:S(2)}) collective-permute-start(bf16[128,1664]{1,0:T(8,128)(2,1)S(1)} %convert_dynamic-update-slice_fusion.refs_6_), channel_id=1, source_target_pairs={{0,2},{2,0},{4,6},{6,4},{1,3},{3,1},{5,7},{7,5},{8,10},{10,8},{12,... | collective-permute-start | bytes 1277960 | tf_op jit(solution)/shard_map/ppermute | solution.py:54
  113.8 12.9 %collective-permute-start.21 = (bf16[128,1536]{1,0:T(8,128)(2,1)}, bf16[128,1536]{1,0:T(8,128)(2,1)S(1)}, u32[]{:S(2)}, u32[]{:S(2)}) collective-permute-start(bf16[128,1536]{1,0:T(8,128)(2,1)} %select_bitcast_fusion.5), channel_id=1, source_target_pairs={{0,1},{1,0},{2,3},{3,2},{4,5},{5,4},{6,7},{7,6},{8,9},{9,8},{10,11... | collective-permute-start | bytes 1179656 | tf_op jit(solution)/shard_map/ppermute | solution.py:54
  126.0 64.8 %collective-permute-start.29 = (bf16[4,128,1664]{2,1,0:T(8,128)(2,1)S(1)}, bf16[4,128,1664]{2,1,0:T(8,128)(2,1)}, u32[]{:S(2)}, u32[]{:S(2)}) collective-permute-start(bf16[4,128,1664]{2,1,0:T(8,128)(2,1)S(1)} %pad_maximum_fusion.3), channel_id=1, source_target_pairs={{0,1},{1,0},{2,3},{3,2},{4,5},{5,4},{6,7},{7,6},{8,9},{9,8},{10,11... | collective-permute-start | bytes 5111816 | tf_op jit(solution)/shard_map/ppermute | solution.py:54
  130.2 29.0 %collective-permute-start.24 = (bf16[128,1536]{1,0:T(8,128)(2,1)}, bf16[128,1536]{1,0:T(8,128)(2,1)S(1)}, u32[]{:S(2)}, u32[]{:S(2)}) collective-permute-start(bf16[128,1536]{1,0:T(8,128)(2,1)} %get-tuple-element.49.refs_5_), channel_id=1, source_target_pairs={{0,6},{2,4},{4,2},{6,0},{1,7},{3,5},{5,3},{7,1},{8,14},{10,12},{12... | collective-permute-start | bytes 1179656 | tf_op jit(solution)/shard_map/ppermute | solution.py:54
  130.5 34.7 %collective-permute-start.23 = (bf16[128,1536]{1,0:T(8,128)(2,1)}, bf16[128,1536]{1,0:T(8,128)(2,1)}, u32[]{:S(2)}, u32[]{:S(2)}) collective-permute-start(bf16[128,1536]{1,0:T(8,128)(2,1)} %get-tuple-element.49.refs_5_), channel_id=1, source_target_pairs={{0,4},{2,6},{4,0},{6,2},{1,5},{3,7},{5,1},{7,3},{8,12},{10,14},{12... | collective-permute-start | bytes 1179656 | tf_op jit(solution)/shard_map/ppermute | solution.py:54
  134.7 30.4 %collective-permute-start.22 = (bf16[128,1536]{1,0:T(8,128)(2,1)}, bf16[128,1536]{1,0:T(8,128)(2,1)}, u32[]{:S(2)}, u32[]{:S(2)}) collective-permute-start(bf16[128,1536]{1,0:T(8,128)(2,1)} %get-tuple-element.49.refs_5_), channel_id=1, source_target_pairs={{0,2},{2,0},{4,6},{6,4},{1,3},{3,1},{5,7},{7,5},{8,10},{10,8},{12,... | collective-permute-start | bytes 1179656 | tf_op jit(solution)/shard_map/ppermute | solution.py:54
  140.2 29.8 %collective-permute-start.30 = (bf16[3,384,384]{2,1,0:T(8,128)(2,1)}, bf16[3,384,384]{2,1,0:T(8,128)(2,1)}, u32[]{:S(2)}, u32[]{:S(2)}) collective-permute-start(bf16[3,384,384]{2,1,0:T(8,128)(2,1)} %pad_maximum_fusion.6.rest_0_), channel_id=1, source_target_pairs={{0,8},{8,0},{16,24},{24,16},{1,9},{9,1},{17,25},{25,17},{2,10},{10... | collective-permute-start | bytes 2654216 | tf_op jit(solution)/shard_map/ppermute | solution.py:54
  166.8 35.4 %collective-permute-start.25 = (bf16[4,128,1536]{2,1,0:T(8,128)(2,1)S(1)}, bf16[4,128,1536]{2,1,0:T(8,128)(2,1)}, u32[]{:S(2)}, u32[]{:S(2)}) collective-permute-start(bf16[4,128,1536]{2,1,0:T(8,128)(2,1)S(1)} %pad_maximum_fusion.4), channel_id=1, source_target_pairs={{0,1},{1,0},{2,3},{3,2},{4,5},{5,4},{6,7},{7,6},{8,9},{9,8},{10,11... | collective-permute-start | bytes 4718600 | tf_op jit(solution)/shard_map/ppermute | solution.py:54
  168.0 22.8 %collective-permute-start.34 = (bf16[3,384,384]{2,1,0:T(8,128)(2,1)}, bf16[3,384,384]{2,1,0:T(8,128)(2,1)}, u32[]{:S(2)}, u32[]{:S(2)}) collective-permute-start(bf16[3,384,384]{2,1,0:T(8,128)(2,1)} %pad_maximum_fusion.7.rest_4_), channel_id=1, source_target_pairs={{0,16},{8,24},{16,0},{24,8},{1,17},{9,25},{17,1},{25,9},{2,18},{10... | collective-permute-start | bytes 2654216 | tf_op jit(solution)/shard_map/ppermute | solution.py:54
  168.0 41.7 %collective-permute-start.31 = (bf16[3,384,384]{2,1,0:T(8,128)(2,1)}, bf16[3,384,384]{2,1,0:T(8,128)(2,1)}, u32[]{:S(2)}, u32[]{:S(2)}) collective-permute-start(bf16[3,384,384]{2,1,0:T(8,128)(2,1)} %pad_maximum_fusion.6.rest_0_), channel_id=1, source_target_pairs={{0,16},{8,24},{16,0},{24,8},{1,17},{9,25},{17,1},{25,9},{2,18},{10... | collective-permute-start | bytes 2654216 | tf_op jit(solution)/shard_map/ppermute | solution.py:54
  170.0 39.7 %collective-permute-start.33 = (bf16[3,384,384]{2,1,0:T(8,128)(2,1)}, bf16[3,384,384]{2,1,0:T(8,128)(2,1)}, u32[]{:S(2)}, u32[]{:S(2)}) collective-permute-start(bf16[3,384,384]{2,1,0:T(8,128)(2,1)} %pad_maximum_fusion.7.rest_4_), channel_id=1, source_target_pairs={{0,8},{8,0},{16,24},{24,16},{1,9},{9,1},{17,25},{25,17},{2,10},{10... | collective-permute-start | bytes 2654216 | tf_op jit(solution)/shard_map/ppermute | solution.py:54
  190.7 37.5 %collective-permute-start.32 = (bf16[3,384,384]{2,1,0:T(8,128)(2,1)}, bf16[3,384,384]{2,1,0:T(8,128)(2,1)}, u32[]{:S(2)}, u32[]{:S(2)}) collective-permute-start(bf16[3,384,384]{2,1,0:T(8,128)(2,1)} %collective-permute-done.30.rest_1_), channel_id=1, source_target_pairs={{0,16},{8,24},{16,0},{24,8},{1,17},{9,25},{17,1},{25,9},{2,18},{10... | collective-permute-start | bytes 2654216 | tf_op jit(solution)/shard_map/ppermute | solution.py:54
  190.8 37.4 %collective-permute-start.35 = (bf16[3,384,384]{2,1,0:T(8,128)(2,1)}, bf16[3,384,384]{2,1,0:T(8,128)(2,1)}, u32[]{:S(2)}, u32[]{:S(2)}) collective-permute-start(bf16[3,384,384]{2,1,0:T(8,128)(2,1)} %collective-permute-done.34.rest_6_), channel_id=1, source_target_pairs={{0,8},{8,0},{16,24},{24,16},{1,9},{9,1},{17,25},{25,17},{2,10},{10... | collective-permute-start | bytes 2654216 | tf_op jit(solution)/shard_map/ppermute | solution.py:54
  278.5 29.3 %collective-permute-start.36 = (bf16[4,128,1536]{2,1,0:T(8,128)(2,1)S(1)}, bf16[4,128,1536]{2,1,0:T(8,128)(2,1)S(1)}, u32[]{:S(2)}, u32[]{:S(2)}) collective-permute-start(bf16[4,128,1536]{2,1,0:T(8,128)(2,1)S(1)} %bitcast.228), channel_id=1, source_target_pairs={{0,1},{1,0},{2,3},{3,2},{4,5},{5,4},{6,7},{7,6},{8,9},{9,8},{10,11... | collective-permute-start | bytes 4718600 | tf_op jit(solution)/shard_map/ppermute | solution.py:54
  278.6 24.5 %collective-permute-start.86 = (bf16[3,384,384]{2,1,0:T(8,128)(2,1)S(1)}, bf16[3,384,384]{2,1,0:T(8,128)(2,1)S(1)}, u32[]{:S(2)}, u32[]{:S(2)}) collective-permute-start(bf16[3,384,384]{2,1,0:T(8,128)(2,1)S(1)} %copy-done.54), channel_id=1, source_target_pairs={{0,8},{8,0},{16,24},{24,16},{1,9},{9,1},{17,25},{25,17},{2,10},{10... | collective-permute-start | bytes 2654216 | tf_op jit(solution)/shard_map/ppermute | solution.py:54
  284.3 39.5 %collective-permute-start.41 = (bf16[4,128,1664]{2,1,0:T(8,128)(2,1)S(1)}, bf16[4,128,1664]{2,1,0:T(8,128)(2,1)S(1)}, u32[]{:S(2)}, u32[]{:S(2)}) collective-permute-start(bf16[4,128,1664]{2,1,0:T(8,128)(2,1)S(1)} %bitcast.227), channel_id=1, source_target_pairs={{0,1},{1,0},{2,3},{3,2},{4,5},{5,4},{6,7},{7,6},{8,9},{9,8},{10,11... | collective-permute-start | bytes 5111816 | tf_op jit(solution)/shard_map/ppermute | solution.py:54
  284.5 22.5 %collective-permute-start.83 = (bf16[3,384,384]{2,1,0:T(8,128)(2,1)S(1)}, bf16[3,384,384]{2,1,0:T(8,128)(2,1)S(1)}, u32[]{:S(2)}, u32[]{:S(2)}) collective-permute-start(bf16[3,384,384]{2,1,0:T(8,128)(2,1)S(1)} %copy-done.53), channel_id=1, source_target_pairs={{0,16},{8,24},{16,0},{24,8},{1,17},{9,25},{17,1},{25,9},{2,18},{10... | collective-permute-start | bytes 2654216 | tf_op jit(solution)/shard_map/ppermute | solution.py:54
  285.0 37.0 %collective-permute-start.85 = (bf16[3,384,384]{2,1,0:T(8,128)(2,1)S(1)}, bf16[3,384,384]{2,1,0:T(8,128)(2,1)S(1)}, u32[]{:S(2)}, u32[]{:S(2)}) collective-permute-start(bf16[3,384,384]{2,1,0:T(8,128)(2,1)S(1)} %copy-done.52), channel_id=1, source_target_pairs={{0,8},{8,0},{16,24},{24,16},{1,9},{9,1},{17,25},{25,17},{2,10},{10... | collective-permute-start | bytes 2654216 | tf_op jit(solution)/shard_map/ppermute | solution.py:54
  303.3 24.8 %collective-permute-start.87 = (bf16[3,384,384]{2,1,0:T(8,128)(2,1)S(1)}, bf16[3,384,384]{2,1,0:T(8,128)(2,1)S(1)}, u32[]{:S(2)}, u32[]{:S(2)}) collective-permute-start(bf16[3,384,384]{2,1,0:T(8,128)(2,1)S(1)} %add_convert_fusion.1), channel_id=1, source_target_pairs={{0,16},{8,24},{16,0},{24,8},{1,17},{9,25},{17,1},{25,9},{2,18},{10... | collective-permute-start | bytes 2654216 | tf_op jit(solution)/shard_map/ppermute | solution.py:54
  307.0 54.2 %collective-permute-start.82 = (bf16[3,384,384]{2,1,0:T(8,128)(2,1)S(1)}, bf16[3,384,384]{2,1,0:T(8,128)(2,1)S(1)}, u32[]{:S(2)}, u32[]{:S(2)}) collective-permute-start(bf16[3,384,384]{2,1,0:T(8,128)(2,1)S(1)} %copy-done.51), channel_id=1, source_target_pairs={{0,16},{8,24},{16,0},{24,8},{1,17},{9,25},{17,1},{25,9},{2,18},{10... | collective-permute-start | bytes 2654216 | tf_op jit(solution)/shard_map/ppermute | solution.py:54
  307.8 53.6 %collective-permute-start.84 = (bf16[3,384,384]{2,1,0:T(8,128)(2,1)S(1)}, bf16[3,384,384]{2,1,0:T(8,128)(2,1)S(1)}, u32[]{:S(2)}, u32[]{:S(2)}) collective-permute-start(bf16[3,384,384]{2,1,0:T(8,128)(2,1)S(1)} %add_convert_fusion.4), channel_id=1, source_target_pairs={{0,8},{8,0},{16,24},{24,16},{1,9},{9,1},{17,25},{25,17},{2,10},{10... | collective-permute-start | bytes 2654216 | tf_op jit(solution)/shard_map/ppermute | solution.py:54
  322.0 28.9 %collective-permute-start.39 = (bf16[128,1536]{1,0:T(8,128)(2,1)S(1)}, bf16[128,1536]{1,0:T(8,128)(2,1)S(1)}, u32[]{:S(2)}, u32[]{:S(2)}) collective-permute-start(bf16[128,1536]{1,0:T(8,128)(2,1)S(1)} %get-tuple-element.138), channel_id=1, source_target_pairs={{0,6},{2,4},{4,2},{6,0},{1,7},{3,5},{5,3},{7,1},{8,14},{10,12},{12... | collective-permute-start | bytes 1179656 | tf_op jit(solution)/shard_map/ppermute | solution.py:54
  323.8 33.4 %collective-permute-start.38 = (bf16[128,1536]{1,0:T(8,128)(2,1)S(1)}, bf16[128,1536]{1,0:T(8,128)(2,1)S(1)}, u32[]{:S(2)}, u32[]{:S(2)}) collective-permute-start(bf16[128,1536]{1,0:T(8,128)(2,1)S(1)} %get-tuple-element.139), channel_id=1, source_target_pairs={{0,4},{2,6},{4,0},{6,2},{1,5},{3,7},{5,1},{7,3},{8,12},{10,14},{12... | collective-permute-start | bytes 1179656 | tf_op jit(solution)/shard_map/ppermute | solution.py:54
  328.0 32.6 %collective-permute-start.37 = (bf16[128,1536]{1,0:T(8,128)(2,1)S(1)}, bf16[128,1536]{1,0:T(8,128)(2,1)S(1)}, u32[]{:S(2)}, u32[]{:S(2)}) collective-permute-start(bf16[128,1536]{1,0:T(8,128)(2,1)S(1)} %get-tuple-element.137), channel_id=1, source_target_pairs={{0,2},{2,0},{4,6},{6,4},{1,3},{3,1},{5,7},{7,5},{8,10},{10,8},{12,... | collective-permute-start | bytes 1179656 | tf_op jit(solution)/shard_map/ppermute | solution.py:54
  350.9 17.1 %collective-permute-start.42 = (bf16[128,1664]{1,0:T(8,128)(2,1)S(1)}, bf16[128,1664]{1,0:T(8,128)(2,1)S(1)}, u32[]{:S(2)}, u32[]{:S(2)}) collective-permute-start(bf16[128,1664]{1,0:T(8,128)(2,1)S(1)} %get-tuple-element.135), channel_id=1, source_target_pairs={{0,2},{2,0},{4,6},{6,4},{1,3},{3,1},{5,7},{7,5},{8,10},{10,8},{12,... | collective-permute-start | bytes 1277960 | tf_op jit(solution)/shard_map/ppermute | solution.py:54
  357.2 58.0 %collective-permute-start.43 = (bf16[128,1664]{1,0:T(8,128)(2,1)S(1)}, bf16[128,1664]{1,0:T(8,128)(2,1)S(1)}, u32[]{:S(2)}, u32[]{:S(2)}) collective-permute-start(bf16[128,1664]{1,0:T(8,128)(2,1)S(1)} %get-tuple-element.134), channel_id=1, source_target_pairs={{0,4},{2,6},{4,0},{6,2},{1,5},{3,7},{5,1},{7,3},{8,12},{10,14},{12... | collective-permute-start | bytes 1277960 | tf_op jit(solution)/shard_map/ppermute | solution.py:54
  360.6 90.2 %collective-permute-start.44 = (bf16[128,1664]{1,0:T(8,128)(2,1)S(1)}, bf16[128,1664]{1,0:T(8,128)(2,1)S(1)}, u32[]{:S(2)}, u32[]{:S(2)}) collective-permute-start(bf16[128,1664]{1,0:T(8,128)(2,1)S(1)} %get-tuple-element.133), channel_id=1, source_target_pairs={{0,6},{2,4},{4,2},{6,0},{1,7},{3,5},{5,3},{7,1},{8,14},{10,12},{12... | collective-permute-start | bytes 1277960 | tf_op jit(solution)/shard_map/ppermute | solution.py:54
  361.2 96.1 %collective-permute-start.40 = (bf16[128,1536]{1,0:T(8,128)(2,1)S(1)}, bf16[128,1536]{1,0:T(8,128)(2,1)S(1)}, u32[]{:S(2)}, u32[]{:S(2)}) collective-permute-start(bf16[128,1536]{1,0:T(8,128)(2,1)S(1)} %add_convert_fusion.8), channel_id=1, source_target_pairs={{0,1},{1,0},{2,3},{3,2},{4,5},{5,4},{6,7},{7,6},{8,9},{9,8},{10,11... | collective-permute-start | bytes 1179656 | tf_op jit(solution)/shard_map/ppermute | solution.py:54
  469.8 16.0 %collective-permute-start.48 = (bf16[2,512,256]{2,1,0:T(8,128)(2,1)}, bf16[2,512,256]{2,1,0:T(8,128)(2,1)S(1)}, u32[]{:S(2)}, u32[]{:S(2)}) collective-permute-start(bf16[2,512,256]{2,1,0:T(8,128)(2,1)} %get-tuple-element.59), channel_id=1, source_target_pairs={{0,24},{8,16},{16,8},{24,0},{1,25},{9,17},{17,9},{25,1},{2,26},{10... | collective-permute-start | bytes 1572872 | tf_op jit(solution)/shard_map/ppermute | solution.py:54
  469.9 26.7 %collective-permute-start.47 = (bf16[2,512,256]{2,1,0:T(8,128)(2,1)}, bf16[2,512,256]{2,1,0:T(8,128)(2,1)S(1)}, u32[]{:S(2)}, u32[]{:S(2)}) collective-permute-start(bf16[2,512,256]{2,1,0:T(8,128)(2,1)} %get-tuple-element.58), channel_id=1, source_target_pairs={{0,16},{8,24},{16,0},{24,8},{1,17},{9,25},{17,1},{25,9},{2,18},{10... | collective-permute-start | bytes 1572872 | tf_op jit(solution)/shard_map/ppermute | solution.py:54
  472.7 26.2 %collective-permute-start.46 = (bf16[2,512,256]{2,1,0:T(8,128)(2,1)}, bf16[2,512,256]{2,1,0:T(8,128)(2,1)S(1)}, u32[]{:S(2)}, u32[]{:S(2)}) collective-permute-start(bf16[2,512,256]{2,1,0:T(8,128)(2,1)} %get-tuple-element.57), channel_id=1, source_target_pairs={{0,8},{8,0},{16,24},{24,16},{1,9},{9,1},{17,25},{25,17},{2,10},{10... | collective-permute-start | bytes 1572872 | tf_op jit(solution)/shard_map/ppermute | solution.py:54
  477.7 33.3 %collective-permute-start.65 = (bf16[384,768]{1,0:T(8,128)(2,1)S(1)}, bf16[384,768]{1,0:T(8,128)(2,1)S(1)}, u32[]{:S(2)}, u32[]{:S(2)}) collective-permute-start(bf16[384,768]{1,0:T(8,128)(2,1)S(1)} %convolution_convert_fusion.4), channel_id=1, source_target_pairs={{0,8},{8,0},{16,24},{24,16},{1,9},{9,1},{17,25},{25,17},{2,10},{10... | collective-permute-start | bytes 1769480 | tf_op jit(solution)/shard_map/ppermute | solution.py:54
  479.9 61.7 %collective-permute-start.64 = (bf16[384,768]{1,0:T(8,128)(2,1)}, bf16[384,768]{1,0:T(8,128)(2,1)}, u32[]{:S(2)}, u32[]{:S(2)}) collective-permute-start(bf16[384,768]{1,0:T(8,128)(2,1)} %convolution_convert_fusion.6), channel_id=1, source_target_pairs={{0,8},{8,0},{16,24},{24,16},{1,9},{9,1},{17,25},{25,17},{2,10},{10... | collective-permute-start | bytes 1769480 | tf_op jit(solution)/shard_map/ppermute | solution.py:54
  485.8 26.4 %collective-permute-start.74 = (bf16[384,768]{1,0:T(8,128)(2,1)S(1)}, bf16[384,768]{1,0:T(8,128)(2,1)S(1)}, u32[]{:S(2)}, u32[]{:S(2)}) collective-permute-start(bf16[384,768]{1,0:T(8,128)(2,1)S(1)} %convolution_convert_fusion), channel_id=1, source_target_pairs={{0,16},{8,24},{16,0},{24,8},{1,17},{9,25},{17,1},{25,9},{2,18},{10... | collective-permute-start | bytes 1769480 | tf_op jit(solution)/shard_map/ppermute | solution.py:54
  496.6 49.4 %collective-permute-start.73 = (bf16[384,768]{1,0:T(8,128)(2,1)}, bf16[384,768]{1,0:T(8,128)(2,1)}, u32[]{:S(2)}, u32[]{:S(2)}) collective-permute-start(bf16[384,768]{1,0:T(8,128)(2,1)} %convolution_convert_fusion.2), channel_id=1, source_target_pairs={{0,16},{8,24},{16,0},{24,8},{1,17},{9,25},{17,1},{25,9},{2,18},{10... | collective-permute-start | bytes 1769480 | tf_op jit(solution)/shard_map/ppermute | solution.py:54
  499.9 19.4 %collective-permute-start.49 = (bf16[2,128,256]{2,1,0:T(8,128)(2,1)S(1)}, bf16[2,128,256]{2,1,0:T(8,128)(2,1)S(1)}, u32[]{:S(2)}, u32[]{:S(2)}) collective-permute-start(bf16[2,128,256]{2,1,0:T(8,128)(2,1)S(1)} %get-tuple-element.184), channel_id=1, source_target_pairs={{0,2},{2,0},{4,6},{6,4},{1,3},{3,1},{5,7},{7,5},{8,10},{10,8},{12,... | collective-permute-start | bytes 393224 | tf_op jit(solution)/shard_map/ppermute | solution.py:54
  512.2 13.1 %collective-permute-start.51 = (bf16[2,128,256]{2,1,0:T(8,128)(2,1)S(1)}, bf16[2,128,256]{2,1,0:T(8,128)(2,1)S(1)}, u32[]{:S(2)}, u32[]{:S(2)}) collective-permute-start(bf16[2,128,256]{2,1,0:T(8,128)(2,1)S(1)} %get-tuple-element.182), channel_id=1, source_target_pairs={{0,6},{2,4},{4,2},{6,0},{1,7},{3,5},{5,3},{7,1},{8,14},{10,12},{12... | collective-permute-start | bytes 393224 | tf_op jit(solution)/shard_map/ppermute | solution.py:54
  519.3 22.8 %collective-permute-start.66 = (bf16[384,768]{1,0:T(8,128)(2,1)}, bf16[384,768]{1,0:T(8,128)(2,1)}, u32[]{:S(2)}, u32[]{:S(2)}) collective-permute-start(bf16[384,768]{1,0:T(8,128)(2,1)} %fusion.13), channel_id=1, source_target_pairs={{0,16},{8,24},{16,0},{24,8},{1,17},{9,25},{17,1},{25,9},{2,18},{10... | collective-permute-start | bytes 1769480 | tf_op jit(solution)/shard_map/ppermute | solution.py:54
  519.3 28.0 %collective-permute-start.75 = (bf16[384,768]{1,0:T(8,128)(2,1)}, bf16[384,768]{1,0:T(8,128)(2,1)}, u32[]{:S(2)}, u32[]{:S(2)}) collective-permute-start(bf16[384,768]{1,0:T(8,128)(2,1)} %fusion.4), channel_id=1, source_target_pairs={{0,8},{8,0},{16,24},{24,16},{1,9},{9,1},{17,25},{25,17},{2,10},{10... | collective-permute-start | bytes 1769480 | tf_op jit(solution)/shard_map/ppermute | solution.py:54
  540.3 68.6 %collective-permute-start.53 = (f32[128,1536]{1,0:T(8,128)}, f32[128,1536]{1,0:T(8,128)}, u32[]{:S(2)}, u32[]{:S(2)}) collective-permute-start(f32[128,1536]{1,0:T(8,128)} %get-tuple-element.64), channel_id=1, source_target_pairs={{0,1},{1,0},{2,3},{3,2},{4,5},{5,4},{6,7},{7,6},{8,9},{9,8},{10,11... | collective-permute-start | bytes 2359304 | tf_op jit(solution)/shard_map/ppermute | solution.py:54
  541.6 54.9 %collective-permute-start.54 = (f32[1536,128]{1,0:T(8,128)S(1)}, f32[1536,128]{1,0:T(8,128)S(1)}, u32[]{:S(2)}, u32[]{:S(2)}) collective-permute-start(f32[1536,128]{1,0:T(8,128)S(1)} %add.304), channel_id=1, source_target_pairs={{0,1},{1,0},{2,3},{3,2},{4,5},{5,4},{6,7},{7,6},{8,9},{9,8},{10,11... | collective-permute-start | bytes 2359304 | tf_op jit(solution)/shard_map/ppermute | solution.py:54
  543.8 13.3 %collective-permute-start.69 = (bf16[96,768]{1,0:T(8,128)(2,1)S(1)}, bf16[96,768]{1,0:T(8,128)(2,1)S(1)}, u32[]{:S(2)}, u32[]{:S(2)}) collective-permute-start(bf16[96,768]{1,0:T(8,128)(2,1)S(1)} %get-tuple-element.176), channel_id=1, source_target_pairs={{0,6},{2,4},{4,2},{6,0},{1,7},{3,5},{5,3},{7,1},{8,14},{10,12},{12... | collective-permute-start | bytes 442376 | tf_op jit(solution)/shard_map/ppermute | solution.py:54
  546.0 15.2 %collective-permute-start.68 = (bf16[96,768]{1,0:T(8,128)(2,1)S(1)}, bf16[96,768]{1,0:T(8,128)(2,1)S(1)}, u32[]{:S(2)}, u32[]{:S(2)}) collective-permute-start(bf16[96,768]{1,0:T(8,128)(2,1)S(1)} %get-tuple-element.177), channel_id=1, source_target_pairs={{0,4},{2,6},{4,0},{6,2},{1,5},{3,7},{5,1},{7,3},{8,12},{10,14},{12... | collective-permute-start | bytes 442376 | tf_op jit(solution)/shard_map/ppermute | solution.py:54
  547.3 17.3 %collective-permute-start.67 = (bf16[96,768]{1,0:T(8,128)(2,1)S(1)}, bf16[96,768]{1,0:T(8,128)(2,1)S(1)}, u32[]{:S(2)}, u32[]{:S(2)}) collective-permute-start(bf16[96,768]{1,0:T(8,128)(2,1)S(1)} %get-tuple-element.175), channel_id=1, source_target_pairs={{0,2},{2,0},{4,6},{6,4},{1,3},{3,1},{5,7},{7,5},{8,10},{10,8},{12,... | collective-permute-start | bytes 442376 | tf_op jit(solution)/shard_map/ppermute | solution.py:54
  (91 other events, 1022.3 us)
Sparse Core Ops, SparseCore 0:
  364.0 145.4 all-gather.1

commit v2 on v1

v2 whole, which is shorter than its diff:
```python
import jax
import jax.numpy as jnp
from jax import lax
from jax.experimental import pallas as pl
from jax.experimental.pallas import tpu as pltpu
from jax.sharding import PartitionSpec as P

HEAD = 128
LANES = 128
EPSILON = 1e-06
ROPE_BASE = 1000000.0
NEG_FILL = -1e30
KEY_STEP = 256
MOE_ROWS = 512
SLICES = 2
VMEM_BYTES = 60 * 2**20

f32 = jnp.float32
bf16 = jnp.bfloat16
EXACT = lax.Precision.HIGHEST
NN = (((1,), (0,)), ((), ()))
NT = (((1,), (1,)), ((), ()))
TN = (((0,), (0,)), ((), ()))


def mm(left, right, dims=NN, precision=None):
    return lax.dot_general(left, right, dims, precision=precision, preferred_element_type=f32)


def vmem(count):
    return [pl.BlockSpec(memory_space=pltpu.VMEM)] * count


def anywhere(count):
    return [pl.BlockSpec(memory_space=pl.ANY)] * count


def scalars():
    return [pl.BlockSpec(memory_space=pltpu.SMEM)]


def shape(dims, kind):
    return jax.ShapeDtypeStruct(dims, kind)


def cost(flops, moved):
    return pl.CostEstimate(flops=int(flops), bytes_accessed=int(moved), transcendentals=0)


def params():
    return pltpu.CompilerParams(vmem_limit_bytes=VMEM_BYTES)


def swap(value, axis, size, bit):
    return lax.ppermute(value, axis, [(i, i ^ bit) for i in range(size)])


def low_bit(number):
    return number & -number


def high_bit(number):
    return 1 << (number.bit_length() - 1)


def after(value, *earlier):
    return lax.optimization_barrier((value, *earlier))[0]


def gather_first(own, axis, size):
    return [
        own if j == 0 else swap(own, axis, size, j) if low_bit(j) == high_bit(j) else None
        for j in range(size)
    ]


def gather_rest(got, axis, size, dim=0, ties=()):
    rows, got = got[0].shape[dim], list(got)

    def half(j, top):
        if isinstance(got[j], tuple):
            return got[j][0 if top else 1]
        begin = 0 if top else rows // 2
        return after(lax.slice_in_dim(got[j], begin, begin + rows // 2, axis=dim), *ties)

    for j in range(1, size):
        low, high = low_bit(j), high_bit(j)
        if low != high:
            got[j] = (
                swap(half(j ^ high, True), axis, size, high),
                swap(half(j ^ low, False), axis, size, low),
            )
    return [
        (piece, j * rows + row)
        for j, block in enumerate(got)
        for piece, row in (
            ((block[0], 0), (block[1], rows // 2)) if isinstance(block, tuple) else ((block, 0),)
        )
    ]


def held_pieces(pieces, others):
    arrays, others = lax.optimization_barrier(([array for array, _ in pieces], others))
    return [(array, row) for array, (_, row) in zip(arrays, pieces)], others


def add_low(left, right):
    return (left.astype(f32) + right.astype(f32)).astype(bf16)


def scatter_order(size, high):
    bits = size.bit_length() - 1
    if high:
        return list(range(size))
    return [sum(((n >> k) & 1) << (bits - 1 - k) for k in range(bits)) for n in range(size)]


def scatter_bits(size, high):
    bits = [1 << k for k in range(size.bit_length() - 1)]
    return bits[::-1] if high else bits


def scatter_first(send, axis, size, high):
    return swap(send, axis, size, scatter_bits(size, high)[0])


def scatter_rest(keep, got, axis, size, high):
    for bit in scatter_bits(size, high)[1:]:
        count = keep.shape[0] // 2
        send = add_low(keep[count:], got[count:])
        keep, got = add_low(keep[:count], got[:count]), swap(send, axis, size, bit)
    return add_low(keep[0], got[0])


def exchange_direct(blocks, axis, size):
    return [blocks[0]] + [swap(blocks[j], axis, size, j) for j in range(1, size)]


def ordered(blocks, index):
    count = len(blocks)
    bit = 1
    while bit < count:
        flag = (index & bit) != 0
        blocks = [jnp.where(flag, blocks[i ^ bit], blocks[i]) for i in range(count)]
        bit *= 2
    return blocks


def axis_relative(value, dim, index):
    count, bit, dims = value.shape[dim], 1, value.shape
    while bit < count:
        split = value.reshape(*dims[:dim], count // (2 * bit), 2, bit, *dims[dim + 1 :])
        value = jnp.where((index & bit) != 0, jnp.flip(split, dim + 1), split).reshape(dims)
        bit *= 2
    return value


def lanes_relative(value, index, count):
    width = value.shape[-1] // count
    return jnp.concatenate(
        [
            lax.dynamic_slice_in_dim(value, (index ^ j) * width, width, value.ndim - 1)
            for j in range(count)
        ],
        -1,
    )


def rotated(values, cosine, sine):
    return values * cosine + pltpu.roll(values, HEAD // 2, 1) * sine


def norm_scale(values):
    return lax.rsqrt(jnp.mean(values * values, -1, keepdims=True) + EPSILON)


def fetch(sources, targets, sems):
    copies = [
        pltpu.make_async_copy(source, target, sems.at[number])
        for number, (source, target) in enumerate(zip(sources, targets))
    ]
    for copy in copies:
        copy.start()
    return copies


def project_in(x, cosine, sine, pieces, micro, rows, experts):
    total, width = x.shape
    parts = len(pieces)
    columns = pieces[0][0].shape[1] - LANES
    heads = (columns - 2 * HEAD) // HEAD

    def body(x_ref, cos_ref, sin_ref, *rest):
        w_refs, (a_ref, q_ref, kv_ref, all_ref, small_ref, gains_ref, sems) = rest[:parts], rest[parts:]
        copies = fetch(
            w_refs,
            [all_ref.at[pl.ds(row, array.shape[0]), :] for array, row in pieces],
            sems,
        )
        values = x_ref[...].astype(f32)
        normal = values * norm_scale(values)
        for copy in copies:
            copy.wait()
        small = all_ref[:, columns:]
        small_ref[...] = small
        gains = small.astype(f32).T[experts : experts + 8, :]
        gains_ref[...] = gains
        a_ref[...] = (normal * gains[0:1, :]).astype(bf16)
        for m in range(micro):
            span = slice(m * rows, (m + 1) * rows)
            mixed = mm(a_ref[span, :], all_ref[:, :columns])
            cosine_m, sine_m = cos_ref[span, :], sin_ref[span, :]
            for h in range(heads):
                q_ref[m, h * rows : (h + 1) * rows, :] = rotated(
                    mixed[:, h * HEAD : (h + 1) * HEAD], cosine_m, sine_m
                ).astype(bf16)
            kv_ref[m, :, :HEAD] = rotated(
                mixed[:, heads * HEAD : (heads + 1) * HEAD], cosine_m, sine_m
            ).astype(bf16)
            kv_ref[m, :, HEAD:] = mixed[:, (heads + 1) * HEAD :].astype(bf16)

    return pl.pallas_call(
        body,
        name="project_in",
        out_shape=(
            shape((total, width), bf16),
            shape((micro, heads * rows, HEAD), bf16),
            shape((micro, rows, 2 * HEAD), bf16),
            shape((width, columns + LANES), bf16),
            shape((width, LANES), bf16),
            shape((8, width), f32),
        ),
        in_specs=vmem(3) + anywhere(parts),
        out_specs=tuple(vmem(6)),
        scratch_shapes=[pltpu.SemaphoreType.DMA((parts,))],
        compiler_params=params(),
        cost_estimate=cost(2 * total * width * columns, 4 * width * columns),
    )(x, cosine, sine, *[array for array, _ in pieces])


def attend(seen, q, mask, kv, weights):
    micro, stacked, _ = q.shape
    keys, rows = mask.shape[1], mask.shape[2]
    heads = stacked // rows
    blocks, parts = len(kv), len(weights)
    width = sum(array.shape[0] for array, _ in weights)
    steps = keys // KEY_STEP
    scale = HEAD ** (-0.5)

    def body(seen_ref, q_ref, mask_ref, *rest):
        kv_refs, w_refs = rest[:blocks], rest[blocks : blocks + parts]
        branch_ref, o_ref, lse_ref, wo_ref, kv_all, top, total, acc, kv_sems, w_sems = rest[
            blocks + parts :
        ]
        kv_copies = fetch(
            kv_refs, [kv_all.at[:, pl.ds(row, array.shape[1]), :] for array, row in kv], kv_sems
        )
        w_copies = fetch(
            w_refs, [wo_ref.at[pl.ds(row, array.shape[0]), :] for array, row in weights], w_sems
        )
        for copy in kv_copies:
            copy.wait()
        for m in range(micro):
            top[...] = jnp.full_like(top, NEG_FILL)
            total[...] = jnp.zeros_like(total)
            acc[...] = jnp.zeros_like(acc)
            queries = q_ref[m]

            def step(n, carry, m=m, queries=queries):
                @pl.when(seen_ref[m * steps + n] > 0)
                def _():
                    start = pl.multiple_of(n * KEY_STEP, KEY_STEP)
                    keys_n = kv_all[m, pl.ds(start, KEY_STEP), :HEAD]
                    values_n = kv_all[m, pl.ds(start, KEY_STEP), HEAD:]
                    bias = mask_ref[m, pl.ds(start, KEY_STEP), :].astype(f32)
                    scores = mm(keys_n, queries, NT) * scale + jnp.concatenate([bias] * heads, 1)
                    peak = jnp.maximum(top[...], jnp.max(scores, 0, keepdims=True))
                    rescale = jnp.exp(top[...] - peak)
                    weights_n = jnp.exp(scores - peak)
                    total[...] = total[...] * rescale + jnp.sum(weights_n, 0, keepdims=True)
                    acc[...] = acc[...] * rescale + mm(values_n, weights_n.astype(bf16), TN)
                    top[...] = peak

                return carry

            lax.fori_loop(0, steps, step, 0)
            lse_ref[m] = top[...] + jnp.log(total[...])
            mixed = acc[...] / total[...]
            for h in range(heads):
                o_ref[m, :, h * HEAD : (h + 1) * HEAD] = mixed[
                    :, h * rows : (h + 1) * rows
                ].T.astype(bf16)
        for copy in w_copies:
            copy.wait()
        for m in range(micro):
            branch_ref[m] = mm(o_ref[m], wo_ref[...], NT).astype(bf16)

    return pl.pallas_call(
        body,
        name="attend",
        out_shape=(
            shape((micro, rows, width), bf16),
            shape((micro, rows, heads * HEAD), bf16),
            shape((micro, 1, stacked), f32),
            shape((width, heads * HEAD), bf16),
        ),
        in_specs=scalars() + vmem(2) + anywhere(blocks + parts),
        out_specs=tuple(vmem(4)),
        scratch_shapes=[
            pltpu.VMEM((micro, keys, 2 * HEAD), bf16),
            pltpu.VMEM((1, stacked), f32),
            pltpu.VMEM((1, stacked), f32),
            pltpu.VMEM((HEAD, stacked), f32),
            pltpu.SemaphoreType.DMA((blocks,)),
            pltpu.SemaphoreType.DMA((parts,)),
        ],
        compiler_params=params(),
        cost_estimate=cost(
            2 * micro * stacked * keys * HEAD * 2 + 2 * micro * rows * width * heads * HEAD,
            2 * micro * keys * 2 * HEAD + 2 * width * heads * HEAD * 2,
        ),
    )(seen, q, mask, *[array for array, _ in kv], *[array for array, _ in weights])


def second_norm(place, x, branch, other, gain):
    rows, width = other.shape

    def body(place_ref, x_ref, branch_ref, other_ref, gain_ref, middle_ref, b_ref):
        t = place_ref[2]
        middle = (
            x_ref[t].astype(f32) + branch_ref[t].astype(f32) + other_ref[...].astype(f32)
        )
        middle_ref[...] = middle
        b_ref[...] = (middle * norm_scale(middle) * gain_ref[1:2, :]).astype(bf16)

    return pl.pallas_call(
        body,
        name="second_norm",
        out_shape=(shape((rows, width), f32), shape((rows, width), bf16)),
        in_specs=scalars() + vmem(4),
        out_specs=tuple(vmem(2)),
        compiler_params=params(),
        cost_estimate=cost(10 * rows * width, 20 * rows * width),
    )(place, x, branch, other, gain)


def routing(b, router, experts):
    logits = mm(b, router)
    lane = lax.broadcasted_iota(jnp.int32, logits.shape, 1)
    logits = jnp.where(lane < experts, logits, NEG_FILL)
    powers = jnp.exp(logits - jnp.max(logits, -1, keepdims=True))
    return powers / jnp.sum(powers, -1, keepdims=True), lane


def experts_rows(place, b, at, block, cx, router, weights, experts):
    pieces, width = len(at), b[0].shape[1]
    total = pieces * block
    rows = min(MOE_ROWS, total)
    local, _, _, hidden = weights[0][0].shape
    wide = local * hidden
    w_count = len(weights)
    half_rows = total // 2
    k0 = 0.7978845608028654
    k1 = 0.044715

    def body(place_ref, router_ref, *rest):
        b_refs, cx_refs = rest[: len(b)], rest[len(b) : 2 * len(b)]
        w_refs, rest = rest[2 * len(b) : 2 * len(b) + w_count], rest[2 * len(b) + w_count :]
        out_refs, back_refs, (scaled_ref, gate_ref, up_ref) = rest[:2], rest[2:4], rest[4:7]
        b_all, cx_all, w_all, b_sems, cx_sems, w_sems = rest[7:]
        row_copies = fetch(
            [b_refs[n % len(b)].at[pl.ds(row, block), :] for n, row in enumerate(at)],
            [b_all.at[pl.ds(n * block, block), :] for n in range(pieces)],
            b_sems,
        )
        w_copies = fetch(
            [ref.at[e] for ref in w_refs for e in range(local)],
            [
                w_all.at[:, pl.ds(row, array.shape[2]), pl.ds(e * hidden, hidden)]
                for array, row in weights
                for e in range(local)
            ],
            w_sems,
        )
        row_copies += fetch(
            [cx_refs[n % len(b)].at[pl.ds(row, block), :] for n, row in enumerate(at)],
            [cx_all.at[pl.ds(n * block, block), :] for n in range(pieces)],
            cx_sems,
        )
        for copy in row_copies:
            copy.wait()
        lane = lax.broadcasted_iota(jnp.int32, (rows, LANES), 1)
        for start in range(0, total, rows):
            span = slice(start, start + rows)
            probs, _ = routing(b_all[span, :], router_ref[...], experts)
            gates = probs * cx_all[span, width:].astype(f32)
            mine = [lane == place_ref[1] * local + e for e in range(local)]
            gate = jnp.concatenate(
                [
                    jnp.broadcast_to(
                        jnp.sum(jnp.where(mine[e], gates, 0.0), -1, keepdims=True), (rows, hidden)
                    )
                    for e in range(local)
                ],
                1,
            )
            if start == 0:
                for copy in w_copies:
                    copy.wait()
            b_rows = b_all[span, :]
            z = mm(b_rows, w_all[0])
            up = mm(b_rows, w_all[1])
            down_back = mm(cx_all[span, :width], w_all[2])
            square = z * z
            bend = jnp.tanh(k0 * z * (1.0 + k1 * square))
            half = 0.5 * (1.0 + bend)
            active = z * half
            slope = half + 0.5 * z * (1.0 - bend * bend) * (k0 * (1.0 + 3.0 * k1 * square))
            hidden_rows = active * up
            hidden_back = gate * down_back
            scaled_ref[span, :] = (gate * hidden_rows).astype(bf16)
            gate_ref[span, :] = (hidden_back * up * slope).astype(bf16)
            up_ref[span, :] = (hidden_back * active).astype(bf16)
            product = hidden_rows * down_back
            share = jnp.zeros((rows, LANES), f32)
            for e in range(local):
                share += jnp.where(
                    mine[e],
                    jnp.sum(product[:, e * hidden : (e + 1) * hidden], -1, keepdims=True),
                    0.0,
                )
            out = mm(scaled_ref[span, :], w_all[2], NT).astype(bf16)
            back = (
                mm(gate_ref[span, :], w_all[0], NT) + mm(up_ref[span, :], w_all[1], NT)
            ).astype(bf16)
            share = share.astype(bf16)
            for n in range(2):
                low, high = max(start, n * half_rows), min(start + rows, (n + 1) * half_rows)
                if low < high:
                    to = slice(low - n * half_rows, high - n * half_rows)
                    out_refs[n][to, :] = out[low - start : high - start]
                    back_refs[n][to, :width] = back[low - start : high - start]
                    back_refs[n][to, width:] = share[low - start : high - start]

    return pl.pallas_call(
        body,
        name="experts_rows",
        out_shape=(
            *[shape((half_rows, width), bf16)] * 2,
            *[shape((half_rows, width + LANES), bf16)] * 2,
            *[shape((total, wide), bf16)] * 3,
        ),
        in_specs=scalars() + vmem(1) + anywhere(2 * len(b) + w_count),
        out_specs=tuple(vmem(7)),
        scratch_shapes=[
            pltpu.VMEM((total, width), bf16),
            pltpu.VMEM((total, width + LANES), bf16),
            pltpu.VMEM((3, width, wide), bf16),
            pltpu.SemaphoreType.DMA((pieces,)),
            pltpu.SemaphoreType.DMA((pieces,)),
            pltpu.SemaphoreType.DMA((local * w_count,)),
        ],
        compiler_params=params(),
        cost_estimate=cost(12 * total * width * wide, 2 * (4 * total * width + 3 * width * wide)),
    )(place, router, *b, *cx, *[array for array, _ in weights])


def experts_grads(b, cx, at, block, sides, local, parts):
    pieces, width = len(at), b[0].shape[1]
    total = pieces * block
    calls = len(sides)
    each = total // calls
    wide = sides[0][0].shape[1]
    hidden, depth, half = wide // local, width // parts, parts // 2
    fine = depth // 2
    orders = [scatter_order(parts, n == 0) for n in range(2)]

    def body(*refs):
        b_refs, cx_refs, side_refs = refs[: len(b)], refs[len(b) : 2 * len(b)], refs[2 * len(b) :]
        side_refs, rest = side_refs[: 3 * calls], side_refs[3 * calls :]
        grad_refs = rest[:4]
        b_all, c_all, side_all, turned, stage, b_sems, c_sems, s_sems, g_sems = rest[4:]
        b_copies = fetch(
            [b_refs[n % len(b)].at[pl.ds(row, block), :] for n, row in enumerate(at)],
            [b_all.at[pl.ds(n * block, block), :] for n in range(pieces)],
            b_sems,
        )
        s_copies = fetch(
            side_refs,
            [
                side_all.at[n, pl.ds(call * each, each), :]
                for call in range(calls)
                for n in range(3)
            ],
            s_sems,
        )
        c_copies = fetch(
            [
                cx_refs[n % len(b)].at[pl.ds(row, block), pl.ds(0, width)]
                for n, row in enumerate(at)
            ],
            [c_all.at[pl.ds(n * block, block), :] for n in range(pieces)],
            c_sems,
        )
        for copy in b_copies + s_copies:
            copy.wait()
        g_copies = []
        for n, side in ((0, 1), (1, 2), (2, 0)):
            if n == 0:
                turned[...] = b_all[...].T
            if n == 2:
                for copy in c_copies:
                    copy.wait()
                turned[...] = c_all[...].T
            for j in range(parts):
                span = slice(j * depth, (j + 1) * depth)
                stage[n, span, :] = mm(turned[span, :], side_all[side]).astype(bf16)
                for e in range(local):
                    for way in range(2):
                        to = orders[way].index(j)
                        copy = pltpu.make_async_copy(
                            stage.at[
                                n, pl.ds(j * depth + way * fine, fine), pl.ds(e * hidden, hidden)
                            ],
                            grad_refs[2 * way + to // half].at[to % half, e, n],
                            g_sems.at[len(g_copies)],
                        )
                        copy.start()
                        g_copies.append(copy)
        for copy in g_copies:
            copy.wait()

    return pl.pallas_call(
        body,
        name="experts_grads",
        out_shape=tuple([shape((half, local, 3, fine, hidden), bf16)] * 4),
        in_specs=anywhere(2 * len(b) + 3 * calls),
        out_specs=tuple(anywhere(4)),
        scratch_shapes=[
            pltpu.VMEM((total, width), bf16),
            pltpu.VMEM((total, width), bf16),
            pltpu.VMEM((3, total, wide), bf16),
            pltpu.VMEM((width, total), bf16),
            pltpu.VMEM((3, width, wide), bf16),
            pltpu.SemaphoreType.DMA((pieces,)),
            pltpu.SemaphoreType.DMA((pieces,)),
            pltpu.SemaphoreType.DMA((3 * calls,)),
            pltpu.SemaphoreType.DMA((3 * parts * local * 2,)),
        ],
        compiler_params=params(),
        cost_estimate=cost(
            6 * total * width * wide, 2 * (2 * total * width + 3 * total * wide + 3 * width * wide)
        ),
    )(*b, *cx, *[array for side in sides for array in side])


def second_norm_back(sums, middle, b, cx, gain, router, experts):
    rows, width = middle.shape
    slices, count = len(sums), len(sums[0])
    part = rows // slices

    def body(*refs):
        sum_refs, refs = refs[: slices * count], refs[slices * count :]
        middle_ref, b_ref, cx_ref, gain_ref, router_ref, dmiddle_ref, go_ref, dl_ref, dgain_ref = refs
        weights = router_ref[...]
        for n in range(slices):
            span = slice(n * part, (n + 1) * part)
            total = sum_refs[n * count][...].astype(f32)
            for ref in sum_refs[n * count + 1 : (n + 1) * count]:
                total += ref[...].astype(f32)
            b_rows = b_ref[span, :]
            share = total[:, width:] * cx_ref[span, width:].astype(f32)
            probs, _ = routing(b_rows, weights, experts)
            dl = probs * (share - jnp.sum(probs * share, -1, keepdims=True))
            dl_high = dl.astype(bf16)
            dl_low = (dl - dl_high.astype(f32)).astype(bf16)
            db = total[:, :width] + mm(dl_high, weights, NT) + mm(dl_low, weights, NT)
            values = middle_ref[span, :]
            scale = norm_scale(values)
            normal = values * scale
            dn = db * gain_ref[1:2, :]
            dmiddle = cx_ref[span, :width].astype(f32) + scale * (
                dn - normal * jnp.mean(dn * normal, -1, keepdims=True)
            )
            dmiddle_ref[span, :] = dmiddle
            go_ref[span, :] = dmiddle.astype(bf16)
            dl_ref[span, :] = dl_high
            dgain_ref[span, :] = (db * normal).astype(bf16)

    return pl.pallas_call(
        body,
        name="second_norm_back",
        out_shape=(
            shape((rows, width), f32),
            shape((rows, width), bf16),
            shape((rows, LANES), bf16),
            shape((rows, width), bf16),
        ),
        in_specs=vmem(slices * count + 5),
        out_specs=tuple(vmem(4)),
        compiler_params=params(),
        cost_estimate=cost(2 * 20 * rows * width * LANES, 24 * rows * width),
    )(*[part for one in sums for part in one], middle, b, cx, gain, router)


def attend_back(place, seen, go_own, go_other, q, o, lse, mask, cosine, sine, wo, kv, groups):
    micro, stacked, _ = q.shape
    keys, rows = mask.shape[1], mask.shape[2]
    heads = stacked // rows
    blocks = len(kv)
    per_group = keys // groups
    width = wo.shape[0]
    steps = keys // KEY_STEP
    scale = HEAD ** (-0.5)

    def body(place_ref, seen_ref, own_ref, other_ref, q_ref, o_ref, lse_ref, mask_ref, cos_ref, sin_ref, wo_ref, *rest):
        kv_refs = rest[:blocks]
        go_ref, dq_ref = rest[blocks : blocks + 2]
        dkv_refs = rest[blocks + 2 : blocks + groups + 2]
        kv_all, dkv_all, acc, do_all, kv_sems, d_sems = rest[blocks + groups + 2 :]
        kv_copies = fetch(
            kv_refs, [kv_all.at[:, pl.ds(row, array.shape[1]), :] for array, row in kv], kv_sems
        )
        t = place_ref[2]
        go_ref[t] = own_ref[...]
        go_ref[1 - t] = other_ref[...]
        for copy in kv_copies:
            copy.wait()
        for m in range(micro):
            do = mm(go_ref[m], wo_ref[...]).astype(bf16)
            pieces = []
            for h in range(heads):
                do_h = do[:, h * HEAD : (h + 1) * HEAD]
                do_all[h * rows : (h + 1) * rows, :] = do_h
                product = do_h.astype(f32) * o_ref[m, :, h * HEAD : (h + 1) * HEAD].astype(f32)
                pieces.append(jnp.sum(product.T, 0, keepdims=True))
            delta = jnp.concatenate(pieces, 1)
            acc[...] = jnp.zeros_like(acc)
            queries, outs, total = q_ref[m], do_all[...], lse_ref[m]

            def step(n, carry, m=m, queries=queries, outs=outs, total=total, delta=delta):
                start = pl.multiple_of(n * KEY_STEP, KEY_STEP)
                span = pl.ds(start, KEY_STEP)

                @pl.when(seen_ref[m * steps + n] > 0)
                def _():
                    keys_n = kv_all[m, span, :HEAD]
                    values_n = kv_all[m, span, HEAD:]
                    bias = mask_ref[m, span, :].astype(f32)
                    scores = mm(keys_n, queries, NT) * scale + jnp.concatenate([bias] * heads, 1)
                    probs = jnp.exp(scores - total)
                    ds = (probs * (mm(values_n, outs, NT) - delta)).astype(bf16)
                    acc[...] += mm(keys_n, ds, TN)
                    dkv_all[m, span, :HEAD] = (mm(ds, queries) * scale).astype(bf16)
                    dkv_all[m, span, HEAD:] = mm(probs.astype(bf16), outs).astype(bf16)

                @pl.when(seen_ref[m * steps + n] == 0)
                def _():
                    dkv_all[m, span, :] = jnp.zeros((KEY_STEP, 2 * HEAD), bf16)

                return carry

            lax.fori_loop(0, steps, step, 0)
            for h in range(heads):
                back = acc[:, h * rows : (h + 1) * rows].T * scale
                part = slice(m * rows, (m + 1) * rows)
                dq_ref[part, h * HEAD : (h + 1) * HEAD] = rotated(
                    back, cos_ref[part, :], -sin_ref[part, :]
                ).astype(bf16)
        d_copies = fetch(
            [dkv_all.at[:, pl.ds(j * per_group, per_group), :] for j in range(groups)], dkv_refs, d_sems
        )
        for copy in d_copies:
            copy.wait()

    return pl.pallas_call(
        body,
        name="attend_back",
        out_shape=(
            shape((micro, rows, width), bf16),
            shape((micro * rows, heads * HEAD), bf16),
            *[shape((micro, per_group, 2 * HEAD), bf16)] * groups,
        ),
        in_specs=scalars() * 2 + vmem(9) + anywhere(blocks),
        out_specs=(*vmem(2), *anywhere(groups)),
        scratch_shapes=[
            pltpu.VMEM((micro, keys, 2 * HEAD), bf16),
            pltpu.VMEM((micro, keys, 2 * HEAD), bf16),
            pltpu.VMEM((HEAD, stacked), f32),
            pltpu.VMEM((stacked, HEAD), bf16),
            pltpu.SemaphoreType.DMA((blocks,)),
            pltpu.SemaphoreType.DMA((groups,)),
        ],
        compiler_params=params(),
        cost_estimate=cost(
            2 * micro * stacked * keys * HEAD * 5,
            2 * micro * keys * 4 * HEAD + 2 * width * heads * HEAD,
        ),
    )(place, seen, go_own, go_other, q, o, lse, mask, cosine, sine, wo, *[array for array, _ in kv])


def project_back(dkv, dq, cosine, sine, w):
    count = len(dkv)
    micro, rows, _ = dkv[0].shape
    width, columns = w.shape
    columns -= LANES
    wide = columns - 2 * HEAD

    def body(*refs):
        dq_ref, cos_ref, sin_ref, w_ref, dkv_ref, da_ref = refs[count:]
        for m in range(micro):
            part = slice(m * rows, (m + 1) * rows)
            total = refs[0][m].astype(f32)
            for ref in refs[1:count]:
                total += ref[m].astype(f32)
            dkv_ref[part, :HEAD] = rotated(
                total[:, :HEAD], cos_ref[part, :], -sin_ref[part, :]
            ).astype(bf16)
            dkv_ref[part, HEAD:] = total[:, HEAD:].astype(bf16)
            da_ref[m] = (
                mm(dq_ref[part, :], w_ref[:, :wide], NT) + mm(dkv_ref[part, :], w_ref[:, wide:columns], NT)
            ).astype(bf16)

    return pl.pallas_call(
        body,
        name="project_back",
        out_shape=(shape((micro * rows, 2 * HEAD), bf16), shape((micro, rows, width), bf16)),
        in_specs=vmem(count + 4),
        out_specs=tuple(vmem(2)),
        compiler_params=params(),
        cost_estimate=cost(2 * micro * rows * width * columns, 2 * width * columns),
    )(*dkv, dq, cosine, sine, w)


def first_norm_back(place, da, other, x, gain, dmiddle):
    rows, width = dmiddle.shape

    def body(place_ref, da_ref, other_ref, x_ref, gain_ref, dmiddle_ref, ig_ref, dgain_ref):
        t = place_ref[2]
        total = da_ref[t].astype(f32) + other_ref[...].astype(f32)
        values = x_ref[t].astype(f32)
        scale = norm_scale(values)
        normal = values * scale
        dn = total * gain_ref[0:1, :]
        ig_ref[...] = dmiddle_ref[...] + scale * (
            dn - normal * jnp.mean(dn * normal, -1, keepdims=True)
        )
        dgain_ref[...] = (total * normal).astype(bf16)

    return pl.pallas_call(
        body,
        name="first_norm_back",
        out_shape=(shape((rows, width), f32), shape((rows, width), bf16)),
        in_specs=scalars() + vmem(5),
        out_specs=tuple(vmem(2)),
        compiler_params=params(),
        cost_estimate=cost(2 * 6 * rows * width * LANES, 20 * rows * width),
    )(place, da, other, x, gain, dmiddle)


def assemble(gathered):
    count, _, local, _, fine, hidden = gathered.shape
    depth = 2 * fine

    def body(in_ref, gate_ref, up_ref, down_ref):
        for way in range(2):
            span = slice(way * fine, (way + 1) * fine)
            gate_ref[0, span, :] = in_ref[0, way, 0, 0].astype(f32)
            up_ref[0, span, :] = in_ref[0, way, 0, 1].astype(f32)
            down_ref[0, :, span] = in_ref[0, way, 0, 2].astype(f32).T

    at = lambda j, e: (j * local + e, 0, 0)
    return pl.pallas_call(
        body,
        name="assemble",
        grid=(count, local),
        in_specs=[
            pl.BlockSpec((1, 2, 1, 3, fine, hidden), lambda j, e: (j, 0, e, 0, 0, 0))
        ],
        out_specs=(
            pl.BlockSpec((1, depth, hidden), at),
            pl.BlockSpec((1, depth, hidden), at),
            pl.BlockSpec((1, hidden, depth), at),
        ),
        out_shape=(
            *[shape((count * local, depth, hidden), f32)] * 2,
            shape((count * local, hidden, depth), f32),
        ),
        compiler_params=params(),
        cost_estimate=cost(count * local * depth * hidden * 3, count * local * depth * hidden * 18),
    )(gathered)


def attention_grads(a, go, dq, dkv, o, b, dl, dgain_one, dgain_two, experts, parts):
    rows, width = a.shape
    depth = width // parts
    half = parts // 2
    lanes = (dq.shape[1] + dkv.shape[1], o.shape[1] + LANES)

    def body(a_ref, go_ref, dq_ref, dkv_ref, o_ref, b_ref, dl_ref, one_ref, two_ref, *out_refs):
        def put(n, lane, total):
            for to, j in enumerate(scatter_order(parts, n == 0)):
                out_refs[2 * n + to // half][to % half, :, lane : lane + total.shape[1]] = total[
                    j * depth : (j + 1) * depth
                ].astype(bf16)

        turned = a_ref[...].T
        put(0, 0, mm(turned, dq_ref[...]))
        put(0, dq_ref.shape[1], mm(turned, dkv_ref[...]))
        put(1, 0, mm(go_ref[...].T, o_ref[...]))
        lane = lax.broadcasted_iota(jnp.int32, dl_ref.shape, 1)
        put(
            1,
            o_ref.shape[1],
            mm(b_ref[...].T, dl_ref[...])
            + mm(one_ref[...].T, (lane == experts).astype(bf16))
            + mm(two_ref[...].T, (lane == experts + 1).astype(bf16)),
        )

    return pl.pallas_call(
        body,
        name="attention_grads",
        out_shape=tuple(shape((half, depth, lanes[n // 2]), bf16) for n in range(4)),
        in_specs=vmem(9),
        out_specs=tuple(vmem(4)),
        compiler_params=params(),
        cost_estimate=cost(2 * rows * width * sum(lanes), 2 * width * sum(lanes)),
    )(a, go, dq, dkv, o, b, dl, dgain_one, dgain_two)


def solution(mesh):
    F, C, T = mesh.shape["fsdp"], mesh.shape["ctx"], mesh.shape["tp"]

    def local(
        tokens,
        gain_attn,
        w_query,
        w_key,
        w_value,
        w_output,
        gain_mlp,
        w_router,
        w_gate,
        w_up,
        w_down,
        lineage,
        expert_ids,
        cotangent,
    ):
        micro, rows, width = tokens.shape
        depth = width // F
        experts = w_router.shape[1]
        local_experts = experts // C
        slots = lineage.shape[2]
        f, c, t = lax.axis_index("fsdp"), lax.axis_index("ctx"), lax.axis_index("tp")
        place = jnp.stack([f, c, t]).astype(jnp.int32)

        def pick(pair, index):
            return jnp.where(index == 0, pair[0], pair[1])

        def core(value):
            return swap(value, "tp", T, 1)

        small = jnp.concatenate(
            [
                w_router,
                gain_attn[:, None],
                gain_mlp[:, None],
                jnp.zeros((depth, LANES - experts - 2), bf16),
            ],
            1,
        )
        in_own = jnp.concatenate([w_query, w_key, w_value, small], 1)

        def experts_of(index):
            mine = [
                lax.dynamic_slice_in_dim(w, index * local_experts, local_experts, 0)
                for w in (w_gate, w_up, w_down)
            ]
            return jnp.stack([mine[0], mine[1], jnp.swapaxes(mine[2], 1, 2)], 1)

        expert_own = experts_of(c)

        x = lanes_relative(tokens, f, F)
        c_mine = lanes_relative(pick(cotangent, t), f, F)
        ids_mine = pick(expert_ids, t)
        chosen = jnp.sum(
            (ids_mine[:, :, None] == jnp.arange(LANES, dtype=jnp.int32)[None, None, :]).astype(f32), 1
        ).astype(bf16)
        cx_mine = jnp.concatenate([c_mine, chosen], 1)

        f_order = f ^ jnp.arange(F, dtype=jnp.int32)
        c_order = c ^ jnp.arange(C, dtype=jnp.int32)
        block_order = (f_order[:, None] * C + c_order[None, :]).reshape(-1)
        key_index = (block_order[:, None] * rows + jnp.arange(rows, dtype=jnp.int32)).reshape(-1)
        key_owner = lineage[:, 0].reshape(micro, F, C, rows)
        key_owner = axis_relative(axis_relative(key_owner, 1, f), 2, c).reshape(micro, slots)
        first_row = (f * C + c) * rows
        query_lin = lax.dynamic_slice_in_dim(lineage, first_row, rows, 2)
        query_index = first_row + jnp.arange(rows, dtype=jnp.int32)
        owner = key_owner[:, :, None]
        visible = (
            ((owner == query_lin[:, 0, None, :]) & (key_index[None, :, None] <= query_index))
            | (owner == query_lin[:, 1, None, :])
            | (owner == query_lin[:, 2, None, :])
        )
        mask = jnp.where(visible, 0.0, NEG_FILL).astype(bf16)
        counts = jnp.sum(visible.astype(f32).reshape(micro, slots // KEY_STEP, KEY_STEP, rows), 2)
        positions = (jnp.sum(counts, 1) - 1.0).reshape(micro * rows)
        seen = (jnp.max(counts, -1) > 0).astype(jnp.int32).reshape(-1)
        frequency = ROPE_BASE ** (-jnp.arange(HEAD // 2, dtype=f32) / (HEAD // 2))
        angles = positions[:, None] * frequency[None, :]
        cosine, sine = jnp.cos(angles), jnp.sin(angles)
        cosine = jnp.concatenate([cosine, cosine], 1)
        sine = jnp.concatenate([-sine, sine], 1)

        hold = lax.optimization_barrier
        far = C // 2
        in_first = gather_first(in_own, "fsdp", F)
        in_first, mask, cosine, sine, seen, x = hold((in_first, mask, cosine, sine, seen, x))
        in_pieces = gather_rest(in_first, "fsdp", F)
        in_pieces, (out_own, cx_mine, expert_own) = held_pieces(
            in_pieces, (w_output.T, cx_mine, expert_own)
        )
        out_there = exchange_direct([out_own] * F, "fsdp", F)
        a, q, kv_own, in_all, router, gains = project_in(
            x.reshape(micro * rows, width), cosine, sine, in_pieces, micro, rows, experts
        )
        kv_ctx = jnp.concatenate(exchange_direct([kv_own] * C, "ctx", C), 1)
        kv_ctx, out_there, cx_mine = hold((kv_ctx, out_there, cx_mine))
        out_pieces = [(array, j * depth) for j, array in enumerate(out_there)]
        kv = exchange_direct([kv_ctx] * F, "fsdp", F)
        cx_there = [
            cx_mine if k == 0 else None if k == far else swap(cx_mine, "ctx", C, k)
            for k in range(C)
        ]
        cx_far, kv, cx_there, expert_own = hold((cx_mine, kv, cx_there, expert_own))
        kv = [(array, j * C * rows) for j, array in enumerate(kv)]
        expert_first = gather_first(expert_own, "fsdp", F)
        cx_there[far] = swap(cx_far, "ctx", C, far)
        branch, o, lse, wo_all = attend(seen, q, mask, kv, out_pieces)
        cx_other = [core(block) if k != far else None for k, block in enumerate(cx_there)]
        middle, b = second_norm(place, x, branch, core(pick(branch, 1 - t)), gains)
        b, middle, cx_there, cx_other = hold((b, middle, cx_there, cx_other))

        there = exchange_direct([b] * C, "ctx", C)
        expert_pieces = gather_rest(expert_first, "fsdp", F, 2)
        expert_there = [block for block in expert_first if block is not None]
        there, cx_there[far] = after((there, cx_there[far]), *expert_there)
        cx_other[far] = core(cx_there[far])
        cx_both = cx_there + cx_other
        b_both = there + [core(block) for block in there]
        part = rows // SLICES

        def to_sums(own, other):
            got = core(other)
            return [
                add_low(own[k * part : (k + 1) * part], got[k * part : (k + 1) * part])
                for k in range(C)
            ]

        outs, back_sums, sides = [], [], []
        sums = None
        for n in range(SLICES):
            out_mine, out_other, back_mine, back_other, *side = experts_rows(
                place,
                b_both,
                [n * part] * (2 * C),
                part,
                cx_both,
                after(router, *sums) if sums else router,
                expert_pieces,
                experts,
            )
            outs.append((out_mine, out_other))
            sides.append(side)
            sums = to_sums(back_mine, back_other)
            back_sums.append(exchange_direct(sums, "ctx", C))
        b_at = [n * part for n in range(SLICES) for _ in b_both]
        sides, _, outs = hold((sides, sums, outs))
        grads = experts_grads(b_both, cx_both, b_at, part, sides, local_experts, F)
        out_sums = [
            jnp.concatenate(pieces, 0) for pieces in zip(*[to_sums(*pair) for pair in outs])
        ]
        back_sums, grads, out_sums = hold((back_sums, grads, out_sums))

        def first_round(pieces):
            return [scatter_first(pieces[2 * n + 1], "fsdp", F, n == 0) for n in range(2)]

        def other_rounds(pieces, got):
            return [scatter_rest(pieces[2 * n], got[n], "fsdp", F, n == 0) for n in range(2)]

        grads_got = first_round(grads)
        for k in range(1, C):
            if k != far:
                out_sums[k] = swap(out_sums[k], "ctx", C, k)
        dmiddle, go, dl, dgain_two = second_norm_back(
            back_sums, middle, b, cx_mine, gains, router, experts
        )
        go_all, dq, *dkv = attend_back(
            place, seen, go, core(go), q, o, lse, mask, cosine, sine, wo_all, kv, F
        )
        go_all, dq, dkv, out_sums = hold((go_all, dq, dkv, out_sums))
        go_flat, o_flat = go_all.reshape(micro * rows, width), o.reshape(micro * rows, -1)

        dkv = exchange_direct(dkv, "fsdp", F)
        out_sums[far] = swap(out_sums[far], "ctx", C, far)
        total = dkv[0].astype(f32)
        for piece in dkv[1:]:
            total = total + piece.astype(f32)
        total = total.astype(bf16).reshape(micro, C, rows, 2 * HEAD)
        total, grads_got, out_sums = hold((total, grads_got, out_sums))
        grad_own = other_rounds(grads, grads_got)
        dkv = exchange_direct([total[:, k] for k in range(C)], "ctx", C)
        dkv, grad_own = hold((dkv, jnp.stack(grad_own)))
        gathered = lax.all_gather(grad_own, "ctx", axis=0)
        dkv, da = project_back(dkv, dq, cosine, sine, in_all)
        input_grad, dgain_one = first_norm_back(
            place, da, core(pick(da, 1 - t)), x, gains, dmiddle
        )
        attn_grads = attention_grads(
            a, go_flat, dq, dkv, o_flat, b, dl, dgain_one, dgain_two, experts, F
        )
        attn_got = first_round(attn_grads)
        pieces = other_rounds(attn_grads, attn_got)
        step = depth // C
        pieces = jnp.concatenate(pieces, 1)
        got = exchange_direct(
            [lax.dynamic_slice_in_dim(pieces, (c ^ k) * step, step, 0) for k in range(C)], "ctx", C
        )
        wide = w_query.shape[1]
        total = got[0].astype(f32)
        for piece in got[1:]:
            total = total + piece.astype(f32)
        total = total.astype(bf16)
        tail = total[:, wide + 2 * HEAD + o_flat.shape[1] :]
        total = jnp.concatenate([total[:, : wide + 2 * HEAD + o_flat.shape[1]], add_low(tail, core(tail))], 1)
        got = exchange_direct([total] * C, "ctx", C)
        grad_gate, grad_up, grad_down = assemble(gathered)
        grad_all = jnp.concatenate(ordered(got, c), 0).astype(f32)
        grad_q, grad_k, grad_v = jnp.split(grad_all[:, : wide + 2 * HEAD], (wide, wide + HEAD), 1)
        grad_out, grad_small = jnp.split(grad_all[:, wide + 2 * HEAD :], (o_flat.shape[1],), 1)
        result = sum((piece.astype(f32) for piece in out_sums), middle).astype(bf16)

        def whole(mine_value):
            other = core(mine_value)
            both = jnp.stack([pick((mine_value, other), t), pick((other, mine_value), t)])
            return lanes_relative(both, f, F)

        return (
            whole(result),
            whole(input_grad),
            grad_small[:, experts],
            grad_q,
            grad_k,
            grad_v,
            grad_out.T,
            grad_small[:, experts + 1],
            grad_small[:, :experts],
            grad_gate,
            grad_up,
            grad_down,
        )

    rows_of = P(None, ("fsdp", "ctx"), None)
    weights = (
        P("fsdp"),
        P("fsdp", "tp"),
        P("fsdp", "tp"),
        P("fsdp", "tp"),
        P("tp", "fsdp"),
        P("fsdp"),
        P("fsdp", None),
        P(None, "fsdp", "tp"),
        P(None, "fsdp", "tp"),
        P(None, "tp", "fsdp"),
    )
    return jax.shard_map(
        local,
        mesh=mesh,
        in_specs=(rows_of, *weights, P(), rows_of, rows_of),
        out_specs=(rows_of, rows_of, *weights),
        check_vma=False,
    )
```

time: 673 us -> 570 us (0.85)
  the two profiles are of different devices: /device:TPU:8 before, /device:TPU:0 now
where the time goes in v2:
time: 570 us; the launch traced here: 562 us
  waiting for transfers between devices  252 us (44%)
  starting transfers between devices  122 us (21%)
  Pallas kernels  101 us (18%)
  other arithmetic  37.8 us (7%)
  local copies, waits for them, and re-layouts  33.9 us (6%)
  between operations  15.1 us (3%)
    ppermute x70, waiting for transfers between devices, swap(): return lax.ppermute(value, axis, [(i, i ^ bit) for i in range(size)])  252 us
    ppermute x70, starting transfers between devices, swap(): return lax.ppermute(value, axis, [(i, i ^ bit) for i in range(size)])  122 us
    pallas_call x2, Pallas kernels, experts_rows(): pl.pallas_call(body, name='experts_rows', out_shape=(*[shape((half_rows,...  32.5 us
    unnamed x101, local copies, waits for them, and re-layouts  16.2 us
    pallas_call x1, Pallas kernels, experts_grads(): pl.pallas_call(body, name='experts_grads', out_shape=tuple([shape((half,...  13.6 us
  transfers between devices with their start and end apart: 71, of which 37 were waited for; matrix products, arithmetic and copies ran while one was open for 10% of the time, Pallas kernels for 10%

profile of v2, /device:TPU:0, one launch (start us, length us, event | category | flops | bytes accessed | tf_op | source)
XLA Modules:
  0.0 561.9 jit_solution(16859406623274264486)
XLA Ops:
  11.9 3.0 collective-permute-start
  22.3 1.9 slice_select_fusion
  29.0 2.0 constant_dynamic-slice_fusion.6
  33.7 2.1 pad_maximum_fusion.3.x_ref
  36.1 2.2 select_convert_fusion.mask_ref
  38.3 1.9 slice.233
  47.0 4.7 collective-permute-done.2.rest_3_
  51.8 2.1 collective-permute-done.3.rest_4_
  57.4 5.6 project_in.1
  64.6 2.6 collective-permute-start.5
  68.3 4.0 collective-permute-start.6
  72.3 3.3 collective-permute-done.5
  76.6 2.6 collective-permute-done.8.rest_6_
  79.2 1.8 collective-permute-done.9.rest_7_
  86.1 2.5 collective-permute-start.14
  88.5 7.9 %collective-permute-done.13.rest_9_.refs_9_ = bf16[128,1664]{1,0:T(8,128)(2,1)} collective-permute-done((bf16[128,1664]{1,0:T(8,128)(2,1)}, bf16[128,1664]{1,0:T(8,128)(2,1)}, u32[]{:S(2)}, u32[]{:S(2)}) %collective-permute-start.13) | collective-permute-done | bytes 426016 | tf_op jit(solution)/shard_map/ppermute | solution.py:55
  96.4 7.6 %collective-permute-done.14.rest_11_.refs_11_ = bf16[128,1664]{1,0:T(8,128)(2,1)} collective-permute-done((bf16[128,1664]{1,0:T(8,128)(2,1)}, bf16[128,1664]{1,0:T(8,128)(2,1)}, u32[]{:S(2)}, u32[]{:S(2)}) %collective-permute-start.14) | collective-permute-done | bytes 426016 | tf_op jit(solution)/shard_map/ppermute | solution.py:55
  106.8 2.5 collective-permute-start.16
  109.3 8.0 %attend.1 = (bf16[2,128,1536]{2,1,0:T(8,128)(2,1)}, bf16[2,128,768]{2,1,0:T(8,128)(2,1)}, f32[2,1,768]{2,1,0:T(1,128)}, bf16[1536,768]{1,0:T(8,128)(2,1)}) custom-call(s32[16]{0:T(128)} %reshape.190.seen_ref, bf16[2,768,128]{2,1,0:T(8,128)(2,1)} %get-tuple-element.169.q_ref, bf16[2,2048,128]{2,1,0:T(8,128)(2,1)} %select_convert_fusion.mask_ref, ...), custom_call_target="tpu_custom_call" | custom-call | flops 2214592512 | bytes 6815744 | tf_op jit(solution)/shard_map/attend/pallas_call | solution.py:298
  120.4 2.4 collective-permute-done.16.rest_10_.refs_10_
  123.4 2.7 second_norm.1
  126.9 3.4 collective-permute-start.21
  130.6 11.5 %collective-permute-done.23.rest_17_ = bf16[2,3,384,384]{3,2,1,0:T(8,128)(2,1)S(1)} collective-permute-done((bf16[2,3,384,384]{3,2,1,0:T(8,128)(2,1)S(1)}, bf16[2,3,384,384]{3,2,1,0:T(8,128)(2,1)S(1)}, u32[]{:S(2)}, u32[]{:S(2)}) %collective-permute-start.23) | collective-permute-done | bytes 1769504 | tf_op jit(solution)/shard_map/ppermute | solution.py:55
  142.7 2.3 collective-permute-done.24.rest_18_
  146.2 2.2 collective-permute-start.31
  148.4 8.9 %collective-permute-done.21.rest_2_.refs_2_ = bf16[128,1536]{1,0:T(8,128)(2,1)S(1)} collective-permute-done((bf16[128,1536]{1,0:T(8,128)(2,1)}, bf16[128,1536]{1,0:T(8,128)(2,1)S(1)}, u32[]{:S(2)}, u32[]{:S(2)}) %collective-permute-start.21) | collective-permute-done | bytes 393248 | tf_op jit(solution)/shard_map/ppermute | solution.py:55
  163.9 16.1 %experts_rows.2 = (bf16[256,1536]{1,0:T(8,128)(2,1)}, bf16[256,1536]{1,0:T(8,128)(2,1)}, bf16[256,1664]{1,0:T(8,128)(2,1)}, bf16[256,1664]{1,0:T(8,128)(2,1)}, b...) custom-call(s32[3]{0:T(128)} %pad_add_fusion.place_ref, ...), custom_call_target="tpu_custom_call" | custom-call | flops 7247757312 | bytes 13369344 | tf_op jit(solution)/shard_map/experts_rows/pallas_call | solution.py:445
  180.1 2.5 collective-permute-done.32
  182.6 2.3 add_convert_fusion.19
  184.9 16.5 %experts_rows.3 = (bf16[256,1536]{1,0:T(8,128)(2,1)}, bf16[256,1536]{1,0:T(8,128)(2,1)}, bf16[256,1664]{1,0:T(8,128)(2,1)}, bf16[256,1664]{1,0:T(8,128)(2,1)}, b...) custom-call(s32[3]{0:T(128)} %pad_add_fusion.place_ref, ...), custom_call_target="tpu_custom_call" | custom-call | flops 7247757312 | bytes 13369344 | tf_op jit(solution)/shard_map/experts_rows/pallas_call | solution.py:445
  201.6 2.4 collective-permute-done.36
  204.0 2.3 add_convert_fusion.15
  206.5 8.5 %collective-permute-start.33 = (bf16[64,1664]{1,0:T(8,128)(2,1)}, bf16[64,1664]{1,0:T(8,128)(2,1)}, u32[]{:S(2)}, u32[]{:S(2)}) collective-permute-start(bf16[64,1664]{1,0:T(8,128)(2,1)} %get-tuple-element.362), channel_id=1, source_target_pairs={{0,2},{2,0},{4,6},{6,4},{1,3},{3,1},{5,7},{7,5},{8,10},{10,8},{12,... | collective-permute-start | bytes 638984 | tf_op jit(solution)/shard_map/ppermute | solution.py:55
  217.4 13.6 %experts_grads.1 = (bf16[2,2,3,192,384]{4,3,2,1,0:T(8,128)(2,1)}, bf16[2,2,3,192,384]{4,3,2,1,0:T(8,128)(2,1)}, bf16[2,2,3,192,384]{4,3,2,1,0:T(8,128)(2,1)}, bf16[2,2,3,192,384]{4,3,2,1,0:T(8,128)(2,1)}) custom-call(bf16[128,1536]{1,0:T(8,128)(2,1)} %get-tuple-element.198.rest_0_.refs_0_.refs_9_.b_ref, bf16[128,1536]{1,0:T(8,128)(2,1)} %copy-done.39, ...), custom_call_target="tpu_custom_call" | custom-call | flops 7247757312 | bytes 18087936 | tf_op jit(solution)/shard_map/experts_grads/pallas_call | solution.py:533
  232.4 1.9 collective-permute-start.38
  238.5 3.9 collective-permute-done.37.refs_5_
  242.4 9.1 %collective-permute-done.38.refs_6_ = bf16[64,1664]{1,0:T(8,128)(2,1)S(1)} collective-permute-done((bf16[64,1664]{1,0:T(8,128)(2,1)}, bf16[64,1664]{1,0:T(8,128)(2,1)S(1)}, u32[]{:S(2)}, u32[]{:S(2)}) %collective-permute-start.38) | collective-permute-done | bytes 213024 | tf_op jit(solution)/shard_map/ppermute | solution.py:55
  254.4 4.8 second_norm_back.1
  259.2 4.5 collective-permute-start.43
  263.7 2.4 collective-permute-start.44
  266.1 9.8 %attend_back.1 = (bf16[2,128,1536]{2,1,0:T(8,128)(2,1)}, bf16[256,768]{1,0:T(8,128)(2,1)}, bf16[2,512,256]{2,1,0:T(8,128)(2,1)}, bf16[2,512,256]{2,1,0:T(8,128)(...) custom-call(s32[3]{0:T(128)} %pad_add_fusion.place_ref, s32[16]{0:T(128)} %reshape.190.seen_ref, ...), custom_call_target="tpu_custom_call" | custom-call | flops 4026531840 | bytes 6553600 | tf_op jit(solution)/shard_map/attend_back/pallas_call | solution.py:676
  275.9 8.4 %collective-permute-done.44 = bf16[128,1536]{1,0:T(8,128)(2,1)} collective-permute-done((bf16[128,1536]{1,0:T(8,128)(2,1)S(1)}, bf16[128,1536]{1,0:T(8,128)(2,1)}, u32[]{:S(2)}, u32[]{:S(2)}) %collective-permute-start.44) | collective-permute-done | bytes 393248 | tf_op jit(solution)/shard_map/ppermute | solution.py:55
  287.8 18.7 %collective-permute-done.45 = bf16[2,512,256]{2,1,0:T(8,128)(2,1)S(1)} collective-permute-done((bf16[2,512,256]{2,1,0:T(8,128)(2,1)}, bf16[2,512,256]{2,1,0:T(8,128)(2,1)S(1)}, u32[]{:S(2)}, u32[]{:S(2)}) %collective-permute-start.45) | collective-permute-done | bytes 524320 | tf_op jit(solution)/shard_map/ppermute | solution.py:55
  306.5 4.5 collective-permute-start.50
  311.0 4.4 collective-permute-done.47
  316.7 8.6 %collective-permute-done.50 = bf16[128,1536]{1,0:T(8,128)(2,1)S(1)} collective-permute-done((bf16[128,1536]{1,0:T(8,128)(2,1)}, bf16[128,1536]{1,0:T(8,128)(2,1)S(1)}, u32[]{:S(2)}, u32[]{:S(2)}) %collective-permute-start.50) | collective-permute-done | bytes 393248 | tf_op jit(solution)/shard_map/ppermute | solution.py:55
  326.3 1.8 collective-permute-start.55
  330.6 2.0 collective-permute-start.53
  332.6 2.4 collective-permute-start.54
  335.0 11.8 %collective-permute-done.55 = bf16[1,2,3,192,384]{4,3,2,1,0:T(8,128)(2,1)S(1)} collective-permute-done((bf16[1,2,3,192,384]{4,3,2,1,0:T(8,128)(2,1)S(1)}, bf16[1,2,3,192,384]{4,3,2,1,0:T(8,128)(2,1)S(1)}, u32[]{:S(2)}, u32[]{:S(2)}) %collective-permute-start.55) | collective-permute-done | bytes 884768 | tf_op jit(solution)/shard_map/ppermute | solution.py:55
  351.1 5.5 project_back.1
  360.4 3.2 first_norm_back.1
  363.6 5.6 attention_grads.1
  372.8 29.0 %collective-permute-done.61 = bf16[2,384,896]{2,1,0:T(8,128)(2,1)} collective-permute-done((bf16[2,384,896]{2,1,0:T(8,128)(2,1)}, bf16[2,384,896]{2,1,0:T(8,128)(2,1)}, u32[]{:S(2)}, u32[]{:S(2)}) %collective-permute-start.61) | collective-permute-done | bytes 1376288 | tf_op jit(solution)/shard_map/ppermute | solution.py:55
  404.6 2.4 collective-permute-done.59
  409.3 11.6 %collective-permute-done.62 = bf16[1,384,896]{2,1,0:T(8,128)(2,1)S(1)} collective-permute-done((bf16[1,384,896]{2,1,0:T(8,128)(2,1)S(1)}, bf16[1,384,896]{2,1,0:T(8,128)(2,1)S(1)}, u32[]{:S(2)}, u32[]{:S(2)}) %collective-permute-start.62) | collective-permute-done | bytes 688160 | tf_op jit(solution)/shard_map/ppermute | solution.py:55
  422.2 2.8 collective-permute-done.60
  425.6 2.7 collective-permute-start.64
  431.0 26.3 %collective-permute-done.63 = bf16[96,1920]{1,0:T(8,128)(2,1)S(1)} collective-permute-done((bf16[96,1920]{1,0:T(8,128)(2,1)S(1)}, bf16[96,1920]{1,0:T(8,128)(2,1)S(1)}, u32[]{:S(2)}, u32[]{:S(2)}) %collective-permute-start.63) | collective-permute-done | bytes 368672 | tf_op jit(solution)/shard_map/ppermute | solution.py:55
  457.4 10.7 %collective-permute-done.64 = bf16[96,1920]{1,0:T(8,128)(2,1)S(1)} collective-permute-done((bf16[96,1920]{1,0:T(8,128)(2,1)S(1)}, bf16[96,1920]{1,0:T(8,128)(2,1)S(1)}, u32[]{:S(2)}, u32[]{:S(2)}) %collective-permute-start.64) | collective-permute-done | bytes 368672 | tf_op jit(solution)/shard_map/ppermute | solution.py:55
  468.1 7.4 %collective-permute-done.65 = bf16[96,1920]{1,0:T(8,128)(2,1)S(1)} collective-permute-done((bf16[96,1920]{1,0:T(8,128)(2,1)S(1)}, bf16[96,1920]{1,0:T(8,128)(2,1)S(1)}, u32[]{:S(2)}, u32[]{:S(2)}) %collective-permute-start.65) | collective-permute-done | bytes 368672 | tf_op jit(solution)/shard_map/ppermute | solution.py:55
  478.8 32.7 %collective-permute-start.68 = (bf16[96,1920]{1,0:T(8,128)(2,1)S(1)}, bf16[96,1920]{1,0:T(8,128)(2,1)S(1)}, u32[]{:S(2)}, u32[]{:S(2)}) collective-permute-start(bf16[96,1920]{1,0:T(8,128)(2,1)S(1)} %pad_maximum_fusion.10), channel_id=1, source_target_pairs={{0,4},{2,6},{4,0},{6,2},{1,5},{3,7},{5,1},{7,3},{8,12},{10,14},{12... | collective-permute-start | bytes 1105928 | tf_op jit(solution)/shard_map/ppermute | solution.py:55
  513.0 26.3 %collective-permute-done.68 = bf16[96,1920]{1,0:T(8,128)(2,1)S(1)} collective-permute-done((bf16[96,1920]{1,0:T(8,128)(2,1)S(1)}, bf16[96,1920]{1,0:T(8,128)(2,1)S(1)}, u32[]{:S(2)}, u32[]{:S(2)}) %collective-permute-start.68) | collective-permute-done | bytes 368672 | tf_op jit(solution)/shard_map/ppermute | solution.py:55
  544.7 10.1 %assemble.1 = (f32[8,384,384]{2,1,0:T(8,128)}, f32[8,384,384]{2,1,0:T(8,128)}, f32[8,384,384]{2,1,0:T(8,128)}) custom-call(bf16[4,2,2,3,192,384]{5,4,3,2,1,0:T(8,128)(2,1)} %bitcast.78), custom_call_target="tpu_custom_call" | custom-call | flops 3538944 | bytes 21233664 | tf_op jit(solution)/shard_map/assemble/pallas_call | solution.py:773
  (289 shorter events, 105.7 us)
Async XLA Ops:
  7.2 537.5 %all-gather.3.cloned.1.call-start = ((), (), s32[]{:S(2)}) async-start(), calls=%async_computation | async-start | bytes 8847360 | tf_op jit(solution)/shard_map/all_gather | solution.py:1016
  11.9 26.5 %collective-permute-start = (bf16[384,1152]{1,0:T(8,128)(2,1)S(1)}, bf16[384,1152]{1,0:T(8,128)(2,1)}, u32[]{:S(2)}, u32[]{:S(2)}) collective-permute-start(bf16[384,1152]{1,0:T(8,128)(2,1)S(1)} %concatenate.45.rest_0_), channel_id=1, source_target_pairs={{0,8},{8,0},{16,24},{24,16},{1,9},{9,1},{17,25},{25,17},{2,10},{10... | collective-permute-start | bytes 2654216 | tf_op jit(solution)/shard_map/ppermute | solution.py:55
  14.9 23.5 %collective-permute-start.1 = (bf16[384,1152]{1,0:T(8,128)(2,1)S(1)}, bf16[384,1152]{1,0:T(8,128)(2,1)}, u32[]{:S(2)}, u32[]{:S(2)}) collective-permute-start(bf16[384,1152]{1,0:T(8,128)(2,1)S(1)} %concatenate.45.rest_0_), channel_id=1, source_target_pairs={{0,16},{8,24},{16,0},{24,8},{1,17},{9,25},{17,1},{25,9},{2,18},{10... | collective-permute-start | bytes 2654216 | tf_op jit(solution)/shard_map/ppermute | solution.py:55
  40.2 11.6 %collective-permute-start.2 = (bf16[192,1152]{1,0:T(8,128)(2,1)}, bf16[192,1152]{1,0:T(8,128)(2,1)S(1)}, u32[]{:S(2)}, u32[]{:S(2)}) collective-permute-start(bf16[192,1152]{1,0:T(8,128)(2,1)} %slice.233), channel_id=1, source_target_pairs={{0,16},{8,24},{16,0},{24,8},{1,17},{9,25},{17,1},{25,9},{2,18},{10... | collective-permute-start | bytes 1327112 | tf_op jit(solution)/shard_map/ppermute | solution.py:55
  42.5 11.4 %collective-permute-start.3 = (bf16[192,1152]{1,0:T(8,128)(2,1)}, bf16[192,1152]{1,0:T(8,128)(2,1)}, u32[]{:S(2)}, u32[]{:S(2)}) collective-permute-start(bf16[192,1152]{1,0:T(8,128)(2,1)} %slice.234), channel_id=1, source_target_pairs={{0,8},{8,0},{16,24},{24,16},{1,9},{9,1},{17,25},{25,17},{2,10},{10... | collective-permute-start | bytes 1327112 | tf_op jit(solution)/shard_map/ppermute | solution.py:55
  53.9 22.7 %collective-permute-start.7 = (bf16[384,768]{1,0:T(8,128)(2,1)S(1)}, bf16[384,768]{1,0:T(8,128)(2,1)}, u32[]{:S(2)}, u32[]{:S(2)}) collective-permute-start(bf16[384,768]{1,0:T(8,128)(2,1)S(1)} %bitcast.81), channel_id=1, source_target_pairs={{0,8},{8,0},{16,24},{24,16},{1,9},{9,1},{17,25},{25,17},{2,10},{10... | collective-permute-start | bytes 1769480 | tf_op jit(solution)/shard_map/ppermute | solution.py:55
  54.3 24.9 %collective-permute-start.8 = (bf16[384,768]{1,0:T(8,128)(2,1)S(1)}, bf16[384,768]{1,0:T(8,128)(2,1)}, u32[]{:S(2)}, u32[]{:S(2)}) collective-permute-start(bf16[384,768]{1,0:T(8,128)(2,1)S(1)} %bitcast.82), channel_id=1, source_target_pairs={{0,16},{8,24},{16,0},{24,8},{1,17},{9,25},{17,1},{25,9},{2,18},{10... | collective-permute-start | bytes 1769480 | tf_op jit(solution)/shard_map/ppermute | solution.py:55
  56.0 25.0 %collective-permute-start.9 = (bf16[384,768]{1,0:T(8,128)(2,1)S(1)}, bf16[384,768]{1,0:T(8,128)(2,1)}, u32[]{:S(2)}, u32[]{:S(2)}) collective-permute-start(bf16[384,768]{1,0:T(8,128)(2,1)S(1)} %bitcast.83), channel_id=1, source_target_pairs={{0,24},{8,16},{16,8},{24,0},{1,25},{9,17},{17,9},{25,1},{2,26},{10... | collective-permute-start | bytes 1769480 | tf_op jit(solution)/shard_map/ppermute | solution.py:55
  63.0 5.3 collective-permute-start.4
  64.6 11.0 %collective-permute-start.5 = (bf16[2,128,256]{2,1,0:T(8,128)(2,1)}, bf16[2,128,256]{2,1,0:T(8,128)(2,1)S(1)}, u32[]{:S(2)}, u32[]{:S(2)}) collective-permute-start(bf16[2,128,256]{2,1,0:T(8,128)(2,1)} %get-tuple-element.171), channel_id=1, source_target_pairs={{0,4},{2,6},{4,0},{6,2},{1,5},{3,7},{5,1},{7,3},{8,12},{10,14},{12... | collective-permute-start | bytes 393224 | tf_op jit(solution)/shard_map/ppermute | solution.py:55
  68.3 7.3 %collective-permute-start.6 = (bf16[2,128,256]{2,1,0:T(8,128)(2,1)}, bf16[2,128,256]{2,1,0:T(8,128)(2,1)S(1)}, u32[]{:S(2)}, u32[]{:S(2)}) collective-permute-start(bf16[2,128,256]{2,1,0:T(8,128)(2,1)} %get-tuple-element.171), channel_id=1, source_target_pairs={{0,6},{2,4},{4,2},{6,0},{1,7},{3,5},{5,3},{7,1},{8,14},{10,12},{12... | collective-permute-start | bytes 393224 | tf_op jit(solution)/shard_map/ppermute | solution.py:55
  81.0 23.0 %collective-permute-start.10 = (bf16[2,512,256]{2,1,0:T(8,128)(2,1)S(1)}, bf16[2,512,256]{2,1,0:T(8,128)(2,1)S(1)}, u32[]{:S(2)}, u32[]{:S(2)}) collective-permute-start(bf16[2,512,256]{2,1,0:T(8,128)(2,1)S(1)} %pad_maximum_fusion.5.rest_0_), channel_id=1, source_target_pairs={{0,8},{8,0},{16,24},{24,16},{1,9},{9,1},{17,25},{25,17},{2,10},{10... | collective-permute-start | bytes 1572872 | tf_op jit(solution)/shard_map/ppermute | solution.py:55
  81.7 22.3 %collective-permute-start.11 = (bf16[2,512,256]{2,1,0:T(8,128)(2,1)S(1)}, bf16[2,512,256]{2,1,0:T(8,128)(2,1)S(1)}, u32[]{:S(2)}, u32[]{:S(2)}) collective-permute-start(bf16[2,512,256]{2,1,0:T(8,128)(2,1)S(1)} %pad_maximum_fusion.5.rest_0_), channel_id=1, source_target_pairs={{0,16},{8,24},{16,0},{24,8},{1,17},{9,25},{17,1},{25,9},{2,18},{10... | collective-permute-start | bytes 1572872 | tf_op jit(solution)/shard_map/ppermute | solution.py:55
  83.3 22.3 %collective-permute-start.12 = (bf16[2,512,256]{2,1,0:T(8,128)(2,1)S(1)}, bf16[2,512,256]{2,1,0:T(8,128)(2,1)}, u32[]{:S(2)}, u32[]{:S(2)}) collective-permute-start(bf16[2,512,256]{2,1,0:T(8,128)(2,1)S(1)} %pad_maximum_fusion.5.rest_0_), channel_id=1, source_target_pairs={{0,24},{8,16},{16,8},{24,0},{1,25},{9,17},{17,9},{25,1},{2,26},{10... | collective-permute-start | bytes 1572872 | tf_op jit(solution)/shard_map/ppermute | solution.py:55
  84.5 11.9 %collective-permute-start.13 = (bf16[128,1664]{1,0:T(8,128)(2,1)}, bf16[128,1664]{1,0:T(8,128)(2,1)}, u32[]{:S(2)}, u32[]{:S(2)}) collective-permute-start(bf16[128,1664]{1,0:T(8,128)(2,1)} %convert_dynamic-update-slice_fusion.rest_8_.refs_8_.refs_10_), channel_id=1, source_target_pairs={{0,2},{2,0},{4,6},{6,4},{1,3},{3,1},{5,7},{7,5},{8,10},{10,8},{12,... | collective-permute-start | bytes 1277960 | tf_op jit(solution)/shard_map/ppermute | solution.py:55
  86.1 17.9 %collective-permute-start.14 = (bf16[128,1664]{1,0:T(8,128)(2,1)}, bf16[128,1664]{1,0:T(8,128)(2,1)}, u32[]{:S(2)}, u32[]{:S(2)}) collective-permute-start(bf16[128,1664]{1,0:T(8,128)(2,1)} %convert_dynamic-update-slice_fusion.rest_8_.refs_8_.refs_10_), channel_id=1, source_target_pairs={{0,6},{2,4},{4,2},{6,0},{1,7},{3,5},{5,3},{7,1},{8,14},{10,12},{12... | collective-permute-start | bytes 1277960 | tf_op jit(solution)/shard_map/ppermute | solution.py:55
  105.6 36.5 %collective-permute-start.23 = (bf16[2,3,384,384]{3,2,1,0:T(8,128)(2,1)S(1)}, bf16[2,3,384,384]{3,2,1,0:T(8,128)(2,1)S(1)}, u32[]{:S(2)}, u32[]{:S(2)}) collective-permute-start(bf16[2,3,384,384]{3,2,1,0:T(8,128)(2,1)S(1)} %pad_maximum_fusion.rest_16_), channel_id=1, source_target_pairs={{0,8},{8,0},{16,24},{24,16},{1,9},{9,1},{17,25},{25,17},{2,10},{10... | collective-permute-start | bytes 5308424 | tf_op jit(solution)/shard_map/ppermute | solution.py:55
  106.2 38.8 %collective-permute-start.24 = (bf16[2,3,384,384]{3,2,1,0:T(8,128)(2,1)S(1)}, bf16[2,3,384,384]{3,2,1,0:T(8,128)(2,1)}, u32[]{:S(2)}, u32[]{:S(2)}) collective-permute-start(bf16[2,3,384,384]{3,2,1,0:T(8,128)(2,1)S(1)} %pad_maximum_fusion.rest_16_), channel_id=1, source_target_pairs={{0,16},{8,24},{16,0},{24,8},{1,17},{9,25},{17,1},{25,9},{2,18},{10... | collective-permute-start | bytes 5308424 | tf_op jit(solution)/shard_map/ppermute | solution.py:55
  106.8 16.1 %collective-permute-start.16 = (bf16[128,1664]{1,0:T(8,128)(2,1)}, bf16[128,1664]{1,0:T(8,128)(2,1)}, u32[]{:S(2)}, u32[]{:S(2)}) collective-permute-start(bf16[128,1664]{1,0:T(8,128)(2,1)} %convert_dynamic-update-slice_fusion.rest_8_.refs_8_.refs_10_), channel_id=1, source_target_pairs={{0,4},{2,6},{4,0},{6,2},{1,5},{3,7},{5,1},{7,3},{8,12},{10,14},{12... | collective-permute-start | bytes 1277960 | tf_op jit(solution)/shard_map/ppermute | solution.py:55
  118.5 7.6 %collective-permute-start.17 = (bf16[128,1664]{1,0:T(8,128)(2,1)}, bf16[128,1664]{1,0:T(8,128)(2,1)}, u32[]{:S(2)}, u32[]{:S(2)}) collective-permute-start(bf16[128,1664]{1,0:T(8,128)(2,1)} %convert_dynamic-update-slice_fusion.rest_8_.refs_8_.refs_10_), channel_id=1, source_target_pairs={{0,1},{1,0},{2,3},{3,2},{4,5},{5,4},{6,7},{7,6},{8,9},{9,8},{10,11... | collective-permute-start | bytes 1277960 | tf_op jit(solution)/shard_map/ppermute | solution.py:55
  120.2 5.9 %collective-permute-start.18 = (bf16[128,1664]{1,0:T(8,128)(2,1)}, bf16[128,1664]{1,0:T(8,128)(2,1)}, u32[]{:S(2)}, u32[]{:S(2)}) collective-permute-start(bf16[128,1664]{1,0:T(8,128)(2,1)} %collective-permute-done.13.rest_9_.refs_9_), channel_id=1, source_target_pairs={{0,1},{1,0},{2,3},{3,2},{4,5},{5,4},{6,7},{7,6},{8,9},{9,8},{10,11... | collective-permute-start | bytes 1277960 | tf_op jit(solution)/shard_map/ppermute | solution.py:55
  122.8 3.3 collective-permute-start.19
  126.2 22.2 %collective-permute-start.20 = (bf16[128,1536]{1,0:T(8,128)(2,1)}, bf16[128,1536]{1,0:T(8,128)(2,1)S(1)}, u32[]{:S(2)}, u32[]{:S(2)}) collective-permute-start(bf16[128,1536]{1,0:T(8,128)(2,1)} %get-tuple-element.198.rest_0_.refs_0_.refs_9_.b_ref), channel_id=1, source_target_pairs={{0,2},{2,0},{4,6},{6,4},{1,3},{3,1},{5,7},{7,5},{8,10},{10,8},{12,... | collective-permute-start | bytes 1179656 | tf_op jit(solution)/shard_map/ppermute | solution.py:55
  126.9 30.4 %collective-permute-start.21 = (bf16[128,1536]{1,0:T(8,128)(2,1)}, bf16[128,1536]{1,0:T(8,128)(2,1)S(1)}, u32[]{:S(2)}, u32[]{:S(2)}) collective-permute-start(bf16[128,1536]{1,0:T(8,128)(2,1)} %get-tuple-element.198.rest_0_.refs_0_.refs_9_.b_ref), channel_id=1, source_target_pairs={{0,4},{2,6},{4,0},{6,2},{1,5},{3,7},{5,1},{7,3},{8,12},{10,14},{12... | collective-permute-start | bytes 1179656 | tf_op jit(solution)/shard_map/ppermute | solution.py:55
  130.3 27.0 %collective-permute-start.22 = (bf16[128,1536]{1,0:T(8,128)(2,1)}, bf16[128,1536]{1,0:T(8,128)(2,1)S(1)}, u32[]{:S(2)}, u32[]{:S(2)}) collective-permute-start(bf16[128,1536]{1,0:T(8,128)(2,1)} %get-tuple-element.198.rest_0_.refs_0_.refs_9_.b_ref), channel_id=1, source_target_pairs={{0,6},{2,4},{4,2},{6,0},{1,7},{3,5},{5,3},{7,1},{8,14},{10,12},{12... | collective-permute-start | bytes 1179656 | tf_op jit(solution)/shard_map/ppermute | solution.py:55
  142.2 19.8 %collective-permute-start.30 = (bf16[2,3,192,384]{3,2,1,0:T(8,128)(2,1)S(1)}, bf16[2,3,192,384]{3,2,1,0:T(8,128)(2,1)S(1)}, u32[]{:S(2)}, u32[]{:S(2)}) collective-permute-start(bf16[2,3,192,384]{3,2,1,0:T(8,128)(2,1)S(1)} %slice.302), channel_id=1, source_target_pairs={{0,16},{8,24},{16,0},{24,8},{1,17},{9,25},{17,1},{25,9},{2,18},{10... | collective-permute-start | bytes 2654216 | tf_op jit(solution)/shard_map/ppermute | solution.py:55
  146.2 15.8 %collective-permute-start.31 = (bf16[2,3,192,384]{3,2,1,0:T(8,128)(2,1)S(1)}, bf16[2,3,192,384]{3,2,1,0:T(8,128)(2,1)S(1)}, u32[]{:S(2)}, u32[]{:S(2)}) collective-permute-start(bf16[2,3,192,384]{3,2,1,0:T(8,128)(2,1)S(1)} %slice.303), channel_id=1, source_target_pairs={{0,8},{8,0},{16,24},{24,16},{1,9},{9,1},{17,25},{25,17},{2,10},{10... | collective-permute-start | bytes 2654216 | tf_op jit(solution)/shard_map/ppermute | solution.py:55
  157.4 2.8 collective-permute-start.26
  157.9 4.1 collective-permute-start.29
  179.9 2.7 collective-permute-start.32
  206.3 24.7 %collective-permute-start.40 = (bf16[256,1536]{1,0:T(8,128)(2,1)}, bf16[256,1536]{1,0:T(8,128)(2,1)S(1)}, u32[]{:S(2)}, u32[]{:S(2)}) collective-permute-start(bf16[256,1536]{1,0:T(8,128)(2,1)} %get-tuple-element.235), channel_id=1, source_target_pairs={{0,1},{1,0},{2,3},{3,2},{4,5},{5,4},{6,7},{7,6},{8,9},{9,8},{10,11... | collective-permute-start | bytes 2359304 | tf_op jit(solution)/shard_map/ppermute | solution.py:55
  206.5 29.6 %collective-permute-start.33 = (bf16[64,1664]{1,0:T(8,128)(2,1)}, bf16[64,1664]{1,0:T(8,128)(2,1)}, u32[]{:S(2)}, u32[]{:S(2)}) collective-permute-start(bf16[64,1664]{1,0:T(8,128)(2,1)} %get-tuple-element.362), channel_id=1, source_target_pairs={{0,2},{2,0},{4,6},{6,4},{1,3},{3,1},{5,7},{7,5},{8,10},{10,8},{12,... | collective-permute-start | bytes 638984 | tf_op jit(solution)/shard_map/ppermute | solution.py:55
  215.0 23.5 %collective-permute-start.34 = (bf16[64,1664]{1,0:T(8,128)(2,1)}, bf16[64,1664]{1,0:T(8,128)(2,1)}, u32[]{:S(2)}, u32[]{:S(2)}) collective-permute-start(bf16[64,1664]{1,0:T(8,128)(2,1)} %get-tuple-element.361), channel_id=1, source_target_pairs={{0,4},{2,6},{4,0},{6,2},{1,5},{3,7},{5,1},{7,3},{8,12},{10,14},{12... | collective-permute-start | bytes 638984 | tf_op jit(solution)/shard_map/ppermute | solution.py:55
  215.9 22.5 %collective-permute-start.35 = (bf16[64,1664]{1,0:T(8,128)(2,1)}, bf16[64,1664]{1,0:T(8,128)(2,1)}, u32[]{:S(2)}, u32[]{:S(2)}) collective-permute-start(bf16[64,1664]{1,0:T(8,128)(2,1)} %get-tuple-element.360), channel_id=1, source_target_pairs={{0,6},{2,4},{4,2},{6,0},{1,7},{3,5},{5,3},{7,1},{8,14},{10,12},{12... | collective-permute-start | bytes 638984 | tf_op jit(solution)/shard_map/ppermute | solution.py:55
  217.4 15.0 %collective-permute-start.41 = (bf16[256,1536]{1,0:T(8,128)(2,1)}, bf16[256,1536]{1,0:T(8,128)(2,1)S(1)}, u32[]{:S(2)}, u32[]{:S(2)}) collective-permute-start(bf16[256,1536]{1,0:T(8,128)(2,1)} %get-tuple-element.237), channel_id=1, source_target_pairs={{0,1},{1,0},{2,3},{3,2},{4,5},{5,4},{6,7},{7,6},{8,9},{9,8},{10,11... | collective-permute-start | bytes 2359304 | tf_op jit(solution)/shard_map/ppermute | solution.py:55
  231.0 11.3 %collective-permute-start.37 = (bf16[64,1664]{1,0:T(8,128)(2,1)}, bf16[64,1664]{1,0:T(8,128)(2,1)S(1)}, u32[]{:S(2)}, u32[]{:S(2)}) collective-permute-start(bf16[64,1664]{1,0:T(8,128)(2,1)} %get-tuple-element.358), channel_id=1, source_target_pairs={{0,2},{2,0},{4,6},{6,4},{1,3},{3,1},{5,7},{7,5},{8,10},{10,8},{12,... | collective-permute-start | bytes 638984 | tf_op jit(solution)/shard_map/ppermute | solution.py:55
  232.4 19.1 %collective-permute-start.38 = (bf16[64,1664]{1,0:T(8,128)(2,1)}, bf16[64,1664]{1,0:T(8,128)(2,1)S(1)}, u32[]{:S(2)}, u32[]{:S(2)}) collective-permute-start(bf16[64,1664]{1,0:T(8,128)(2,1)} %get-tuple-element.357), channel_id=1, source_target_pairs={{0,4},{2,6},{4,0},{6,2},{1,5},{3,7},{5,1},{7,3},{8,12},{10,14},{12... | collective-permute-start | bytes 638984 | tf_op jit(solution)/shard_map/ppermute | solution.py:55
  236.1 15.4 %collective-permute-start.39 = (bf16[64,1664]{1,0:T(8,128)(2,1)S(1)}, bf16[64,1664]{1,0:T(8,128)(2,1)S(1)}, u32[]{:S(2)}, u32[]{:S(2)}) collective-permute-start(bf16[64,1664]{1,0:T(8,128)(2,1)S(1)} %copy-done.26), channel_id=1, source_target_pairs={{0,6},{2,4},{4,2},{6,0},{1,7},{3,5},{5,3},{7,1},{8,14},{10,12},{12... | collective-permute-start | bytes 638984 | tf_op jit(solution)/shard_map/ppermute | solution.py:55
  252.2 73.1 %collective-permute-start.48 = (bf16[2,2,3,192,384]{4,3,2,1,0:T(8,128)(2,1)}, bf16[2,2,3,192,384]{4,3,2,1,0:T(8,128)(2,1)S(1)}, u32[]{:S(2)}, u32[]{:S(2)}) collective-permute-start(bf16[2,2,3,192,384]{4,3,2,1,0:T(8,128)(2,1)} %get-tuple-element.264), channel_id=1, source_target_pairs={{0,16},{8,24},{16,0},{24,8},{1,17},{9,25},{17,1},{25,9},{2,18},{10... | collective-permute-start | bytes 5308424 | tf_op jit(solution)/shard_map/ppermute | solution.py:55
  253.5 71.8 %collective-permute-start.49 = (bf16[2,2,3,192,384]{4,3,2,1,0:T(8,128)(2,1)}, bf16[2,2,3,192,384]{4,3,2,1,0:T(8,128)(2,1)S(1)}, u32[]{:S(2)}, u32[]{:S(2)}) collective-permute-start(bf16[2,2,3,192,384]{4,3,2,1,0:T(8,128)(2,1)} %get-tuple-element.265), channel_id=1, source_target_pairs={{0,8},{8,0},{16,24},{24,16},{1,9},{9,1},{17,25},{25,17},{2,10},{10... | collective-permute-start | bytes 5308424 | tf_op jit(solution)/shard_map/ppermute | solution.py:55
  259.2 6.9 %collective-permute-start.42 = (bf16[128,1536]{1,0:T(8,128)(2,1)}, bf16[128,1536]{1,0:T(8,128)(2,1)}, u32[]{:S(2)}, u32[]{:S(2)}) collective-permute-start(bf16[128,1536]{1,0:T(8,128)(2,1)} %get-tuple-element.246.own_ref), channel_id=1, source_target_pairs={{0,1},{1,0},{2,3},{3,2},{4,5},{5,4},{6,7},{7,6},{8,9},{9,8},{10,11... | collective-permute-start | bytes 1179656 | tf_op jit(solution)/shard_map/ppermute | solution.py:55
  259.2 16.7 %collective-permute-start.43 = (bf16[128,1536]{1,0:T(8,128)(2,1)}, bf16[128,1536]{1,0:T(8,128)(2,1)}, u32[]{:S(2)}, u32[]{:S(2)}) collective-permute-start(bf16[128,1536]{1,0:T(8,128)(2,1)} %pad_maximum_fusion.7), channel_id=1, source_target_pairs={{0,2},{2,0},{4,6},{6,4},{1,3},{3,1},{5,7},{7,5},{8,10},{10,8},{12,... | collective-permute-start | bytes 1179656 | tf_op jit(solution)/shard_map/ppermute | solution.py:55
  263.7 20.6 %collective-permute-start.44 = (bf16[128,1536]{1,0:T(8,128)(2,1)S(1)}, bf16[128,1536]{1,0:T(8,128)(2,1)}, u32[]{:S(2)}, u32[]{:S(2)}) collective-permute-start(bf16[128,1536]{1,0:T(8,128)(2,1)S(1)} %pad_maximum_fusion.9), channel_id=1, source_target_pairs={{0,6},{2,4},{4,2},{6,0},{1,7},{3,5},{5,3},{7,1},{8,14},{10,12},{12... | collective-permute-start | bytes 1179656 | tf_op jit(solution)/shard_map/ppermute | solution.py:55
  284.3 22.2 %collective-permute-start.45 = (bf16[2,512,256]{2,1,0:T(8,128)(2,1)}, bf16[2,512,256]{2,1,0:T(8,128)(2,1)S(1)}, u32[]{:S(2)}, u32[]{:S(2)}) collective-permute-start(bf16[2,512,256]{2,1,0:T(8,128)(2,1)} %get-tuple-element.261), channel_id=1, source_target_pairs={{0,8},{8,0},{16,24},{24,16},{1,9},{9,1},{17,25},{25,17},{2,10},{10... | collective-permute-start | bytes 1572872 | tf_op jit(solution)/shard_map/ppermute | solution.py:55
  284.6 26.4 %collective-permute-start.46 = (bf16[2,512,256]{2,1,0:T(8,128)(2,1)}, bf16[2,512,256]{2,1,0:T(8,128)(2,1)S(1)}, u32[]{:S(2)}, u32[]{:S(2)}) collective-permute-start(bf16[2,512,256]{2,1,0:T(8,128)(2,1)} %get-tuple-element.262), channel_id=1, source_target_pairs={{0,16},{8,24},{16,0},{24,8},{1,17},{9,25},{17,1},{25,9},{2,18},{10... | collective-permute-start | bytes 1572872 | tf_op jit(solution)/shard_map/ppermute | solution.py:55
  286.2 29.3 %collective-permute-start.47 = (bf16[2,512,256]{2,1,0:T(8,128)(2,1)}, bf16[2,512,256]{2,1,0:T(8,128)(2,1)S(1)}, u32[]{:S(2)}, u32[]{:S(2)}) collective-permute-start(bf16[2,512,256]{2,1,0:T(8,128)(2,1)} %get-tuple-element.263), channel_id=1, source_target_pairs={{0,24},{8,16},{16,8},{24,0},{1,25},{9,17},{17,9},{25,1},{2,26},{10... | collective-permute-start | bytes 1572872 | tf_op jit(solution)/shard_map/ppermute | solution.py:55
  306.5 18.8 %collective-permute-start.50 = (bf16[128,1536]{1,0:T(8,128)(2,1)}, bf16[128,1536]{1,0:T(8,128)(2,1)S(1)}, u32[]{:S(2)}, u32[]{:S(2)}) collective-permute-start(bf16[128,1536]{1,0:T(8,128)(2,1)} %pad_maximum_fusion.8), channel_id=1, source_target_pairs={{0,4},{2,6},{4,0},{6,2},{1,5},{3,7},{5,1},{7,3},{8,12},{10,14},{12... | collective-permute-start | bytes 1179656 | tf_op jit(solution)/shard_map/ppermute | solution.py:55
  326.3 20.4 %collective-permute-start.55 = (bf16[1,2,3,192,384]{4,3,2,1,0:T(8,128)(2,1)S(1)}, bf16[1,2,3,192,384]{4,3,2,1,0:T(8,128)(2,1)S(1)}, u32[]{:S(2)}, u32[]{:S(2)}) collective-permute-start(bf16[1,2,3,192,384]{4,3,2,1,0:T(8,128)(2,1)S(1)} %add_convert_fusion.4), channel_id=1, source_target_pairs={{0,8},{8,0},{16,24},{24,16},{1,9},{9,1},{17,25},{25,17},{2,10},{10... | collective-permute-start | bytes 2654216 | tf_op jit(solution)/shard_map/ppermute | solution.py:55
  328.4 20.1 %collective-permute-start.56 = (bf16[1,2,3,192,384]{4,3,2,1,0:T(8,128)(2,1)S(1)}, bf16[1,2,3,192,384]{4,3,2,1,0:T(8,128)(2,1)S(1)}, u32[]{:S(2)}, u32[]{:S(2)}) collective-permute-start(bf16[1,2,3,192,384]{4,3,2,1,0:T(8,128)(2,1)S(1)} %add_convert_fusion.1), channel_id=1, source_target_pairs={{0,16},{8,24},{16,0},{24,8},{1,17},{9,25},{17,1},{25,9},{2,18},{10... | collective-permute-start | bytes 2654216 | tf_op jit(solution)/shard_map/ppermute | solution.py:55
  330.6 19.7 %collective-permute-start.52 = (bf16[2,128,256]{2,1,0:T(8,128)(2,1)}, bf16[2,128,256]{2,1,0:T(8,128)(2,1)S(1)}, u32[]{:S(2)}, u32[]{:S(2)}) collective-permute-start(bf16[2,128,256]{2,1,0:T(8,128)(2,1)} %get-tuple-element.399), channel_id=1, source_target_pairs={{0,2},{2,0},{4,6},{6,4},{1,3},{3,1},{5,7},{7,5},{8,10},{10,8},{12,... | collective-permute-start | bytes 393224 | tf_op jit(solution)/shard_map/ppermute | solution.py:55
  330.6 19.7 %collective-permute-start.53 = (bf16[2,128,256]{2,1,0:T(8,128)(2,1)}, bf16[2,128,256]{2,1,0:T(8,128)(2,1)S(1)}, u32[]{:S(2)}, u32[]{:S(2)}) collective-permute-start(bf16[2,128,256]{2,1,0:T(8,128)(2,1)} %get-tuple-element.398), channel_id=1, source_target_pairs={{0,4},{2,6},{4,0},{6,2},{1,5},{3,7},{5,1},{7,3},{8,12},{10,14},{12... | collective-permute-start | bytes 393224 | tf_op jit(solution)/shard_map/ppermute | solution.py:55
  332.6 17.7 %collective-permute-start.54 = (bf16[2,128,256]{2,1,0:T(8,128)(2,1)}, bf16[2,128,256]{2,1,0:T(8,128)(2,1)S(1)}, u32[]{:S(2)}, u32[]{:S(2)}) collective-permute-start(bf16[2,128,256]{2,1,0:T(8,128)(2,1)} %get-tuple-element.397), channel_id=1, source_target_pairs={{0,6},{2,4},{4,2},{6,0},{1,7},{3,5},{5,3},{7,1},{8,14},{10,12},{12... | collective-permute-start | bytes 393224 | tf_op jit(solution)/shard_map/ppermute | solution.py:55
  369.2 32.6 %collective-permute-start.61 = (bf16[2,384,896]{2,1,0:T(8,128)(2,1)}, bf16[2,384,896]{2,1,0:T(8,128)(2,1)}, u32[]{:S(2)}, u32[]{:S(2)}) collective-permute-start(bf16[2,384,896]{2,1,0:T(8,128)(2,1)} %get-tuple-element.297), channel_id=1, source_target_pairs={{0,8},{8,0},{16,24},{24,16},{1,9},{9,1},{17,25},{25,17},{2,10},{10... | collective-permute-start | bytes 4128776 | tf_op jit(solution)/shard_map/ppermute | solution.py:55
  369.7 37.3 %collective-permute-start.59 = (bf16[2,384,1024]{2,1,0:T(8,128)(2,1)}, bf16[2,384,1024]{2,1,0:T(8,128)(2,1)S(1)}, u32[]{:S(2)}, u32[]{:S(2)}) collective-permute-start(bf16[2,384,1024]{2,1,0:T(8,128)(2,1)} %get-tuple-element.295), channel_id=1, source_target_pairs={{0,16},{8,24},{16,0},{24,8},{1,17},{9,25},{17,1},{25,9},{2,18},{10... | collective-permute-start | bytes 4718600 | tf_op jit(solution)/shard_map/ppermute | solution.py:55
  372.7 36.4 %collective-permute-start.51 = (bf16[128,1536]{1,0:T(8,128)(2,1)S(1)}, bf16[128,1536]{1,0:T(8,128)(2,1)S(1)}, u32[]{:S(2)}, u32[]{:S(2)}) collective-permute-start(bf16[128,1536]{1,0:T(8,128)(2,1)S(1)} %add_convert_fusion.13), channel_id=1, source_target_pairs={{0,1},{1,0},{2,3},{3,2},{4,5},{5,4},{6,7},{7,6},{8,9},{9,8},{10,11... | collective-permute-start | bytes 1179656 | tf_op jit(solution)/shard_map/ppermute | solution.py:55
  403.1 17.8 %collective-permute-start.62 = (bf16[1,384,896]{2,1,0:T(8,128)(2,1)S(1)}, bf16[1,384,896]{2,1,0:T(8,128)(2,1)S(1)}, u32[]{:S(2)}, u32[]{:S(2)}) collective-permute-start(bf16[1,384,896]{2,1,0:T(8,128)(2,1)S(1)} %add_convert_fusion.10), channel_id=1, source_target_pairs={{0,16},{8,24},{16,0},{24,8},{1,17},{9,25},{17,1},{25,9},{2,18},{10... | collective-permute-start | bytes 2064392 | tf_op jit(solution)/shard_map/ppermute | solution.py:55
  407.3 17.7 %collective-permute-start.60 = (bf16[1,384,1024]{2,1,0:T(8,128)(2,1)S(1)}, bf16[1,384,1024]{2,1,0:T(8,128)(2,1)S(1)}, u32[]{:S(2)}, u32[]{:S(2)}) collective-permute-start(bf16[1,384,1024]{2,1,0:T(8,128)(2,1)S(1)} %add_convert_fusion.7), channel_id=1, source_target_pairs={{0,8},{8,0},{16,24},{24,16},{1,9},{9,1},{17,25},{25,17},{2,10},{10... | collective-permute-start | bytes 2359304 | tf_op jit(solution)/shard_map/ppermute | solution.py:55
  409.2 66.6 %collective-permute-start.58 = (f32[128,1536]{1,0:T(8,128)S(1)}, f32[128,1536]{1,0:T(8,128)S(1)}, u32[]{:S(2)}, u32[]{:S(2)}) collective-permute-start(f32[128,1536]{1,0:T(8,128)S(1)} %copy-done.15), channel_id=1, source_target_pairs={{0,1},{1,0},{2,3},{3,2},{4,5},{5,4},{6,7},{7,6},{8,9},{9,8},{10,11... | collective-permute-start | bytes 2359304 | tf_op jit(solution)/shard_map/ppermute | solution.py:55
  425.6 31.8 %collective-permute-start.63 = (bf16[96,1920]{1,0:T(8,128)(2,1)S(1)}, bf16[96,1920]{1,0:T(8,128)(2,1)S(1)}, u32[]{:S(2)}, u32[]{:S(2)}) collective-permute-start(bf16[96,1920]{1,0:T(8,128)(2,1)S(1)} %get-tuple-element.384), channel_id=1, source_target_pairs={{0,2},{2,0},{4,6},{6,4},{1,3},{3,1},{5,7},{7,5},{8,10},{10,8},{12,... | collective-permute-start | bytes 1105928 | tf_op jit(solution)/shard_map/ppermute | solution.py:55
  425.6 42.4 %collective-permute-start.64 = (bf16[96,1920]{1,0:T(8,128)(2,1)S(1)}, bf16[96,1920]{1,0:T(8,128)(2,1)S(1)}, u32[]{:S(2)}, u32[]{:S(2)}) collective-permute-start(bf16[96,1920]{1,0:T(8,128)(2,1)S(1)} %get-tuple-element.385), channel_id=1, source_target_pairs={{0,4},{2,6},{4,0},{6,2},{1,5},{3,7},{5,1},{7,3},{8,12},{10,14},{12... | collective-permute-start | bytes 1105928 | tf_op jit(solution)/shard_map/ppermute | solution.py:55
  428.4 47.2 %collective-permute-start.65 = (bf16[96,1920]{1,0:T(8,128)(2,1)S(1)}, bf16[96,1920]{1,0:T(8,128)(2,1)S(1)}, u32[]{:S(2)}, u32[]{:S(2)}) collective-permute-start(bf16[96,1920]{1,0:T(8,128)(2,1)S(1)} %get-tuple-element.386), channel_id=1, source_target_pairs={{0,6},{2,4},{4,2},{6,0},{1,7},{3,5},{5,3},{7,1},{8,14},{10,12},{12... | collective-permute-start | bytes 1105928 | tf_op jit(solution)/shard_map/ppermute | solution.py:55
  477.0 36.0 %collective-permute-start.67 = (bf16[96,1920]{1,0:T(8,128)(2,1)S(1)}, bf16[96,1920]{1,0:T(8,128)(2,1)S(1)}, u32[]{:S(2)}, u32[]{:S(2)}) collective-permute-start(bf16[96,1920]{1,0:T(8,128)(2,1)S(1)} %pad_maximum_fusion.10), channel_id=1, source_target_pairs={{0,6},{2,4},{4,2},{6,0},{1,7},{3,5},{5,3},{7,1},{8,14},{10,12},{12... | collective-permute-start | bytes 1105928 | tf_op jit(solution)/shard_map/ppermute | solution.py:55
  478.8 60.4 %collective-permute-start.68 = (bf16[96,1920]{1,0:T(8,128)(2,1)S(1)}, bf16[96,1920]{1,0:T(8,128)(2,1)S(1)}, u32[]{:S(2)}, u32[]{:S(2)}) collective-permute-start(bf16[96,1920]{1,0:T(8,128)(2,1)S(1)} %pad_maximum_fusion.10), channel_id=1, source_target_pairs={{0,4},{2,6},{4,0},{6,2},{1,5},{3,7},{5,1},{7,3},{8,12},{10,14},{12... | collective-permute-start | bytes 1105928 | tf_op jit(solution)/shard_map/ppermute | solution.py:55
  511.5 27.8 %collective-permute-start.69 = (bf16[96,1920]{1,0:T(8,128)(2,1)S(1)}, bf16[96,1920]{1,0:T(8,128)(2,1)S(1)}, u32[]{:S(2)}, u32[]{:S(2)}) collective-permute-start(bf16[96,1920]{1,0:T(8,128)(2,1)S(1)} %pad_maximum_fusion.10), channel_id=1, source_target_pairs={{0,2},{2,0},{4,6},{6,4},{1,3},{3,1},{5,7},{7,5},{8,10},{10,8},{12,... | collective-permute-start | bytes 1105928 | tf_op jit(solution)/shard_map/ppermute | solution.py:55
  (54 other events, 498.7 us)
Sparse Core Ops, SparseCore 0:
  350.5 176.3 all-gather.2

commit v3 on v2

--- a/solution.py
+++ b/solution.py
@@ -12,7 +12,7 @@
 NEG_FILL = -1e30
 KEY_STEP = 256
 MOE_ROWS = 512
-SLICES = 2
+SLICES = 1
 VMEM_BYTES = 60 * 2**20
 
 f32 = jnp.float32
@@ -74,8 +74,22 @@
     ]
 
 
+def gather_first_halves(own, axis, size):
+    rows = own.shape[0] // 2
+    halves = (own[:rows], own[rows:])
+    return [
+        halves
+        if j == 0
+        else tuple(swap(half, axis, size, j) for half in halves)
+        if low_bit(j) == high_bit(j)
+        else None
+        for j in range(size)
+    ]
+
+
 def gather_rest(got, axis, size, dim=0, ties=()):
-    rows, got = got[0].shape[dim], list(got)
+    got = list(got)
+    rows = 2 * got[0][0].shape[dim] if isinstance(got[0], tuple) else got[0].shape[dim]
 
     def half(j, top):
         if isinstance(got[j], tuple):
@@ -134,16 +148,6 @@
 
 def exchange_direct(blocks, axis, size):
     return [blocks[0]] + [swap(blocks[j], axis, size, j) for j in range(1, size)]
-
-
-def ordered(blocks, index):
-    count = len(blocks)
-    bit = 1
-    while bit < count:
-        flag = (index & bit) != 0
-        blocks = [jnp.where(flag, blocks[i ^ bit], blocks[i]) for i in range(count)]
-        bit *= 2
-    return blocks
 
 
 def axis_relative(value, dim, index):
@@ -366,8 +370,16 @@
     def body(place_ref, router_ref, *rest):
         b_refs, cx_refs = rest[: len(b)], rest[len(b) : 2 * len(b)]
         w_refs, rest = rest[2 * len(b) : 2 * len(b) + w_count], rest[2 * len(b) + w_count :]
-        out_refs, back_refs, (scaled_ref, gate_ref, up_ref) = rest[:2], rest[2:4], rest[4:7]
-        b_all, cx_all, w_all, b_sems, cx_sems, w_sems = rest[7:]
+        out_refs, back_refs, side_refs = rest[:2], rest[2:4], rest[4:7]
+        b_all, cx_all, w_all, out_low, back_low, sides, b_sems, cx_sems, w_sems, o_sems = rest[7:]
+        scaled_ref, gate_ref, up_ref = (sides.at[n] for n in range(3))
+        o_copies = []
+
+        def send(source, target):
+            copy = pltpu.make_async_copy(source, target, o_sems.at[len(o_copies)])
+            copy.start()
+            o_copies.append(copy)
+
         row_copies = fetch(
             [b_refs[n % len(b)].at[pl.ds(row, block), :] for n, row in enumerate(at)],
             [b_all.at[pl.ds(n * block, block), :] for n in range(pieces)],
@@ -429,18 +441,21 @@
                     jnp.sum(product[:, e * hidden : (e + 1) * hidden], -1, keepdims=True),
                     0.0,
                 )
-            out = mm(scaled_ref[span, :], w_all[2], NT).astype(bf16)
-            back = (
+            for n in range(3):
+                send(sides.at[n, pl.ds(start, rows), :], side_refs[n].at[pl.ds(start, rows), :])
+            out_low[span, :] = mm(scaled_ref[span, :], w_all[2], NT).astype(bf16)
+            back_low[span, :width] = (
                 mm(gate_ref[span, :], w_all[0], NT) + mm(up_ref[span, :], w_all[1], NT)
             ).astype(bf16)
-            share = share.astype(bf16)
+            back_low[span, width:] = share.astype(bf16)
             for n in range(2):
                 low, high = max(start, n * half_rows), min(start + rows, (n + 1) * half_rows)
                 if low < high:
-                    to = slice(low - n * half_rows, high - n * half_rows)
-                    out_refs[n][to, :] = out[low - start : high - start]
-                    back_refs[n][to, :width] = back[low - start : high - start]
-                    back_refs[n][to, width:] = share[low - start : high - start]
+                    to = pl.ds(low - n * half_rows, high - low)
+                    send(out_low.at[pl.ds(low, high - low), :], out_refs[n].at[to, :])
+                    send(back_low.at[pl.ds(low, high - low), :], back_refs[n].at[to, :])
+        for copy in o_copies:
+            copy.wait()
 
     return pl.pallas_call(
         body,
@@ -451,14 +466,18 @@
             *[shape((total, wide), bf16)] * 3,
         ),
         in_specs=scalars() + vmem(1) + anywhere(2 * len(b) + w_count),
-        out_specs=tuple(vmem(7)),
+        out_specs=tuple(anywhere(7)),
         scratch_shapes=[
             pltpu.VMEM((total, width), bf16),
             pltpu.VMEM((total, width + LANES), bf16),
             pltpu.VMEM((3, width, wide), bf16),
+            pltpu.VMEM((total, width), bf16),
+            pltpu.VMEM((total, width + LANES), bf16),
+            pltpu.VMEM((3, total, wide), bf16),
             pltpu.SemaphoreType.DMA((pieces,)),
             pltpu.SemaphoreType.DMA((pieces,)),
             pltpu.SemaphoreType.DMA((local * w_count,)),
+            pltpu.SemaphoreType.DMA((7 * total // rows,)),
         ],
         compiler_params=params(),
         cost_estimate=cost(12 * total * width * wide, 2 * (4 * total * width + 3 * width * wide)),
@@ -791,6 +810,41 @@
     )(gathered)
 
 
+def assemble_attention(place, blocks, wide, out_wide):
+    count = len(blocks)
+    step, total = blocks[0].shape
+    depth = count * step
+    tail = total - wide - 2 * HEAD - out_wide
+
+    def body(place_ref, *refs):
+        q_ref, k_ref, v_ref, out_ref, small_ref, whole = refs[count:]
+        for n in range(count):
+            row = pl.multiple_of(lax.bitwise_xor(place_ref[1], n) * step, 8)
+            whole[pl.ds(row, step), :] = refs[n][...].astype(f32)
+        q_ref[...] = whole[:, :wide]
+        k_ref[...] = whole[:, wide : wide + HEAD]
+        v_ref[...] = whole[:, wide + HEAD : wide + 2 * HEAD]
+        out_ref[...] = whole[:, wide + 2 * HEAD : wide + 2 * HEAD + out_wide].T
+        small_ref[...] = whole[:, wide + 2 * HEAD + out_wide :]
+
+    return pl.pallas_call(
+        body,
+        name="assemble_attention",
+        out_shape=(
+            shape((depth, wide), f32),
+            shape((depth, HEAD), f32),
+            shape((depth, HEAD), f32),
+            shape((out_wide, depth), f32),
+            shape((depth, tail), f32),
+        ),
+        in_specs=scalars() + vmem(count),
+        out_specs=tuple(vmem(5)),
+        scratch_shapes=[pltpu.VMEM((depth, total), f32)],
+        compiler_params=params(),
+        cost_estimate=cost(depth * total, 6 * depth * total),
+    )(place, *blocks)
+
+
 def attention_grads(a, go, dq, dkv, o, b, dl, dgain_one, dgain_two, experts, parts):
     rows, width = a.shape
     depth = width // parts
@@ -916,7 +970,7 @@
 
         hold = lax.optimization_barrier
         far = C // 2
-        in_first = gather_first(in_own, "fsdp", F)
+        in_first = gather_first_halves(in_own, "fsdp", F)
         in_first, mask, cosine, sine, seen, x = hold((in_first, mask, cosine, sine, seen, x))
         in_pieces = gather_rest(in_first, "fsdp", F)
         in_pieces, (out_own, cx_mine, expert_own) = held_pieces(
@@ -977,20 +1031,25 @@
             sums = to_sums(back_mine, back_other)
             back_sums.append(exchange_direct(sums, "ctx", C))
         b_at = [n * part for n in range(SLICES) for _ in b_both]
+
+        def first_round(pieces):
+            return [scatter_first(pieces[2 * n + 1], "fsdp", F, n == 0) for n in range(2)]
+
+        def other_rounds(pieces, got):
+            return [scatter_rest(pieces[2 * n], got[n], "fsdp", F, n == 0) for n in range(2)]
+
         sides, _, outs = hold((sides, sums, outs))
         grads = experts_grads(b_both, cx_both, b_at, part, sides, local_experts, F)
+        near = [k for k in range(C) if k != far]
+        grads, back_near = hold((grads, [back_sums[0][k] for k in near]))
+        for k, block in zip(near, back_near):
+            back_sums[0][k] = block
+        grads_got = first_round(grads)
         out_sums = [
             jnp.concatenate(pieces, 0) for pieces in zip(*[to_sums(*pair) for pair in outs])
         ]
-        back_sums, grads, out_sums = hold((back_sums, grads, out_sums))
-
-        def first_round(pieces):
-            return [scatter_first(pieces[2 * n + 1], "fsdp", F, n == 0) for n in range(2)]
-
-        def other_rounds(pieces, got):
-            return [scatter_rest(pieces[2 * n], got[n], "fsdp", F, n == 0) for n in range(2)]
-
-        grads_got = first_round(grads)
+        back_sums, out_sums = hold((back_sums, out_sums))
+        out_far = out_sums[far]
         for k in range(1, C):
             if k != far:
                 out_sums[k] = swap(out_sums[k], "ctx", C, k)
@@ -1000,19 +1059,20 @@
         go_all, dq, *dkv = attend_back(
             place, seen, go, core(go), q, o, lse, mask, cosine, sine, wo_all, kv, F
         )
-        go_all, dq, dkv, out_sums = hold((go_all, dq, dkv, out_sums))
+        go_all, dq, dkv, out_sums, out_far, grads_got = hold(
+            (go_all, dq, dkv, out_sums, out_far, grads_got)
+        )
+        grad_own = jnp.stack(other_rounds(grads, grads_got))
+        out_sums[far] = swap(out_far, "ctx", C, far)
+        dkv, grad_own, out_sums = hold((dkv, grad_own, out_sums))
         go_flat, o_flat = go_all.reshape(micro * rows, width), o.reshape(micro * rows, -1)
 
         dkv = exchange_direct(dkv, "fsdp", F)
-        out_sums[far] = swap(out_sums[far], "ctx", C, far)
         total = dkv[0].astype(f32)
         for piece in dkv[1:]:
             total = total + piece.astype(f32)
         total = total.astype(bf16).reshape(micro, C, rows, 2 * HEAD)
-        total, grads_got, out_sums = hold((total, grads_got, out_sums))
-        grad_own = other_rounds(grads, grads_got)
         dkv = exchange_direct([total[:, k] for k in range(C)], "ctx", C)
-        dkv, grad_own = hold((dkv, jnp.stack(grad_own)))
         gathered = lax.all_gather(grad_own, "ctx", axis=0)
         dkv, da = project_back(dkv, dq, cosine, sine, in_all)
         input_grad, dgain_one = first_norm_back(
@@ -1037,9 +1097,10 @@
         total = jnp.concatenate([total[:, : wide + 2 * HEAD + o_flat.shape[1]], add_low(tail, core(tail))], 1)
         got = exchange_direct([total] * C, "ctx", C)
         grad_gate, grad_up, grad_down = assemble(gathered)
-        grad_all = jnp.concatenate(ordered(got, c), 0).astype(f32)
-        grad_q, grad_k, grad_v = jnp.split(grad_all[:, : wide + 2 * HEAD], (wide, wide + HEAD), 1)
-        grad_out, grad_small = jnp.split(grad_all[:, wide + 2 * HEAD :], (o_flat.shape[1],), 1)
+        got, grad_gate, grad_up, grad_down = hold((got, grad_gate, grad_up, grad_down))
+        grad_q, grad_k, grad_v, grad_out, grad_small = assemble_attention(
+            place, got, wide, o_flat.shape[1]
+        )
         result = sum((piece.astype(f32) for piece in out_sums), middle).astype(bf16)
 
         def whole(mine_value):
@@ -1054,7 +1115,7 @@
             grad_q,
             grad_k,
             grad_v,
-            grad_out.T,
+            grad_out,
             grad_small[:, experts + 1],
             grad_small[:, :experts],
             grad_gate,

time: 570 us -> 523 us (0.918)
  the two profiles are of different devices: /device:TPU:0 before, /device:TPU:8 now
where the time goes in v3:
time: 523 us; the launch traced here: 515 us
  waiting for transfers between devices  267 us (51%)
  Pallas kernels  97 us (19%)
  starting transfers between devices  76 us (15%)
  other arithmetic  35.2 us (7%)
  local copies, waits for them, and re-layouts  25.4 us (5%)
  between operations  15 us (3%)
    ppermute x67, waiting for transfers between devices, swap(): return lax.ppermute(value, axis, [(i, i ^ bit) for i in range(size)])  267 us
    ppermute x67, starting transfers between devices, swap(): return lax.ppermute(value, axis, [(i, i ^ bit) for i in range(size)])  75.9 us
    pallas_call x1, Pallas kernels, experts_rows(): pl.pallas_call(body, name='experts_rows', out_shape=(*[shape((half_rows,...  25.3 us
    pallas_call x1, Pallas kernels, experts_grads(): pl.pallas_call(body, name='experts_grads', out_shape=tuple([shape((half,...  13.3 us
    convert_element_type x11, other arithmetic, add_low(): return (left.astype(f32) + right.astype(f32)).astype(bf16)  12.2 us
    unnamed x106, local copies, waits for them, and re-layouts  10.7 us
  transfers between devices with their start and end apart: 68, of which 41 were waited for; matrix products, arithmetic and copies ran while one was open for 8% of the time, Pallas kernels for 13%

profile of v3, /device:TPU:8, one launch (start us, length us, event | category | flops | bytes accessed | tf_op | source)
XLA Modules:
  0.0 515.4 jit_solution(13177536257393691945)
XLA Ops:
  27.3 2.0 constant_dynamic-slice_fusion.6
  30.2 2.1 pad_maximum_fusion.3.x_ref
  32.2 3.4 select_convert_fusion.mask_ref
  42.3 4.5 collective-permute-done.4.rest_6_
  48.6 2.4 collective-permute-start.11
  51.6 5.7 %project_in.1 = (bf16[256,1536]{1,0:T(8,128)(2,1)}, bf16[2,768,128]{2,1,0:T(8,128)(2,1)}, bf16[2,128,256]{2,1,0:T(8,128)(2,1)}, bf16[1536,1152]{1,0:T(8,128)(2,1...) custom-call(bf16[256,1536]{1,0:T(8,128)(2,1)} %bitcast.84, f32[256,128]{1,0:T(8,128)} %pad_maximum_fusion.7.cos_ref.refs_5_, ...), custom_call_target="tpu_custom_call" | custom-call | flops 805306368 | bytes 6291456 | tf_op jit(solution)/shard_map/project_in/pallas_call | solution.py:226
  57.8 2.6 collective-permute-start.7
  60.4 2.1 collective-permute-done.6
  62.5 1.9 collective-permute-start.8
  64.5 2.0 collective-permute-done.7
  66.5 3.3 collective-permute-done.8
  70.7 2.8 collective-permute-done.10.rest_6_
  78.8 2.7 collective-permute-start.16
  81.5 9.9 %collective-permute-done.15.rest_9_.refs_9_ = bf16[128,1664]{1,0:T(8,128)(2,1)} collective-permute-done((bf16[128,1664]{1,0:T(8,128)(2,1)}, bf16[128,1664]{1,0:T(8,128)(2,1)}, u32[]{:S(2)}, u32[]{:S(2)}) %collective-permute-start.15) | collective-permute-done | bytes 426016 | tf_op jit(solution)/shard_map/ppermute | solution.py:55
  91.4 6.0 %collective-permute-done.16.rest_11_.refs_11_ = bf16[128,1664]{1,0:T(8,128)(2,1)} collective-permute-done((bf16[128,1664]{1,0:T(8,128)(2,1)}, bf16[128,1664]{1,0:T(8,128)(2,1)}, u32[]{:S(2)}, u32[]{:S(2)}) %collective-permute-start.16) | collective-permute-done | bytes 426016 | tf_op jit(solution)/shard_map/ppermute | solution.py:55
  97.4 2.2 collective-permute-done.13.rest_2_
  99.8 2.4 collective-permute-start.26
  102.2 2.6 collective-permute-start.18
  104.8 8.0 %attend.1 = (bf16[2,128,1536]{2,1,0:T(8,128)(2,1)}, bf16[2,128,768]{2,1,0:T(8,128)(2,1)}, f32[2,1,768]{2,1,0:T(1,128)}, bf16[1536,768]{1,0:T(8,128)(2,1)}) custom-call(s32[16]{0:T(128)} %reshape.190.seen_ref, bf16[2,768,128]{2,1,0:T(8,128)(2,1)} %get-tuple-element.178.q_ref, bf16[2,2048,128]{2,1,0:T(8,128)(2,1)} %select_convert_fusion.mask_ref, ...), custom_call_target="tpu_custom_call" | custom-call | flops 2214592512 | bytes 6815744 | tf_op jit(solution)/shard_map/attend/pallas_call | solution.py:302
  115.9 1.9 collective-permute-done.18.rest_10_.refs_10_
  118.4 2.7 second_norm.1
  122.6 2.1 collective-permute-start.23
  125.2 10.2 %collective-permute-done.25.rest_17_ = bf16[2,3,384,384]{3,2,1,0:T(8,128)(2,1)S(1)} collective-permute-done((bf16[2,3,384,384]{3,2,1,0:T(8,128)(2,1)S(1)}, bf16[2,3,384,384]{3,2,1,0:T(8,128)(2,1)S(1)}, u32[]{:S(2)}, u32[]{:S(2)}) %collective-permute-start.25) | collective-permute-done | bytes 1769504 | tf_op jit(solution)/shard_map/ppermute | solution.py:55
  136.4 4.0 collective-permute-done.26.rest_18_
  141.8 9.5 %collective-permute-done.23.rest_2_.refs_2_ = bf16[128,1536]{1,0:T(8,128)(2,1)S(1)} collective-permute-done((bf16[128,1536]{1,0:T(8,128)(2,1)}, bf16[128,1536]{1,0:T(8,128)(2,1)S(1)}, u32[]{:S(2)}, u32[]{:S(2)}) %collective-permute-start.23) | collective-permute-done | bytes 393248 | tf_op jit(solution)/shard_map/ppermute | solution.py:55
  151.4 8.9 %collective-permute-done.24.rest_3_.refs_3_ = bf16[128,1536]{1,0:T(8,128)(2,1)S(1)} collective-permute-done((bf16[128,1536]{1,0:T(8,128)(2,1)}, bf16[128,1536]{1,0:T(8,128)(2,1)S(1)}, u32[]{:S(2)}, u32[]{:S(2)}) %collective-permute-start.24) | collective-permute-done | bytes 393248 | tf_op jit(solution)/shard_map/ppermute | solution.py:55
  166.7 25.3 %experts_rows.1 = (bf16[512,1536]{1,0:T(8,128)(2,1)}, bf16[512,1536]{1,0:T(8,128)(2,1)}, bf16[512,1664]{1,0:T(8,128)(2,1)}, bf16[512,1664]{1,0:T(8,128)(2,1)}, b...) custom-call(s32[3]{0:T(128)} %pad_add_fusion.place_ref, ...), custom_call_target="tpu_custom_call" | custom-call | flops 14495514624 | bytes 19660800 | tf_op jit(solution)/shard_map/experts_rows/pallas_call | solution.py:460
  192.2 3.7 collective-permute-done.34
  195.9 2.7 add_convert_fusion.13
  200.2 13.3 %experts_grads.1 = (bf16[2,2,3,192,384]{4,3,2,1,0:T(8,128)(2,1)}, bf16[2,2,3,192,384]{4,3,2,1,0:T(8,128)(2,1)}, bf16[2,2,3,192,384]{4,3,2,1,0:T(8,128)(2,1)}, bf16[2,2,3,192,384]{4,3,2,1,0:T(8,128)(2,1)}) custom-call(bf16[128,1536]{1,0:T(8,128)(2,1)} %get-tuple-element.206.rest_0_.refs_0_.refs_5_.b_ref, bf16[128,1536]{1,0:T(8,128)(2,1)} %copy-done.41, ...), custom_call_target="tpu_custom_call" | custom-call | flops 7247757312 | bytes 18087936 | tf_op jit(solution)/shard_map/experts_grads/pallas_call | solution.py:552
  215.3 8.8 %collective-permute-start.37 = (bf16[128,1664]{1,0:T(8,128)(2,1)}, bf16[128,1664]{1,0:T(8,128)(2,1)}, u32[]{:S(2)}, u32[]{:S(2)}) collective-permute-start(bf16[128,1664]{1,0:T(8,128)(2,1)} %get-tuple-element.361), channel_id=1, source_target_pairs={{0,4},{2,6},{4,0},{6,2},{1,5},{3,7},{5,1},{7,3},{8,12},{10,14},{12... | collective-permute-start | bytes 1277960 | tf_op jit(solution)/shard_map/ppermute | solution.py:55
  224.1 2.6 add_convert_fusion.18
  226.8 14.8 %collective-permute-done.37.refs_2_ = bf16[128,1664]{1,0:T(8,128)(2,1)} collective-permute-done((bf16[128,1664]{1,0:T(8,128)(2,1)}, bf16[128,1664]{1,0:T(8,128)(2,1)}, u32[]{:S(2)}, u32[]{:S(2)}) %collective-permute-start.37) | collective-permute-done | bytes 426016 | tf_op jit(solution)/shard_map/ppermute | solution.py:55
  241.6 4.3 second_norm_back.1
  245.9 2.5 collective-permute-start.40
  250.7 9.8 %attend_back.1 = (bf16[2,128,1536]{2,1,0:T(8,128)(2,1)}, bf16[256,768]{1,0:T(8,128)(2,1)}, bf16[2,512,256]{2,1,0:T(8,128)(2,1)}, bf16[2,512,256]{2,1,0:T(8,128)(...) custom-call(s32[3]{0:T(128)} %pad_add_fusion.place_ref, s32[16]{0:T(128)} %reshape.190.seen_ref, ...), custom_call_target="tpu_custom_call" | custom-call | flops 4026531840 | bytes 6553600 | tf_op jit(solution)/shard_map/attend_back/pallas_call | solution.py:695
  260.5 7.8 %collective-permute-done.41 = bf16[128,1536]{1,0:T(8,128)(2,1)} collective-permute-done((bf16[128,1536]{1,0:T(8,128)(2,1)}, bf16[128,1536]{1,0:T(8,128)(2,1)}, u32[]{:S(2)}, u32[]{:S(2)}) %collective-permute-start.41) | collective-permute-done | bytes 393248 | tf_op jit(solution)/shard_map/ppermute | solution.py:55
  271.5 1.8 collective-permute-start.45
  274.5 15.0 %collective-permute-done.44 = bf16[1,2,3,192,384]{4,3,2,1,0:T(8,128)(2,1)S(1)} collective-permute-done((bf16[1,2,3,192,384]{4,3,2,1,0:T(8,128)(2,1)S(1)}, bf16[1,2,3,192,384]{4,3,2,1,0:T(8,128)(2,1)S(1)}, u32[]{:S(2)}, u32[]{:S(2)}) %collective-permute-start.44) | collective-permute-done | bytes 884768 | tf_op jit(solution)/shard_map/ppermute | solution.py:55
  294.5 1.7 collective-permute-start.49
  296.9 11.0 %collective-permute-done.48 = bf16[2,512,256]{2,1,0:T(8,128)(2,1)S(1)} collective-permute-done((bf16[2,512,256]{2,1,0:T(8,128)(2,1)S(1)}, bf16[2,512,256]{2,1,0:T(8,128)(2,1)S(1)}, u32[]{:S(2)}, u32[]{:S(2)}) %collective-permute-start.48) | collective-permute-done | bytes 524320 | tf_op jit(solution)/shard_map/ppermute | solution.py:55
  307.9 7.9 %collective-permute-done.49 = bf16[2,512,256]{2,1,0:T(8,128)(2,1)S(1)} collective-permute-done((bf16[2,512,256]{2,1,0:T(8,128)(2,1)S(1)}, bf16[2,512,256]{2,1,0:T(8,128)(2,1)S(1)}, u32[]{:S(2)}, u32[]{:S(2)}) %collective-permute-start.49) | collective-permute-done | bytes 524320 | tf_op jit(solution)/shard_map/ppermute | solution.py:55
  317.5 4.4 collective-permute-start.51
  323.4 10.4 %collective-permute-done.51.refs_1_ = bf16[2,128,256]{2,1,0:T(8,128)(2,1)S(1)} collective-permute-done((bf16[2,128,256]{2,1,0:T(8,128)(2,1)S(1)}, bf16[2,128,256]{2,1,0:T(8,128)(2,1)S(1)}, u32[]{:S(2)}, u32[]{:S(2)}) %collective-permute-start.51) | collective-permute-done | bytes 131104 | tf_op jit(solution)/shard_map/ppermute | solution.py:55
  333.8 6.0 %collective-permute-done.52.refs_2_ = bf16[2,128,256]{2,1,0:T(8,128)(2,1)S(1)} collective-permute-done((bf16[2,128,256]{2,1,0:T(8,128)(2,1)S(1)}, bf16[2,128,256]{2,1,0:T(8,128)(2,1)S(1)}, u32[]{:S(2)}, u32[]{:S(2)}) %collective-permute-start.52) | collective-permute-done | bytes 131104 | tf_op jit(solution)/shard_map/ppermute | solution.py:55
  339.7 10.5 %collective-permute-done.53.refs_3_ = bf16[2,128,256]{2,1,0:T(8,128)(2,1)S(1)} collective-permute-done((bf16[2,128,256]{2,1,0:T(8,128)(2,1)S(1)}, bf16[2,128,256]{2,1,0:T(8,128)(2,1)S(1)}, u32[]{:S(2)}, u32[]{:S(2)}) %collective-permute-start.53) | collective-permute-done | bytes 131104 | tf_op jit(solution)/shard_map/ppermute | solution.py:55
  350.9 5.6 %project_back.1 = (bf16[256,256]{1,0:T(8,128)(2,1)}, bf16[2,128,1536]{2,1,0:T(8,128)(2,1)}) custom-call(bf16[2,128,256]{2,1,0:T(8,128)(2,1)} %get-tuple-element.392.refs_0_, bf16[2,128,256]{2,1,0:T(8,128)(2,1)} %copy-done.26, bf16[2,128,256]{2,1,0:T(8,128)(2,1)} %copy-done.27, bf16[2,128,256]{2,1,0:T(8,128)(2,1)} %copy-done.28, ...), custom_call_target="tpu_custom_call" | custom-call | flops 805306368 | bytes 3145728 | tf_op jit(solution)/shard_map/project_back/pallas_call | solution.py:743
  357.7 1.7 collective-permute-done.54.other_ref
  360.2 3.1 first_norm_back.1
  363.3 5.6 %attention_grads.1 = (bf16[2,384,1024]{2,1,0:T(8,128)(2,1)}, bf16[2,384,1024]{2,1,0:T(8,128)(2,1)}, bf16[2,384,896]{2,1,0:T(8,128)(2,1)}, bf16[2,384,896]{2,1,0:T(8,128)(2,1)}) custom-call(bf16[256,1536]{1,0:T(8,128)(2,1)} %get-tuple-element.282.a_ref, bf16[256,1536]{1,0:T(8,128)(2,1)} %bitcast.95, bf16[256,768]{1,0:T(8,128)(2,1)} %get-tuple-element.277.refs_4_.dq_ref, ...), custom_call_target="tpu_custom_call" | custom-call | flops 1509949440 | bytes 5898240 | tf_op jit(solution)/shard_map/attention_grads/pallas_call | solution.py:874
  373.2 28.2 %collective-permute-done.58 = bf16[2,384,896]{2,1,0:T(8,128)(2,1)} collective-permute-done((bf16[2,384,896]{2,1,0:T(8,128)(2,1)}, bf16[2,384,896]{2,1,0:T(8,128)(2,1)}, u32[]{:S(2)}, u32[]{:S(2)}) %collective-permute-start.58) | collective-permute-done | bytes 1376288 | tf_op jit(solution)/shard_map/ppermute | solution.py:55
  404.0 3.7 collective-permute-done.56
  409.0 12.4 %collective-permute-done.59 = bf16[1,384,896]{2,1,0:T(8,128)(2,1)S(1)} collective-permute-done((bf16[1,384,896]{2,1,0:T(8,128)(2,1)S(1)}, bf16[1,384,896]{2,1,0:T(8,128)(2,1)S(1)}, u32[]{:S(2)}, u32[]{:S(2)}) %collective-permute-start.59) | collective-permute-done | bytes 688160 | tf_op jit(solution)/shard_map/ppermute | solution.py:55
  422.7 2.8 collective-permute-done.57
  426.1 2.5 collective-permute-start.61
  430.6 14.1 %collective-permute-done.60 = bf16[96,1920]{1,0:T(8,128)(2,1)S(1)} collective-permute-done((bf16[96,1920]{1,0:T(8,128)(2,1)S(1)}, bf16[96,1920]{1,0:T(8,128)(2,1)S(1)}, u32[]{:S(2)}, u32[]{:S(2)}) %collective-permute-start.60) | collective-permute-done | bytes 368672 | tf_op jit(solution)/shard_map/ppermute | solution.py:55
  444.7 9.9 %collective-permute-done.61 = bf16[96,1920]{1,0:T(8,128)(2,1)S(1)} collective-permute-done((bf16[96,1920]{1,0:T(8,128)(2,1)S(1)}, bf16[96,1920]{1,0:T(8,128)(2,1)S(1)}, u32[]{:S(2)}, u32[]{:S(2)}) %collective-permute-start.61) | collective-permute-done | bytes 368672 | tf_op jit(solution)/shard_map/ppermute | solution.py:55
  454.6 9.5 %collective-permute-done.62 = bf16[96,1920]{1,0:T(8,128)(2,1)S(1)} collective-permute-done((bf16[96,1920]{1,0:T(8,128)(2,1)S(1)}, bf16[96,1920]{1,0:T(8,128)(2,1)S(1)}, u32[]{:S(2)}, u32[]{:S(2)}) %collective-permute-start.62) | collective-permute-done | bytes 368672 | tf_op jit(solution)/shard_map/ppermute | solution.py:55
  466.7 2.5 collective-permute-start.66
  470.7 10.1 %assemble.1 = (f32[8,384,384]{2,1,0:T(8,128)}, f32[8,384,384]{2,1,0:T(8,128)}, f32[8,384,384]{2,1,0:T(8,128)}) custom-call(bf16[4,2,2,3,192,384]{5,4,3,2,1,0:T(8,128)(2,1)} %bitcast.85), custom_call_target="tpu_custom_call" | custom-call | flops 3538944 | bytes 21233664 | tf_op jit(solution)/shard_map/assemble/pallas_call | solution.py:792
  480.8 3.3 collective-permute-done.65.refs_2_
  484.1 17.3 %collective-permute-done.66.refs_3_ = bf16[96,1920]{1,0:T(8,128)(2,1)} collective-permute-done((bf16[96,1920]{1,0:T(8,128)(2,1)S(1)}, bf16[96,1920]{1,0:T(8,128)(2,1)}, u32[]{:S(2)}, u32[]{:S(2)}) %collective-permute-start.66) | collective-permute-done | bytes 368672 | tf_op jit(solution)/shard_map/ppermute | solution.py:55
  501.4 3.4 assemble_attention.1
  504.9 1.9 slice_reduce_fusion
  (276 shorter events, 90.2 us)
Async XLA Ops:
  7.2 463.5 %all-gather.3.cloned.1.call-start = ((), (), s32[]{:S(2)}) async-start(), calls=%async_computation | async-start | bytes 8847360 | tf_op jit(solution)/shard_map/all_gather | solution.py:1076
  12.8 22.9 %collective-permute-start = (bf16[192,1152]{1,0:T(8,128)(2,1)}, bf16[192,1152]{1,0:T(8,128)(2,1)}, u32[]{:S(2)}, u32[]{:S(2)}) collective-permute-start(bf16[192,1152]{1,0:T(8,128)(2,1)} %get-tuple-element.170.rest_0_), channel_id=1, source_target_pairs={{0,8},{8,0},{16,24},{24,16},{1,9},{9,1},{17,25},{25,17},{2,10},{10... | collective-permute-start | bytes 1327112 | tf_op jit(solution)/shard_map/ppermute | solution.py:55
  14.3 21.4 %collective-permute-start.2 = (bf16[192,1152]{1,0:T(8,128)(2,1)}, bf16[192,1152]{1,0:T(8,128)(2,1)}, u32[]{:S(2)}, u32[]{:S(2)}) collective-permute-start(bf16[192,1152]{1,0:T(8,128)(2,1)} %get-tuple-element.170.rest_0_), channel_id=1, source_target_pairs={{0,16},{8,24},{16,0},{24,8},{1,17},{9,25},{17,1},{25,9},{2,18},{10... | collective-permute-start | bytes 1327112 | tf_op jit(solution)/shard_map/ppermute | solution.py:55
  15.8 19.8 %collective-permute-start.1 = (bf16[192,1152]{1,0:T(8,128)(2,1)}, bf16[192,1152]{1,0:T(8,128)(2,1)}, u32[]{:S(2)}, u32[]{:S(2)}) collective-permute-start(bf16[192,1152]{1,0:T(8,128)(2,1)} %get-tuple-element.171.rest_1_), channel_id=1, source_target_pairs={{0,8},{8,0},{16,24},{24,16},{1,9},{9,1},{17,25},{25,17},{2,10},{10... | collective-permute-start | bytes 1327112 | tf_op jit(solution)/shard_map/ppermute | solution.py:55
  16.4 19.4 %collective-permute-start.3 = (bf16[192,1152]{1,0:T(8,128)(2,1)}, bf16[192,1152]{1,0:T(8,128)(2,1)}, u32[]{:S(2)}, u32[]{:S(2)}) collective-permute-start(bf16[192,1152]{1,0:T(8,128)(2,1)} %get-tuple-element.171.rest_1_), channel_id=1, source_target_pairs={{0,16},{8,24},{16,0},{24,8},{1,17},{9,25},{17,1},{25,9},{2,18},{10... | collective-permute-start | bytes 1327112 | tf_op jit(solution)/shard_map/ppermute | solution.py:55
  35.7 11.1 %collective-permute-start.4 = (bf16[192,1152]{1,0:T(8,128)(2,1)}, bf16[192,1152]{1,0:T(8,128)(2,1)}, u32[]{:S(2)}, u32[]{:S(2)}) collective-permute-start(bf16[192,1152]{1,0:T(8,128)(2,1)} %collective-permute-done.rest_2_), channel_id=1, source_target_pairs={{0,16},{8,24},{16,0},{24,8},{1,17},{9,25},{17,1},{25,9},{2,18},{10... | collective-permute-start | bytes 1327112 | tf_op jit(solution)/shard_map/ppermute | solution.py:55
  37.3 10.8 %collective-permute-start.5 = (bf16[192,1152]{1,0:T(8,128)(2,1)}, bf16[192,1152]{1,0:T(8,128)(2,1)}, u32[]{:S(2)}, u32[]{:S(2)}) collective-permute-start(bf16[192,1152]{1,0:T(8,128)(2,1)} %collective-permute-done.3.rest_5_), channel_id=1, source_target_pairs={{0,8},{8,0},{16,24},{24,16},{1,9},{9,1},{17,25},{25,17},{2,10},{10... | collective-permute-start | bytes 1327112 | tf_op jit(solution)/shard_map/ppermute | solution.py:55
  48.1 25.4 %collective-permute-start.10 = (bf16[384,768]{1,0:T(8,128)(2,1)S(1)}, bf16[384,768]{1,0:T(8,128)(2,1)S(1)}, u32[]{:S(2)}, u32[]{:S(2)}) collective-permute-start(bf16[384,768]{1,0:T(8,128)(2,1)S(1)} %bitcast.89), channel_id=1, source_target_pairs={{0,16},{8,24},{16,0},{24,8},{1,17},{9,25},{17,1},{25,9},{2,18},{10... | collective-permute-start | bytes 1769480 | tf_op jit(solution)/shard_map/ppermute | solution.py:55
  48.6 24.9 %collective-permute-start.11 = (bf16[384,768]{1,0:T(8,128)(2,1)S(1)}, bf16[384,768]{1,0:T(8,128)(2,1)}, u32[]{:S(2)}, u32[]{:S(2)}) collective-permute-start(bf16[384,768]{1,0:T(8,128)(2,1)S(1)} %bitcast.90), channel_id=1, source_target_pairs={{0,24},{8,16},{16,8},{24,0},{1,25},{9,17},{17,9},{25,1},{2,26},{10... | collective-permute-start | bytes 1769480 | tf_op jit(solution)/shard_map/ppermute | solution.py:55
  51.1 23.8 %collective-permute-start.9 = (bf16[384,768]{1,0:T(8,128)(2,1)S(1)}, bf16[384,768]{1,0:T(8,128)(2,1)}, u32[]{:S(2)}, u32[]{:S(2)}) collective-permute-start(bf16[384,768]{1,0:T(8,128)(2,1)S(1)} %bitcast.91), channel_id=1, source_target_pairs={{0,8},{8,0},{16,24},{24,16},{1,9},{9,1},{17,25},{25,17},{2,10},{10... | collective-permute-start | bytes 1769480 | tf_op jit(solution)/shard_map/ppermute | solution.py:55
  57.3 5.2 %collective-permute-start.6 = (bf16[2,128,256]{2,1,0:T(8,128)(2,1)}, bf16[2,128,256]{2,1,0:T(8,128)(2,1)S(1)}, u32[]{:S(2)}, u32[]{:S(2)}) collective-permute-start(bf16[2,128,256]{2,1,0:T(8,128)(2,1)} %get-tuple-element.180), channel_id=1, source_target_pairs={{0,2},{2,0},{4,6},{6,4},{1,3},{3,1},{5,7},{7,5},{8,10},{10,8},{12,... | collective-permute-start | bytes 393224 | tf_op jit(solution)/shard_map/ppermute | solution.py:55
  57.8 8.7 %collective-permute-start.7 = (bf16[2,128,256]{2,1,0:T(8,128)(2,1)}, bf16[2,128,256]{2,1,0:T(8,128)(2,1)S(1)}, u32[]{:S(2)}, u32[]{:S(2)}) collective-permute-start(bf16[2,128,256]{2,1,0:T(8,128)(2,1)} %get-tuple-element.180), channel_id=1, source_target_pairs={{0,4},{2,6},{4,0},{6,2},{1,5},{3,7},{5,1},{7,3},{8,12},{10,14},{12... | collective-permute-start | bytes 393224 | tf_op jit(solution)/shard_map/ppermute | solution.py:55
  62.5 7.2 %collective-permute-start.8 = (bf16[2,128,256]{2,1,0:T(8,128)(2,1)}, bf16[2,128,256]{2,1,0:T(8,128)(2,1)S(1)}, u32[]{:S(2)}, u32[]{:S(2)}) collective-permute-start(bf16[2,128,256]{2,1,0:T(8,128)(2,1)} %get-tuple-element.180), channel_id=1, source_target_pairs={{0,6},{2,4},{4,2},{6,0},{1,7},{3,5},{5,3},{7,1},{8,14},{10,12},{12... | collective-permute-start | bytes 393224 | tf_op jit(solution)/shard_map/ppermute | solution.py:55
  74.8 22.6 %collective-permute-start.12 = (bf16[2,512,256]{2,1,0:T(8,128)(2,1)S(1)}, bf16[2,512,256]{2,1,0:T(8,128)(2,1)S(1)}, u32[]{:S(2)}, u32[]{:S(2)}) collective-permute-start(bf16[2,512,256]{2,1,0:T(8,128)(2,1)S(1)} %pad_maximum_fusion.5.rest_0_), channel_id=1, source_target_pairs={{0,8},{8,0},{16,24},{24,16},{1,9},{9,1},{17,25},{25,17},{2,10},{10... | collective-permute-start | bytes 1572872 | tf_op jit(solution)/shard_map/ppermute | solution.py:55
  76.3 23.3 %collective-permute-start.13 = (bf16[2,512,256]{2,1,0:T(8,128)(2,1)S(1)}, bf16[2,512,256]{2,1,0:T(8,128)(2,1)}, u32[]{:S(2)}, u32[]{:S(2)}) collective-permute-start(bf16[2,512,256]{2,1,0:T(8,128)(2,1)S(1)} %pad_maximum_fusion.5.rest_0_), channel_id=1, source_target_pairs={{0,16},{8,24},{16,0},{24,8},{1,17},{9,25},{17,1},{25,9},{2,18},{10... | collective-permute-start | bytes 1572872 | tf_op jit(solution)/shard_map/ppermute | solution.py:55
  77.4 22.2 %collective-permute-start.14 = (bf16[2,512,256]{2,1,0:T(8,128)(2,1)S(1)}, bf16[2,512,256]{2,1,0:T(8,128)(2,1)}, u32[]{:S(2)}, u32[]{:S(2)}) collective-permute-start(bf16[2,512,256]{2,1,0:T(8,128)(2,1)S(1)} %pad_maximum_fusion.5.rest_0_), channel_id=1, source_target_pairs={{0,24},{8,16},{16,8},{24,0},{1,25},{9,17},{17,9},{25,1},{2,26},{10... | collective-permute-start | bytes 1572872 | tf_op jit(solution)/shard_map/ppermute | solution.py:55
  78.3 13.1 %collective-permute-start.15 = (bf16[128,1664]{1,0:T(8,128)(2,1)}, bf16[128,1664]{1,0:T(8,128)(2,1)}, u32[]{:S(2)}, u32[]{:S(2)}) collective-permute-start(bf16[128,1664]{1,0:T(8,128)(2,1)} %convert_dynamic-update-slice_fusion.rest_8_.refs_8_.refs_6_), channel_id=1, source_target_pairs={{0,2},{2,0},{4,6},{6,4},{1,3},{3,1},{5,7},{7,5},{8,10},{10,8},{12,... | collective-permute-start | bytes 1277960 | tf_op jit(solution)/shard_map/ppermute | solution.py:55
  78.8 18.7 %collective-permute-start.16 = (bf16[128,1664]{1,0:T(8,128)(2,1)}, bf16[128,1664]{1,0:T(8,128)(2,1)}, u32[]{:S(2)}, u32[]{:S(2)}) collective-permute-start(bf16[128,1664]{1,0:T(8,128)(2,1)} %convert_dynamic-update-slice_fusion.rest_8_.refs_8_.refs_6_), channel_id=1, source_target_pairs={{0,6},{2,4},{4,2},{6,0},{1,7},{3,5},{5,3},{7,1},{8,14},{10,12},{12... | collective-permute-start | bytes 1277960 | tf_op jit(solution)/shard_map/ppermute | solution.py:55
  99.6 35.8 %collective-permute-start.25 = (bf16[2,3,384,384]{3,2,1,0:T(8,128)(2,1)S(1)}, bf16[2,3,384,384]{3,2,1,0:T(8,128)(2,1)S(1)}, u32[]{:S(2)}, u32[]{:S(2)}) collective-permute-start(bf16[2,3,384,384]{3,2,1,0:T(8,128)(2,1)S(1)} %pad_maximum_fusion.rest_16_), channel_id=1, source_target_pairs={{0,8},{8,0},{16,24},{24,16},{1,9},{9,1},{17,25},{25,17},{2,10},{10... | collective-permute-start | bytes 5308424 | tf_op jit(solution)/shard_map/ppermute | solution.py:55
  99.8 40.6 %collective-permute-start.26 = (bf16[2,3,384,384]{3,2,1,0:T(8,128)(2,1)S(1)}, bf16[2,3,384,384]{3,2,1,0:T(8,128)(2,1)}, u32[]{:S(2)}, u32[]{:S(2)}) collective-permute-start(bf16[2,3,384,384]{3,2,1,0:T(8,128)(2,1)S(1)} %pad_maximum_fusion.rest_16_), channel_id=1, source_target_pairs={{0,16},{8,24},{16,0},{24,8},{1,17},{9,25},{17,1},{25,9},{2,18},{10... | collective-permute-start | bytes 5308424 | tf_op jit(solution)/shard_map/ppermute | solution.py:55
  102.2 15.7 %collective-permute-start.18 = (bf16[128,1664]{1,0:T(8,128)(2,1)}, bf16[128,1664]{1,0:T(8,128)(2,1)}, u32[]{:S(2)}, u32[]{:S(2)}) collective-permute-start(bf16[128,1664]{1,0:T(8,128)(2,1)} %convert_dynamic-update-slice_fusion.rest_8_.refs_8_.refs_6_), channel_id=1, source_target_pairs={{0,4},{2,6},{4,0},{6,2},{1,5},{3,7},{5,1},{7,3},{8,12},{10,14},{12... | collective-permute-start | bytes 1277960 | tf_op jit(solution)/shard_map/ppermute | solution.py:55
  114.0 1.8 collective-permute-start.17
  114.1 7.1 %collective-permute-start.19 = (bf16[128,1664]{1,0:T(8,128)(2,1)}, bf16[128,1664]{1,0:T(8,128)(2,1)}, u32[]{:S(2)}, u32[]{:S(2)}) collective-permute-start(bf16[128,1664]{1,0:T(8,128)(2,1)} %convert_dynamic-update-slice_fusion.rest_8_.refs_8_.refs_6_), channel_id=1, source_target_pairs={{0,1},{1,0},{2,3},{3,2},{4,5},{5,4},{6,7},{7,6},{8,9},{9,8},{10,11... | collective-permute-start | bytes 1277960 | tf_op jit(solution)/shard_map/ppermute | solution.py:55
  115.8 5.4 %collective-permute-start.20 = (bf16[128,1664]{1,0:T(8,128)(2,1)}, bf16[128,1664]{1,0:T(8,128)(2,1)}, u32[]{:S(2)}, u32[]{:S(2)}) collective-permute-start(bf16[128,1664]{1,0:T(8,128)(2,1)} %collective-permute-done.15.rest_9_.refs_9_), channel_id=1, source_target_pairs={{0,1},{1,0},{2,3},{3,2},{4,5},{5,4},{6,7},{7,6},{8,9},{9,8},{10,11... | collective-permute-start | bytes 1277960 | tf_op jit(solution)/shard_map/ppermute | solution.py:55
  117.8 3.3 collective-permute-start.21
  121.2 20.6 %collective-permute-start.22 = (bf16[128,1536]{1,0:T(8,128)(2,1)}, bf16[128,1536]{1,0:T(8,128)(2,1)S(1)}, u32[]{:S(2)}, u32[]{:S(2)}) collective-permute-start(bf16[128,1536]{1,0:T(8,128)(2,1)} %get-tuple-element.206.rest_0_.refs_0_.refs_5_.b_ref), channel_id=1, source_target_pairs={{0,2},{2,0},{4,6},{6,4},{1,3},{3,1},{5,7},{7,5},{8,10},{10,8},{12,... | collective-permute-start | bytes 1179656 | tf_op jit(solution)/shard_map/ppermute | solution.py:55
  122.6 28.7 %collective-permute-start.23 = (bf16[128,1536]{1,0:T(8,128)(2,1)}, bf16[128,1536]{1,0:T(8,128)(2,1)S(1)}, u32[]{:S(2)}, u32[]{:S(2)}) collective-permute-start(bf16[128,1536]{1,0:T(8,128)(2,1)} %get-tuple-element.206.rest_0_.refs_0_.refs_5_.b_ref), channel_id=1, source_target_pairs={{0,4},{2,6},{4,0},{6,2},{1,5},{3,7},{5,1},{7,3},{8,12},{10,14},{12... | collective-permute-start | bytes 1179656 | tf_op jit(solution)/shard_map/ppermute | solution.py:55
  124.7 35.6 %collective-permute-start.24 = (bf16[128,1536]{1,0:T(8,128)(2,1)}, bf16[128,1536]{1,0:T(8,128)(2,1)S(1)}, u32[]{:S(2)}, u32[]{:S(2)}) collective-permute-start(bf16[128,1536]{1,0:T(8,128)(2,1)} %get-tuple-element.206.rest_0_.refs_0_.refs_5_.b_ref), channel_id=1, source_target_pairs={{0,6},{2,4},{4,2},{6,0},{1,7},{3,5},{5,3},{7,1},{8,14},{10,12},{12... | collective-permute-start | bytes 1179656 | tf_op jit(solution)/shard_map/ppermute | solution.py:55
  135.5 29.3 %collective-permute-start.32 = (bf16[2,3,192,384]{3,2,1,0:T(8,128)(2,1)S(1)}, bf16[2,3,192,384]{3,2,1,0:T(8,128)(2,1)S(1)}, u32[]{:S(2)}, u32[]{:S(2)}) collective-permute-start(bf16[2,3,192,384]{3,2,1,0:T(8,128)(2,1)S(1)} %slice.230), channel_id=1, source_target_pairs={{0,16},{8,24},{16,0},{24,8},{1,17},{9,25},{17,1},{25,9},{2,18},{10... | collective-permute-start | bytes 2654216 | tf_op jit(solution)/shard_map/ppermute | solution.py:55
  141.7 23.2 %collective-permute-start.33 = (bf16[2,3,192,384]{3,2,1,0:T(8,128)(2,1)S(1)}, bf16[2,3,192,384]{3,2,1,0:T(8,128)(2,1)S(1)}, u32[]{:S(2)}, u32[]{:S(2)}) collective-permute-start(bf16[2,3,192,384]{3,2,1,0:T(8,128)(2,1)S(1)} %slice.231), channel_id=1, source_target_pairs={{0,8},{8,0},{16,24},{24,16},{1,9},{9,1},{17,25},{25,17},{2,10},{10... | collective-permute-start | bytes 2654216 | tf_op jit(solution)/shard_map/ppermute | solution.py:55
  160.3 2.8 collective-permute-start.28
  160.8 4.1 collective-permute-start.31
  192.0 3.9 collective-permute-start.34
  198.6 25.6 %collective-permute-start.38 = (bf16[512,1536]{1,0:T(8,128)(2,1)}, bf16[512,1536]{1,0:T(8,128)(2,1)}, u32[]{:S(2)}, u32[]{:S(2)}) collective-permute-start(bf16[512,1536]{1,0:T(8,128)(2,1)} %get-tuple-element.236), channel_id=1, source_target_pairs={{0,1},{1,0},{2,3},{3,2},{4,5},{5,4},{6,7},{7,6},{8,9},{9,8},{10,11... | collective-permute-start | bytes 4718600 | tf_op jit(solution)/shard_map/ppermute | solution.py:55
  198.7 14.8 %collective-permute-start.35 = (bf16[128,1664]{1,0:T(8,128)(2,1)}, bf16[128,1664]{1,0:T(8,128)(2,1)S(1)}, u32[]{:S(2)}, u32[]{:S(2)}) collective-permute-start(bf16[128,1664]{1,0:T(8,128)(2,1)} %get-tuple-element.362), channel_id=1, source_target_pairs={{0,2},{2,0},{4,6},{6,4},{1,3},{3,1},{5,7},{7,5},{8,10},{10,8},{12,... | collective-permute-start | bytes 1277960 | tf_op jit(solution)/shard_map/ppermute | solution.py:55
  198.7 14.9 %collective-permute-start.36 = (bf16[128,1664]{1,0:T(8,128)(2,1)S(1)}, bf16[128,1664]{1,0:T(8,128)(2,1)S(1)}, u32[]{:S(2)}, u32[]{:S(2)}) collective-permute-start(bf16[128,1664]{1,0:T(8,128)(2,1)S(1)} %get-tuple-element.360), channel_id=1, source_target_pairs={{0,6},{2,4},{4,2},{6,0},{1,7},{3,5},{5,3},{7,1},{8,14},{10,12},{12... | collective-permute-start | bytes 1277960 | tf_op jit(solution)/shard_map/ppermute | solution.py:55
  214.5 53.9 %collective-permute-start.42 = (bf16[2,2,3,192,384]{4,3,2,1,0:T(8,128)(2,1)}, bf16[2,2,3,192,384]{4,3,2,1,0:T(8,128)(2,1)}, u32[]{:S(2)}, u32[]{:S(2)}) collective-permute-start(bf16[2,2,3,192,384]{4,3,2,1,0:T(8,128)(2,1)} %get-tuple-element.255), channel_id=1, source_target_pairs={{0,16},{8,24},{16,0},{24,8},{1,17},{9,25},{17,1},{25,9},{2,18},{10... | collective-permute-start | bytes 5308424 | tf_op jit(solution)/shard_map/ppermute | solution.py:55
  214.8 53.6 %collective-permute-start.43 = (bf16[2,2,3,192,384]{4,3,2,1,0:T(8,128)(2,1)}, bf16[2,2,3,192,384]{4,3,2,1,0:T(8,128)(2,1)S(1)}, u32[]{:S(2)}, u32[]{:S(2)}) collective-permute-start(bf16[2,2,3,192,384]{4,3,2,1,0:T(8,128)(2,1)} %get-tuple-element.256), channel_id=1, source_target_pairs={{0,8},{8,0},{16,24},{24,16},{1,9},{9,1},{17,25},{25,17},{2,10},{10... | collective-permute-start | bytes 5308424 | tf_op jit(solution)/shard_map/ppermute | solution.py:55
  215.3 26.2 %collective-permute-start.37 = (bf16[128,1664]{1,0:T(8,128)(2,1)}, bf16[128,1664]{1,0:T(8,128)(2,1)}, u32[]{:S(2)}, u32[]{:S(2)}) collective-permute-start(bf16[128,1664]{1,0:T(8,128)(2,1)} %get-tuple-element.361), channel_id=1, source_target_pairs={{0,4},{2,6},{4,0},{6,2},{1,5},{3,7},{5,1},{7,3},{8,12},{10,14},{12... | collective-permute-start | bytes 1277960 | tf_op jit(solution)/shard_map/ppermute | solution.py:55
  245.9 4.0 collective-permute-start.39
  245.9 14.6 %collective-permute-start.40 = (bf16[128,1536]{1,0:T(8,128)(2,1)}, bf16[128,1536]{1,0:T(8,128)(2,1)}, u32[]{:S(2)}, u32[]{:S(2)}) collective-permute-start(bf16[128,1536]{1,0:T(8,128)(2,1)} %get-tuple-element.252), channel_id=1, source_target_pairs={{0,2},{2,0},{4,6},{6,4},{1,3},{3,1},{5,7},{7,5},{8,10},{10,8},{12,... | collective-permute-start | bytes 1179656 | tf_op jit(solution)/shard_map/ppermute | solution.py:55
  248.4 19.9 %collective-permute-start.41 = (bf16[128,1536]{1,0:T(8,128)(2,1)}, bf16[128,1536]{1,0:T(8,128)(2,1)}, u32[]{:S(2)}, u32[]{:S(2)}) collective-permute-start(bf16[128,1536]{1,0:T(8,128)(2,1)} %get-tuple-element.253), channel_id=1, source_target_pairs={{0,6},{2,4},{4,2},{6,0},{1,7},{3,5},{5,3},{7,1},{8,14},{10,12},{12... | collective-permute-start | bytes 1179656 | tf_op jit(solution)/shard_map/ppermute | solution.py:55
  269.7 19.8 %collective-permute-start.44 = (bf16[1,2,3,192,384]{4,3,2,1,0:T(8,128)(2,1)S(1)}, bf16[1,2,3,192,384]{4,3,2,1,0:T(8,128)(2,1)S(1)}, u32[]{:S(2)}, u32[]{:S(2)}) collective-permute-start(bf16[1,2,3,192,384]{4,3,2,1,0:T(8,128)(2,1)S(1)} %add_convert_fusion.4), channel_id=1, source_target_pairs={{0,8},{8,0},{16,24},{24,16},{1,9},{9,1},{17,25},{25,17},{2,10},{10... | collective-permute-start | bytes 2654216 | tf_op jit(solution)/shard_map/ppermute | solution.py:55
  271.5 19.6 %collective-permute-start.45 = (bf16[1,2,3,192,384]{4,3,2,1,0:T(8,128)(2,1)S(1)}, bf16[1,2,3,192,384]{4,3,2,1,0:T(8,128)(2,1)S(1)}, u32[]{:S(2)}, u32[]{:S(2)}) collective-permute-start(bf16[1,2,3,192,384]{4,3,2,1,0:T(8,128)(2,1)S(1)} %add_convert_fusion.1), channel_id=1, source_target_pairs={{0,16},{8,24},{16,0},{24,8},{1,17},{9,25},{17,1},{25,9},{2,18},{10... | collective-permute-start | bytes 2654216 | tf_op jit(solution)/shard_map/ppermute | solution.py:55
  273.3 19.6 %collective-permute-start.46 = (bf16[128,1536]{1,0:T(8,128)(2,1)}, bf16[128,1536]{1,0:T(8,128)(2,1)}, u32[]{:S(2)}, u32[]{:S(2)}) collective-permute-start(bf16[128,1536]{1,0:T(8,128)(2,1)} %get-tuple-element.267), channel_id=1, source_target_pairs={{0,4},{2,6},{4,0},{6,2},{1,5},{3,7},{5,1},{7,3},{8,12},{10,14},{12... | collective-permute-start | bytes 1179656 | tf_op jit(solution)/shard_map/ppermute | solution.py:55
  293.0 14.9 %collective-permute-start.48 = (bf16[2,512,256]{2,1,0:T(8,128)(2,1)S(1)}, bf16[2,512,256]{2,1,0:T(8,128)(2,1)S(1)}, u32[]{:S(2)}, u32[]{:S(2)}) collective-permute-start(bf16[2,512,256]{2,1,0:T(8,128)(2,1)S(1)} %copy-done.39), channel_id=1, source_target_pairs={{0,8},{8,0},{16,24},{24,16},{1,9},{9,1},{17,25},{25,17},{2,10},{10... | collective-permute-start | bytes 1572872 | tf_op jit(solution)/shard_map/ppermute | solution.py:55
  294.5 21.4 %collective-permute-start.49 = (bf16[2,512,256]{2,1,0:T(8,128)(2,1)S(1)}, bf16[2,512,256]{2,1,0:T(8,128)(2,1)S(1)}, u32[]{:S(2)}, u32[]{:S(2)}) collective-permute-start(bf16[2,512,256]{2,1,0:T(8,128)(2,1)S(1)} %copy-done.38), channel_id=1, source_target_pairs={{0,16},{8,24},{16,0},{24,8},{1,17},{9,25},{17,1},{25,9},{2,18},{10... | collective-permute-start | bytes 1572872 | tf_op jit(solution)/shard_map/ppermute | solution.py:55
  296.2 20.3 %collective-permute-start.50 = (bf16[2,512,256]{2,1,0:T(8,128)(2,1)S(1)}, bf16[2,512,256]{2,1,0:T(8,128)(2,1)S(1)}, u32[]{:S(2)}, u32[]{:S(2)}) collective-permute-start(bf16[2,512,256]{2,1,0:T(8,128)(2,1)S(1)} %copy-done.37), channel_id=1, source_target_pairs={{0,24},{8,16},{16,8},{24,0},{1,25},{9,17},{17,9},{25,1},{2,26},{10... | collective-permute-start | bytes 1572872 | tf_op jit(solution)/shard_map/ppermute | solution.py:55
  317.5 16.2 %collective-permute-start.51 = (bf16[2,128,256]{2,1,0:T(8,128)(2,1)S(1)}, bf16[2,128,256]{2,1,0:T(8,128)(2,1)S(1)}, u32[]{:S(2)}, u32[]{:S(2)}) collective-permute-start(bf16[2,128,256]{2,1,0:T(8,128)(2,1)S(1)} %get-tuple-element.391), channel_id=1, source_target_pairs={{0,2},{2,0},{4,6},{6,4},{1,3},{3,1},{5,7},{7,5},{8,10},{10,8},{12,... | collective-permute-start | bytes 393224 | tf_op jit(solution)/shard_map/ppermute | solution.py:55
  321.9 17.9 %collective-permute-start.52 = (bf16[2,128,256]{2,1,0:T(8,128)(2,1)S(1)}, bf16[2,128,256]{2,1,0:T(8,128)(2,1)S(1)}, u32[]{:S(2)}, u32[]{:S(2)}) collective-permute-start(bf16[2,128,256]{2,1,0:T(8,128)(2,1)S(1)} %get-tuple-element.390), channel_id=1, source_target_pairs={{0,4},{2,6},{4,0},{6,2},{1,5},{3,7},{5,1},{7,3},{8,12},{10,14},{12... | collective-permute-start | bytes 393224 | tf_op jit(solution)/shard_map/ppermute | solution.py:55
  322.7 27.5 %collective-permute-start.53 = (bf16[2,128,256]{2,1,0:T(8,128)(2,1)S(1)}, bf16[2,128,256]{2,1,0:T(8,128)(2,1)S(1)}, u32[]{:S(2)}, u32[]{:S(2)}) collective-permute-start(bf16[2,128,256]{2,1,0:T(8,128)(2,1)S(1)} %get-tuple-element.389), channel_id=1, source_target_pairs={{0,6},{2,4},{4,2},{6,0},{1,7},{3,5},{5,3},{7,1},{8,14},{10,12},{12... | collective-permute-start | bytes 393224 | tf_op jit(solution)/shard_map/ppermute | solution.py:55
  357.6 1.8 collective-permute-start.54
  368.9 32.5 %collective-permute-start.58 = (bf16[2,384,896]{2,1,0:T(8,128)(2,1)}, bf16[2,384,896]{2,1,0:T(8,128)(2,1)}, u32[]{:S(2)}, u32[]{:S(2)}) collective-permute-start(bf16[2,384,896]{2,1,0:T(8,128)(2,1)} %get-tuple-element.291), channel_id=1, source_target_pairs={{0,8},{8,0},{16,24},{24,16},{1,9},{9,1},{17,25},{25,17},{2,10},{10... | collective-permute-start | bytes 4128776 | tf_op jit(solution)/shard_map/ppermute | solution.py:55
  370.2 37.5 %collective-permute-start.56 = (bf16[2,384,1024]{2,1,0:T(8,128)(2,1)}, bf16[2,384,1024]{2,1,0:T(8,128)(2,1)S(1)}, u32[]{:S(2)}, u32[]{:S(2)}) collective-permute-start(bf16[2,384,1024]{2,1,0:T(8,128)(2,1)} %get-tuple-element.289), channel_id=1, source_target_pairs={{0,16},{8,24},{16,0},{24,8},{1,17},{9,25},{17,1},{25,9},{2,18},{10... | collective-permute-start | bytes 4718600 | tf_op jit(solution)/shard_map/ppermute | solution.py:55
  373.1 35.6 %collective-permute-start.47 = (bf16[128,1536]{1,0:T(8,128)(2,1)S(1)}, bf16[128,1536]{1,0:T(8,128)(2,1)S(1)}, u32[]{:S(2)}, u32[]{:S(2)}) collective-permute-start(bf16[128,1536]{1,0:T(8,128)(2,1)S(1)} %add_convert_fusion.17), channel_id=1, source_target_pairs={{0,1},{1,0},{2,3},{3,2},{4,5},{5,4},{6,7},{7,6},{8,9},{9,8},{10,11... | collective-permute-start | bytes 1179656 | tf_op jit(solution)/shard_map/ppermute | solution.py:55
  402.7 18.6 %collective-permute-start.59 = (bf16[1,384,896]{2,1,0:T(8,128)(2,1)S(1)}, bf16[1,384,896]{2,1,0:T(8,128)(2,1)S(1)}, u32[]{:S(2)}, u32[]{:S(2)}) collective-permute-start(bf16[1,384,896]{2,1,0:T(8,128)(2,1)S(1)} %add_convert_fusion.10), channel_id=1, source_target_pairs={{0,16},{8,24},{16,0},{24,8},{1,17},{9,25},{17,1},{25,9},{2,18},{10... | collective-permute-start | bytes 2064392 | tf_op jit(solution)/shard_map/ppermute | solution.py:55
  408.0 17.4 %collective-permute-start.57 = (bf16[1,384,1024]{2,1,0:T(8,128)(2,1)S(1)}, bf16[1,384,1024]{2,1,0:T(8,128)(2,1)S(1)}, u32[]{:S(2)}, u32[]{:S(2)}) collective-permute-start(bf16[1,384,1024]{2,1,0:T(8,128)(2,1)S(1)} %add_convert_fusion.7), channel_id=1, source_target_pairs={{0,8},{8,0},{16,24},{24,16},{1,9},{9,1},{17,25},{25,17},{2,10},{10... | collective-permute-start | bytes 2359304 | tf_op jit(solution)/shard_map/ppermute | solution.py:55
  408.9 55.5 %collective-permute-start.55 = (f32[128,1536]{1,0:T(8,128)S(1)}, f32[128,1536]{1,0:T(8,128)S(1)}, u32[]{:S(2)}, u32[]{:S(2)}) collective-permute-start(f32[128,1536]{1,0:T(8,128)S(1)} %copy-done.11), channel_id=1, source_target_pairs={{0,1},{1,0},{2,3},{3,2},{4,5},{5,4},{6,7},{7,6},{8,9},{9,8},{10,11... | collective-permute-start | bytes 2359304 | tf_op jit(solution)/shard_map/ppermute | solution.py:55
  426.0 18.7 %collective-permute-start.60 = (bf16[96,1920]{1,0:T(8,128)(2,1)S(1)}, bf16[96,1920]{1,0:T(8,128)(2,1)S(1)}, u32[]{:S(2)}, u32[]{:S(2)}) collective-permute-start(bf16[96,1920]{1,0:T(8,128)(2,1)S(1)} %get-tuple-element.374), channel_id=1, source_target_pairs={{0,2},{2,0},{4,6},{6,4},{1,3},{3,1},{5,7},{7,5},{8,10},{10,8},{12,... | collective-permute-start | bytes 1105928 | tf_op jit(solution)/shard_map/ppermute | solution.py:55
  426.1 28.5 %collective-permute-start.61 = (bf16[96,1920]{1,0:T(8,128)(2,1)S(1)}, bf16[96,1920]{1,0:T(8,128)(2,1)S(1)}, u32[]{:S(2)}, u32[]{:S(2)}) collective-permute-start(bf16[96,1920]{1,0:T(8,128)(2,1)S(1)} %get-tuple-element.375), channel_id=1, source_target_pairs={{0,4},{2,6},{4,0},{6,2},{1,5},{3,7},{5,1},{7,3},{8,12},{10,14},{12... | collective-permute-start | bytes 1105928 | tf_op jit(solution)/shard_map/ppermute | solution.py:55
  428.6 35.5 %collective-permute-start.62 = (bf16[96,1920]{1,0:T(8,128)(2,1)S(1)}, bf16[96,1920]{1,0:T(8,128)(2,1)S(1)}, u32[]{:S(2)}, u32[]{:S(2)}) collective-permute-start(bf16[96,1920]{1,0:T(8,128)(2,1)S(1)} %get-tuple-element.376), channel_id=1, source_target_pairs={{0,6},{2,4},{4,2},{6,0},{1,7},{3,5},{5,3},{7,1},{8,14},{10,12},{12... | collective-permute-start | bytes 1105928 | tf_op jit(solution)/shard_map/ppermute | solution.py:55
  465.7 15.2 %collective-permute-start.64 = (bf16[96,1920]{1,0:T(8,128)(2,1)S(1)}, bf16[96,1920]{1,0:T(8,128)(2,1)S(1)}, u32[]{:S(2)}, u32[]{:S(2)}) collective-permute-start(bf16[96,1920]{1,0:T(8,128)(2,1)S(1)} %pad_maximum_fusion.6.refs_0_), channel_id=1, source_target_pairs={{0,2},{2,0},{4,6},{6,4},{1,3},{3,1},{5,7},{7,5},{8,10},{10,8},{12,... | collective-permute-start | bytes 1105928 | tf_op jit(solution)/shard_map/ppermute | solution.py:55
  465.7 18.4 %collective-permute-start.65 = (bf16[96,1920]{1,0:T(8,128)(2,1)S(1)}, bf16[96,1920]{1,0:T(8,128)(2,1)S(1)}, u32[]{:S(2)}, u32[]{:S(2)}) collective-permute-start(bf16[96,1920]{1,0:T(8,128)(2,1)S(1)} %pad_maximum_fusion.6.refs_0_), channel_id=1, source_target_pairs={{0,4},{2,6},{4,0},{6,2},{1,5},{3,7},{5,1},{7,3},{8,12},{10,14},{12... | collective-permute-start | bytes 1105928 | tf_op jit(solution)/shard_map/ppermute | solution.py:55
  466.7 34.7 %collective-permute-start.66 = (bf16[96,1920]{1,0:T(8,128)(2,1)S(1)}, bf16[96,1920]{1,0:T(8,128)(2,1)}, u32[]{:S(2)}, u32[]{:S(2)}) collective-permute-start(bf16[96,1920]{1,0:T(8,128)(2,1)S(1)} %pad_maximum_fusion.6.refs_0_), channel_id=1, source_target_pairs={{0,6},{2,4},{4,2},{6,0},{1,7},{3,5},{5,3},{7,1},{8,14},{10,12},{12... | collective-permute-start | bytes 1105928 | tf_op jit(solution)/shard_map/ppermute | solution.py:55
  (54 other events, 585.6 us)
Sparse Core Ops, SparseCore 0:
  293.1 139.1 all-gather.2

commit v4 on v3

--- a/solution.py
+++ b/solution.py
@@ -1040,7 +1040,7 @@
 
         sides, _, outs = hold((sides, sums, outs))
         grads = experts_grads(b_both, cx_both, b_at, part, sides, local_experts, F)
-        near = [k for k in range(C) if k != far]
+        near = list(range(C - 1))
         grads, back_near = hold((grads, [back_sums[0][k] for k in near]))
         for k, block in zip(near, back_near):
             back_sums[0][k] = block

time: 523 us -> 524 us (level)
  transfers between devices with their start and end apart: 68 -> 68, of which waited for: 41 -> 45; matrix products, arithmetic and copies ran while one was open for 8% -> 8% of each run, Pallas kernels for 13% -> 13%
where the time goes in v4:
time: 524 us; the launch traced here: 516 us
  waiting for transfers between devices  271 us (52%)
  Pallas kernels  97 us (19%)
  starting transfers between devices  72.6 us (14%)
  other arithmetic  35.2 us (7%)
  local copies, waits for them, and re-layouts  25.3 us (5%)
  between operations  15 us (3%)
    ppermute x67, waiting for transfers between devices, swap(): return lax.ppermute(value, axis, [(i, i ^ bit) for i in range(size)])  271 us
    ppermute x67, starting transfers between devices, swap(): return lax.ppermute(value, axis, [(i, i ^ bit) for i in range(size)])  72.6 us
    pallas_call x1, Pallas kernels, experts_rows(): pl.pallas_call(body, name='experts_rows', out_shape=(*[shape((half_rows,...  25.3 us
    pallas_call x1, Pallas kernels, experts_grads(): pl.pallas_call(body, name='experts_grads', out_shape=tuple([shape((half,...  13.3 us
    convert_element_type x11, other arithmetic, add_low(): return (left.astype(f32) + right.astype(f32)).astype(bf16)  12.2 us
    unnamed x106, local copies, waits for them, and re-layouts  10.6 us
  transfers between devices with their start and end apart: 68, of which 45 were waited for; matrix products, arithmetic and copies ran while one was open for 8% of the time, Pallas kernels for 13%

profile of v4, /device:TPU:8, one launch (start us, length us, event | category | flops | bytes accessed | tf_op | source)
XLA Modules:
  0.0 515.8 jit_solution(8686006658721236620)
XLA Ops:
  27.3 2.0 constant_dynamic-slice_fusion.6
  30.2 2.1 pad_maximum_fusion.3.x_ref
  32.2 3.4 select_convert_fusion.mask_ref
  42.3 4.5 collective-permute-done.4.rest_6_
  48.6 2.4 collective-permute-start.11
  51.6 5.7 %project_in.1 = (bf16[256,1536]{1,0:T(8,128)(2,1)}, bf16[2,768,128]{2,1,0:T(8,128)(2,1)}, bf16[2,128,256]{2,1,0:T(8,128)(2,1)}, bf16[1536,1152]{1,0:T(8,128)(2,1...) custom-call(bf16[256,1536]{1,0:T(8,128)(2,1)} %bitcast.84, f32[256,128]{1,0:T(8,128)} %pad_maximum_fusion.7.cos_ref.refs_5_, ...), custom_call_target="tpu_custom_call" | custom-call | flops 805306368 | bytes 6291456 | tf_op jit(solution)/shard_map/project_in/pallas_call | solution.py:226
  57.8 2.6 collective-permute-start.7
  60.4 2.1 collective-permute-done.6
  62.5 1.9 collective-permute-start.8
  64.5 2.0 collective-permute-done.7
  66.5 3.3 collective-permute-done.8
  70.7 2.8 collective-permute-done.10.rest_6_
  78.8 2.7 collective-permute-start.16
  81.5 9.9 %collective-permute-done.15.rest_9_.refs_9_ = bf16[128,1664]{1,0:T(8,128)(2,1)} collective-permute-done((bf16[128,1664]{1,0:T(8,128)(2,1)}, bf16[128,1664]{1,0:T(8,128)(2,1)}, u32[]{:S(2)}, u32[]{:S(2)}) %collective-permute-start.15) | collective-permute-done | bytes 426016 | tf_op jit(solution)/shard_map/ppermute | solution.py:55
  91.4 6.0 %collective-permute-done.16.rest_11_.refs_11_ = bf16[128,1664]{1,0:T(8,128)(2,1)} collective-permute-done((bf16[128,1664]{1,0:T(8,128)(2,1)}, bf16[128,1664]{1,0:T(8,128)(2,1)}, u32[]{:S(2)}, u32[]{:S(2)}) %collective-permute-start.16) | collective-permute-done | bytes 426016 | tf_op jit(solution)/shard_map/ppermute | solution.py:55
  97.4 2.2 collective-permute-done.13.rest_2_
  99.8 2.4 collective-permute-start.26
  102.2 2.6 collective-permute-start.18
  104.8 8.0 %attend.1 = (bf16[2,128,1536]{2,1,0:T(8,128)(2,1)}, bf16[2,128,768]{2,1,0:T(8,128)(2,1)}, f32[2,1,768]{2,1,0:T(1,128)}, bf16[1536,768]{1,0:T(8,128)(2,1)}) custom-call(s32[16]{0:T(128)} %reshape.190.seen_ref, bf16[2,768,128]{2,1,0:T(8,128)(2,1)} %get-tuple-element.178.q_ref, bf16[2,2048,128]{2,1,0:T(8,128)(2,1)} %select_convert_fusion.mask_ref, ...), custom_call_target="tpu_custom_call" | custom-call | flops 2214592512 | bytes 6815744 | tf_op jit(solution)/shard_map/attend/pallas_call | solution.py:302
  115.9 1.9 collective-permute-done.18.rest_10_.refs_10_
  118.4 2.7 second_norm.1
  122.6 2.1 collective-permute-start.23
  125.2 10.2 %collective-permute-done.25.rest_17_ = bf16[2,3,384,384]{3,2,1,0:T(8,128)(2,1)S(1)} collective-permute-done((bf16[2,3,384,384]{3,2,1,0:T(8,128)(2,1)S(1)}, bf16[2,3,384,384]{3,2,1,0:T(8,128)(2,1)S(1)}, u32[]{:S(2)}, u32[]{:S(2)}) %collective-permute-start.25) | collective-permute-done | bytes 1769504 | tf_op jit(solution)/shard_map/ppermute | solution.py:55
  136.4 4.0 collective-permute-done.26.rest_18_
  141.8 9.5 %collective-permute-done.23.rest_2_.refs_2_ = bf16[128,1536]{1,0:T(8,128)(2,1)S(1)} collective-permute-done((bf16[128,1536]{1,0:T(8,128)(2,1)}, bf16[128,1536]{1,0:T(8,128)(2,1)S(1)}, u32[]{:S(2)}, u32[]{:S(2)}) %collective-permute-start.23) | collective-permute-done | bytes 393248 | tf_op jit(solution)/shard_map/ppermute | solution.py:55
  151.4 8.9 %collective-permute-done.24.rest_3_.refs_3_ = bf16[128,1536]{1,0:T(8,128)(2,1)S(1)} collective-permute-done((bf16[128,1536]{1,0:T(8,128)(2,1)}, bf16[128,1536]{1,0:T(8,128)(2,1)S(1)}, u32[]{:S(2)}, u32[]{:S(2)}) %collective-permute-start.24) | collective-permute-done | bytes 393248 | tf_op jit(solution)/shard_map/ppermute | solution.py:55
  166.7 25.3 %experts_rows.1 = (bf16[512,1536]{1,0:T(8,128)(2,1)}, bf16[512,1536]{1,0:T(8,128)(2,1)}, bf16[512,1664]{1,0:T(8,128)(2,1)}, bf16[512,1664]{1,0:T(8,128)(2,1)}, b...) custom-call(s32[3]{0:T(128)} %pad_add_fusion.place_ref, ...), custom_call_target="tpu_custom_call" | custom-call | flops 14495514624 | bytes 19660800 | tf_op jit(solution)/shard_map/experts_rows/pallas_call | solution.py:460
  192.2 3.7 collective-permute-done.34
  195.9 2.7 add_convert_fusion.13
  198.7 3.0 collective-permute-start.36
  201.7 13.3 %experts_grads.1 = (bf16[2,2,3,192,384]{4,3,2,1,0:T(8,128)(2,1)}, bf16[2,2,3,192,384]{4,3,2,1,0:T(8,128)(2,1)}, bf16[2,2,3,192,384]{4,3,2,1,0:T(8,128)(2,1)}, bf16[2,2,3,192,384]{4,3,2,1,0:T(8,128)(2,1)}) custom-call(bf16[128,1536]{1,0:T(8,128)(2,1)} %get-tuple-element.206.rest_0_.refs_0_.refs_5_.b_ref, bf16[128,1536]{1,0:T(8,128)(2,1)} %copy-done.41, ...), custom_call_target="tpu_custom_call" | custom-call | flops 7247757312 | bytes 18087936 | tf_op jit(solution)/shard_map/experts_grads/pallas_call | solution.py:552
  215.0 3.0 collective-permute-done.35.refs_1_
  218.1 3.1 collective-permute-done.36.refs_2_
  223.3 2.6 add_convert_fusion.18
  226.0 16.9 %collective-permute-done.37.refs_3_ = bf16[128,1664]{1,0:T(8,128)(2,1)} collective-permute-done((bf16[128,1664]{1,0:T(8,128)(2,1)}, bf16[128,1664]{1,0:T(8,128)(2,1)}, u32[]{:S(2)}, u32[]{:S(2)}) %collective-permute-start.37) | collective-permute-done | bytes 426016 | tf_op jit(solution)/shard_map/ppermute | solution.py:55
  242.9 4.3 second_norm_back.1
  249.9 9.8 %attend_back.1 = (bf16[2,128,1536]{2,1,0:T(8,128)(2,1)}, bf16[256,768]{1,0:T(8,128)(2,1)}, bf16[2,512,256]{2,1,0:T(8,128)(2,1)}, bf16[2,512,256]{2,1,0:T(8,128)(...) custom-call(s32[3]{0:T(128)} %pad_add_fusion.place_ref, s32[16]{0:T(128)} %reshape.190.seen_ref, ...), custom_call_target="tpu_custom_call" | custom-call | flops 4026531840 | bytes 6553600 | tf_op jit(solution)/shard_map/attend_back/pallas_call | solution.py:695
  259.8 2.5 collective-permute-done.42
  263.7 2.2 collective-permute-start.44
  267.2 7.7 %collective-permute-start.46 = (bf16[128,1536]{1,0:T(8,128)(2,1)}, bf16[128,1536]{1,0:T(8,128)(2,1)}, u32[]{:S(2)}, u32[]{:S(2)}) collective-permute-start(bf16[128,1536]{1,0:T(8,128)(2,1)} %get-tuple-element.267), channel_id=1, source_target_pairs={{0,4},{2,6},{4,0},{6,2},{1,5},{3,7},{5,1},{7,3},{8,12},{10,14},{12... | collective-permute-start | bytes 1179656 | tf_op jit(solution)/shard_map/ppermute | solution.py:55
  274.8 11.0 %collective-permute-done.44 = bf16[1,2,3,192,384]{4,3,2,1,0:T(8,128)(2,1)S(1)} collective-permute-done((bf16[1,2,3,192,384]{4,3,2,1,0:T(8,128)(2,1)S(1)}, bf16[1,2,3,192,384]{4,3,2,1,0:T(8,128)(2,1)S(1)}, u32[]{:S(2)}, u32[]{:S(2)}) %collective-permute-start.44) | collective-permute-done | bytes 884768 | tf_op jit(solution)/shard_map/ppermute | solution.py:55
  293.6 11.3 %collective-permute-done.48 = bf16[2,512,256]{2,1,0:T(8,128)(2,1)S(1)} collective-permute-done((bf16[2,512,256]{2,1,0:T(8,128)(2,1)S(1)}, bf16[2,512,256]{2,1,0:T(8,128)(2,1)S(1)}, u32[]{:S(2)}, u32[]{:S(2)}) %collective-permute-start.48) | collective-permute-done | bytes 524320 | tf_op jit(solution)/shard_map/ppermute | solution.py:55
  304.9 10.6 %collective-permute-done.49 = bf16[2,512,256]{2,1,0:T(8,128)(2,1)S(1)} collective-permute-done((bf16[2,512,256]{2,1,0:T(8,128)(2,1)S(1)}, bf16[2,512,256]{2,1,0:T(8,128)(2,1)S(1)}, u32[]{:S(2)}, u32[]{:S(2)}) %collective-permute-start.49) | collective-permute-done | bytes 524320 | tf_op jit(solution)/shard_map/ppermute | solution.py:55
  316.4 4.7 collective-permute-start.51
  322.6 10.5 %collective-permute-done.51.refs_1_ = bf16[2,128,256]{2,1,0:T(8,128)(2,1)S(1)} collective-permute-done((bf16[2,128,256]{2,1,0:T(8,128)(2,1)S(1)}, bf16[2,128,256]{2,1,0:T(8,128)(2,1)S(1)}, u32[]{:S(2)}, u32[]{:S(2)}) %collective-permute-start.51) | collective-permute-done | bytes 131104 | tf_op jit(solution)/shard_map/ppermute | solution.py:55
  333.1 6.0 %collective-permute-done.52.refs_2_ = bf16[2,128,256]{2,1,0:T(8,128)(2,1)S(1)} collective-permute-done((bf16[2,128,256]{2,1,0:T(8,128)(2,1)S(1)}, bf16[2,128,256]{2,1,0:T(8,128)(2,1)S(1)}, u32[]{:S(2)}, u32[]{:S(2)}) %collective-permute-start.52) | collective-permute-done | bytes 131104 | tf_op jit(solution)/shard_map/ppermute | solution.py:55
  339.1 10.6 %collective-permute-done.53.refs_3_ = bf16[2,128,256]{2,1,0:T(8,128)(2,1)S(1)} collective-permute-done((bf16[2,128,256]{2,1,0:T(8,128)(2,1)S(1)}, bf16[2,128,256]{2,1,0:T(8,128)(2,1)S(1)}, u32[]{:S(2)}, u32[]{:S(2)}) %collective-permute-start.53) | collective-permute-done | bytes 131104 | tf_op jit(solution)/shard_map/ppermute | solution.py:55
  350.4 5.6 %project_back.1 = (bf16[256,256]{1,0:T(8,128)(2,1)}, bf16[2,128,1536]{2,1,0:T(8,128)(2,1)}) custom-call(bf16[2,128,256]{2,1,0:T(8,128)(2,1)} %get-tuple-element.392.refs_0_, bf16[2,128,256]{2,1,0:T(8,128)(2,1)} %copy-done.26, bf16[2,128,256]{2,1,0:T(8,128)(2,1)} %copy-done.27, bf16[2,128,256]{2,1,0:T(8,128)(2,1)} %copy-done.28, ...), custom_call_target="tpu_custom_call" | custom-call | flops 805306368 | bytes 3145728 | tf_op jit(solution)/shard_map/project_back/pallas_call | solution.py:743
  359.6 3.1 first_norm_back.1
  362.8 5.6 %attention_grads.1 = (bf16[2,384,1024]{2,1,0:T(8,128)(2,1)}, bf16[2,384,1024]{2,1,0:T(8,128)(2,1)}, bf16[2,384,896]{2,1,0:T(8,128)(2,1)}, bf16[2,384,896]{2,1,0:T(8,128)(2,1)}) custom-call(bf16[256,1536]{1,0:T(8,128)(2,1)} %get-tuple-element.282.a_ref, bf16[256,1536]{1,0:T(8,128)(2,1)} %bitcast.95, bf16[256,768]{1,0:T(8,128)(2,1)} %get-tuple-element.277.refs_4_.dq_ref, ...), custom_call_target="tpu_custom_call" | custom-call | flops 1509949440 | bytes 5898240 | tf_op jit(solution)/shard_map/attention_grads/pallas_call | solution.py:874
  373.0 27.9 %collective-permute-done.58 = bf16[2,384,896]{2,1,0:T(8,128)(2,1)} collective-permute-done((bf16[2,384,896]{2,1,0:T(8,128)(2,1)}, bf16[2,384,896]{2,1,0:T(8,128)(2,1)}, u32[]{:S(2)}, u32[]{:S(2)}) %collective-permute-start.58) | collective-permute-done | bytes 1376288 | tf_op jit(solution)/shard_map/ppermute | solution.py:55
  403.8 3.5 collective-permute-done.56
  408.5 12.4 %collective-permute-done.59 = bf16[1,384,896]{2,1,0:T(8,128)(2,1)S(1)} collective-permute-done((bf16[1,384,896]{2,1,0:T(8,128)(2,1)S(1)}, bf16[1,384,896]{2,1,0:T(8,128)(2,1)S(1)}, u32[]{:S(2)}, u32[]{:S(2)}) %collective-permute-start.59) | collective-permute-done | bytes 688160 | tf_op jit(solution)/shard_map/ppermute | solution.py:55
  422.3 2.8 collective-permute-done.57
  425.7 2.4 collective-permute-start.61
  430.2 13.6 %collective-permute-done.60 = bf16[96,1920]{1,0:T(8,128)(2,1)S(1)} collective-permute-done((bf16[96,1920]{1,0:T(8,128)(2,1)S(1)}, bf16[96,1920]{1,0:T(8,128)(2,1)S(1)}, u32[]{:S(2)}, u32[]{:S(2)}) %collective-permute-start.60) | collective-permute-done | bytes 368672 | tf_op jit(solution)/shard_map/ppermute | solution.py:55
  443.7 11.2 %collective-permute-done.61 = bf16[96,1920]{1,0:T(8,128)(2,1)S(1)} collective-permute-done((bf16[96,1920]{1,0:T(8,128)(2,1)S(1)}, bf16[96,1920]{1,0:T(8,128)(2,1)S(1)}, u32[]{:S(2)}, u32[]{:S(2)}) %collective-permute-start.61) | collective-permute-done | bytes 368672 | tf_op jit(solution)/shard_map/ppermute | solution.py:55
  454.9 9.5 %collective-permute-done.62 = bf16[96,1920]{1,0:T(8,128)(2,1)S(1)} collective-permute-done((bf16[96,1920]{1,0:T(8,128)(2,1)S(1)}, bf16[96,1920]{1,0:T(8,128)(2,1)S(1)}, u32[]{:S(2)}, u32[]{:S(2)}) %collective-permute-start.62) | collective-permute-done | bytes 368672 | tf_op jit(solution)/shard_map/ppermute | solution.py:55
  467.1 2.5 collective-permute-start.66
  471.1 10.1 %assemble.1 = (f32[8,384,384]{2,1,0:T(8,128)}, f32[8,384,384]{2,1,0:T(8,128)}, f32[8,384,384]{2,1,0:T(8,128)}) custom-call(bf16[4,2,2,3,192,384]{5,4,3,2,1,0:T(8,128)(2,1)} %bitcast.85), custom_call_target="tpu_custom_call" | custom-call | flops 3538944 | bytes 21233664 | tf_op jit(solution)/shard_map/assemble/pallas_call | solution.py:792
  481.2 3.3 collective-permute-done.65.refs_2_
  484.5 17.3 %collective-permute-done.66.refs_3_ = bf16[96,1920]{1,0:T(8,128)(2,1)} collective-permute-done((bf16[96,1920]{1,0:T(8,128)(2,1)S(1)}, bf16[96,1920]{1,0:T(8,128)(2,1)}, u32[]{:S(2)}, u32[]{:S(2)}) %collective-permute-start.66) | collective-permute-done | bytes 368672 | tf_op jit(solution)/shard_map/ppermute | solution.py:55
  501.8 3.4 assemble_attention.1
  505.2 1.9 slice_reduce_fusion
  (276 shorter events, 91.6 us)
Async XLA Ops:
  7.2 463.9 %all-gather.3.cloned.1.call-start = ((), (), s32[]{:S(2)}) async-start(), calls=%async_computation | async-start | bytes 8847360 | tf_op jit(solution)/shard_map/all_gather | solution.py:1076
  12.8 22.9 %collective-permute-start = (bf16[192,1152]{1,0:T(8,128)(2,1)}, bf16[192,1152]{1,0:T(8,128)(2,1)}, u32[]{:S(2)}, u32[]{:S(2)}) collective-permute-start(bf16[192,1152]{1,0:T(8,128)(2,1)} %get-tuple-element.170.rest_0_), channel_id=1, source_target_pairs={{0,8},{8,0},{16,24},{24,16},{1,9},{9,1},{17,25},{25,17},{2,10},{10... | collective-permute-start | bytes 1327112 | tf_op jit(solution)/shard_map/ppermute | solution.py:55
  14.3 21.4 %collective-permute-start.2 = (bf16[192,1152]{1,0:T(8,128)(2,1)}, bf16[192,1152]{1,0:T(8,128)(2,1)}, u32[]{:S(2)}, u32[]{:S(2)}) collective-permute-start(bf16[192,1152]{1,0:T(8,128)(2,1)} %get-tuple-element.170.rest_0_), channel_id=1, source_target_pairs={{0,16},{8,24},{16,0},{24,8},{1,17},{9,25},{17,1},{25,9},{2,18},{10... | collective-permute-start | bytes 1327112 | tf_op jit(solution)/shard_map/ppermute | solution.py:55
  15.8 19.8 %collective-permute-start.1 = (bf16[192,1152]{1,0:T(8,128)(2,1)}, bf16[192,1152]{1,0:T(8,128)(2,1)}, u32[]{:S(2)}, u32[]{:S(2)}) collective-permute-start(bf16[192,1152]{1,0:T(8,128)(2,1)} %get-tuple-element.171.rest_1_), channel_id=1, source_target_pairs={{0,8},{8,0},{16,24},{24,16},{1,9},{9,1},{17,25},{25,17},{2,10},{10... | collective-permute-start | bytes 1327112 | tf_op jit(solution)/shard_map/ppermute | solution.py:55
  16.4 19.4 %collective-permute-start.3 = (bf16[192,1152]{1,0:T(8,128)(2,1)}, bf16[192,1152]{1,0:T(8,128)(2,1)}, u32[]{:S(2)}, u32[]{:S(2)}) collective-permute-start(bf16[192,1152]{1,0:T(8,128)(2,1)} %get-tuple-element.171.rest_1_), channel_id=1, source_target_pairs={{0,16},{8,24},{16,0},{24,8},{1,17},{9,25},{17,1},{25,9},{2,18},{10... | collective-permute-start | bytes 1327112 | tf_op jit(solution)/shard_map/ppermute | solution.py:55
  35.7 11.1 %collective-permute-start.4 = (bf16[192,1152]{1,0:T(8,128)(2,1)}, bf16[192,1152]{1,0:T(8,128)(2,1)}, u32[]{:S(2)}, u32[]{:S(2)}) collective-permute-start(bf16[192,1152]{1,0:T(8,128)(2,1)} %collective-permute-done.rest_2_), channel_id=1, source_target_pairs={{0,16},{8,24},{16,0},{24,8},{1,17},{9,25},{17,1},{25,9},{2,18},{10... | collective-permute-start | bytes 1327112 | tf_op jit(solution)/shard_map/ppermute | solution.py:55
  37.3 10.8 %collective-permute-start.5 = (bf16[192,1152]{1,0:T(8,128)(2,1)}, bf16[192,1152]{1,0:T(8,128)(2,1)}, u32[]{:S(2)}, u32[]{:S(2)}) collective-permute-start(bf16[192,1152]{1,0:T(8,128)(2,1)} %collective-permute-done.3.rest_5_), channel_id=1, source_target_pairs={{0,8},{8,0},{16,24},{24,16},{1,9},{9,1},{17,25},{25,17},{2,10},{10... | collective-permute-start | bytes 1327112 | tf_op jit(solution)/shard_map/ppermute | solution.py:55
  48.1 25.4 %collective-permute-start.10 = (bf16[384,768]{1,0:T(8,128)(2,1)S(1)}, bf16[384,768]{1,0:T(8,128)(2,1)S(1)}, u32[]{:S(2)}, u32[]{:S(2)}) collective-permute-start(bf16[384,768]{1,0:T(8,128)(2,1)S(1)} %bitcast.89), channel_id=1, source_target_pairs={{0,16},{8,24},{16,0},{24,8},{1,17},{9,25},{17,1},{25,9},{2,18},{10... | collective-permute-start | bytes 1769480 | tf_op jit(solution)/shard_map/ppermute | solution.py:55
  48.6 24.9 %collective-permute-start.11 = (bf16[384,768]{1,0:T(8,128)(2,1)S(1)}, bf16[384,768]{1,0:T(8,128)(2,1)}, u32[]{:S(2)}, u32[]{:S(2)}) collective-permute-start(bf16[384,768]{1,0:T(8,128)(2,1)S(1)} %bitcast.90), channel_id=1, source_target_pairs={{0,24},{8,16},{16,8},{24,0},{1,25},{9,17},{17,9},{25,1},{2,26},{10... | collective-permute-start | bytes 1769480 | tf_op jit(solution)/shard_map/ppermute | solution.py:55
  51.1 23.8 %collective-permute-start.9 = (bf16[384,768]{1,0:T(8,128)(2,1)S(1)}, bf16[384,768]{1,0:T(8,128)(2,1)}, u32[]{:S(2)}, u32[]{:S(2)}) collective-permute-start(bf16[384,768]{1,0:T(8,128)(2,1)S(1)} %bitcast.91), channel_id=1, source_target_pairs={{0,8},{8,0},{16,24},{24,16},{1,9},{9,1},{17,25},{25,17},{2,10},{10... | collective-permute-start | bytes 1769480 | tf_op jit(solution)/shard_map/ppermute | solution.py:55
  57.3 5.2 %collective-permute-start.6 = (bf16[2,128,256]{2,1,0:T(8,128)(2,1)}, bf16[2,128,256]{2,1,0:T(8,128)(2,1)S(1)}, u32[]{:S(2)}, u32[]{:S(2)}) collective-permute-start(bf16[2,128,256]{2,1,0:T(8,128)(2,1)} %get-tuple-element.180), channel_id=1, source_target_pairs={{0,2},{2,0},{4,6},{6,4},{1,3},{3,1},{5,7},{7,5},{8,10},{10,8},{12,... | collective-permute-start | bytes 393224 | tf_op jit(solution)/shard_map/ppermute | solution.py:55
  57.8 8.7 %collective-permute-start.7 = (bf16[2,128,256]{2,1,0:T(8,128)(2,1)}, bf16[2,128,256]{2,1,0:T(8,128)(2,1)S(1)}, u32[]{:S(2)}, u32[]{:S(2)}) collective-permute-start(bf16[2,128,256]{2,1,0:T(8,128)(2,1)} %get-tuple-element.180), channel_id=1, source_target_pairs={{0,4},{2,6},{4,0},{6,2},{1,5},{3,7},{5,1},{7,3},{8,12},{10,14},{12... | collective-permute-start | bytes 393224 | tf_op jit(solution)/shard_map/ppermute | solution.py:55
  62.5 7.2 %collective-permute-start.8 = (bf16[2,128,256]{2,1,0:T(8,128)(2,1)}, bf16[2,128,256]{2,1,0:T(8,128)(2,1)S(1)}, u32[]{:S(2)}, u32[]{:S(2)}) collective-permute-start(bf16[2,128,256]{2,1,0:T(8,128)(2,1)} %get-tuple-element.180), channel_id=1, source_target_pairs={{0,6},{2,4},{4,2},{6,0},{1,7},{3,5},{5,3},{7,1},{8,14},{10,12},{12... | collective-permute-start | bytes 393224 | tf_op jit(solution)/shard_map/ppermute | solution.py:55
  74.8 22.6 %collective-permute-start.12 = (bf16[2,512,256]{2,1,0:T(8,128)(2,1)S(1)}, bf16[2,512,256]{2,1,0:T(8,128)(2,1)S(1)}, u32[]{:S(2)}, u32[]{:S(2)}) collective-permute-start(bf16[2,512,256]{2,1,0:T(8,128)(2,1)S(1)} %pad_maximum_fusion.5.rest_0_), channel_id=1, source_target_pairs={{0,8},{8,0},{16,24},{24,16},{1,9},{9,1},{17,25},{25,17},{2,10},{10... | collective-permute-start | bytes 1572872 | tf_op jit(solution)/shard_map/ppermute | solution.py:55
  76.3 23.3 %collective-permute-start.13 = (bf16[2,512,256]{2,1,0:T(8,128)(2,1)S(1)}, bf16[2,512,256]{2,1,0:T(8,128)(2,1)}, u32[]{:S(2)}, u32[]{:S(2)}) collective-permute-start(bf16[2,512,256]{2,1,0:T(8,128)(2,1)S(1)} %pad_maximum_fusion.5.rest_0_), channel_id=1, source_target_pairs={{0,16},{8,24},{16,0},{24,8},{1,17},{9,25},{17,1},{25,9},{2,18},{10... | collective-permute-start | bytes 1572872 | tf_op jit(solution)/shard_map/ppermute | solution.py:55
  77.4 22.2 %collective-permute-start.14 = (bf16[2,512,256]{2,1,0:T(8,128)(2,1)S(1)}, bf16[2,512,256]{2,1,0:T(8,128)(2,1)}, u32[]{:S(2)}, u32[]{:S(2)}) collective-permute-start(bf16[2,512,256]{2,1,0:T(8,128)(2,1)S(1)} %pad_maximum_fusion.5.rest_0_), channel_id=1, source_target_pairs={{0,24},{8,16},{16,8},{24,0},{1,25},{9,17},{17,9},{25,1},{2,26},{10... | collective-permute-start | bytes 1572872 | tf_op jit(solution)/shard_map/ppermute | solution.py:55
  78.3 13.1 %collective-permute-start.15 = (bf16[128,1664]{1,0:T(8,128)(2,1)}, bf16[128,1664]{1,0:T(8,128)(2,1)}, u32[]{:S(2)}, u32[]{:S(2)}) collective-permute-start(bf16[128,1664]{1,0:T(8,128)(2,1)} %convert_dynamic-update-slice_fusion.rest_8_.refs_8_.refs_6_), channel_id=1, source_target_pairs={{0,2},{2,0},{4,6},{6,4},{1,3},{3,1},{5,7},{7,5},{8,10},{10,8},{12,... | collective-permute-start | bytes 1277960 | tf_op jit(solution)/shard_map/ppermute | solution.py:55
  78.8 18.7 %collective-permute-start.16 = (bf16[128,1664]{1,0:T(8,128)(2,1)}, bf16[128,1664]{1,0:T(8,128)(2,1)}, u32[]{:S(2)}, u32[]{:S(2)}) collective-permute-start(bf16[128,1664]{1,0:T(8,128)(2,1)} %convert_dynamic-update-slice_fusion.rest_8_.refs_8_.refs_6_), channel_id=1, source_target_pairs={{0,6},{2,4},{4,2},{6,0},{1,7},{3,5},{5,3},{7,1},{8,14},{10,12},{12... | collective-permute-start | bytes 1277960 | tf_op jit(solution)/shard_map/ppermute | solution.py:55
  99.6 35.8 %collective-permute-start.25 = (bf16[2,3,384,384]{3,2,1,0:T(8,128)(2,1)S(1)}, bf16[2,3,384,384]{3,2,1,0:T(8,128)(2,1)S(1)}, u32[]{:S(2)}, u32[]{:S(2)}) collective-permute-start(bf16[2,3,384,384]{3,2,1,0:T(8,128)(2,1)S(1)} %pad_maximum_fusion.rest_16_), channel_id=1, source_target_pairs={{0,8},{8,0},{16,24},{24,16},{1,9},{9,1},{17,25},{25,17},{2,10},{10... | collective-permute-start | bytes 5308424 | tf_op jit(solution)/shard_map/ppermute | solution.py:55
  99.8 40.6 %collective-permute-start.26 = (bf16[2,3,384,384]{3,2,1,0:T(8,128)(2,1)S(1)}, bf16[2,3,384,384]{3,2,1,0:T(8,128)(2,1)}, u32[]{:S(2)}, u32[]{:S(2)}) collective-permute-start(bf16[2,3,384,384]{3,2,1,0:T(8,128)(2,1)S(1)} %pad_maximum_fusion.rest_16_), channel_id=1, source_target_pairs={{0,16},{8,24},{16,0},{24,8},{1,17},{9,25},{17,1},{25,9},{2,18},{10... | collective-permute-start | bytes 5308424 | tf_op jit(solution)/shard_map/ppermute | solution.py:55
  102.2 15.7 %collective-permute-start.18 = (bf16[128,1664]{1,0:T(8,128)(2,1)}, bf16[128,1664]{1,0:T(8,128)(2,1)}, u32[]{:S(2)}, u32[]{:S(2)}) collective-permute-start(bf16[128,1664]{1,0:T(8,128)(2,1)} %convert_dynamic-update-slice_fusion.rest_8_.refs_8_.refs_6_), channel_id=1, source_target_pairs={{0,4},{2,6},{4,0},{6,2},{1,5},{3,7},{5,1},{7,3},{8,12},{10,14},{12... | collective-permute-start | bytes 1277960 | tf_op jit(solution)/shard_map/ppermute | solution.py:55
  114.0 1.8 collective-permute-start.17
  114.1 7.1 %collective-permute-start.19 = (bf16[128,1664]{1,0:T(8,128)(2,1)}, bf16[128,1664]{1,0:T(8,128)(2,1)}, u32[]{:S(2)}, u32[]{:S(2)}) collective-permute-start(bf16[128,1664]{1,0:T(8,128)(2,1)} %convert_dynamic-update-slice_fusion.rest_8_.refs_8_.refs_6_), channel_id=1, source_target_pairs={{0,1},{1,0},{2,3},{3,2},{4,5},{5,4},{6,7},{7,6},{8,9},{9,8},{10,11... | collective-permute-start | bytes 1277960 | tf_op jit(solution)/shard_map/ppermute | solution.py:55
  115.8 5.4 %collective-permute-start.20 = (bf16[128,1664]{1,0:T(8,128)(2,1)}, bf16[128,1664]{1,0:T(8,128)(2,1)}, u32[]{:S(2)}, u32[]{:S(2)}) collective-permute-start(bf16[128,1664]{1,0:T(8,128)(2,1)} %collective-permute-done.15.rest_9_.refs_9_), channel_id=1, source_target_pairs={{0,1},{1,0},{2,3},{3,2},{4,5},{5,4},{6,7},{7,6},{8,9},{9,8},{10,11... | collective-permute-start | bytes 1277960 | tf_op jit(solution)/shard_map/ppermute | solution.py:55
  117.8 3.3 collective-permute-start.21
  121.2 20.6 %collective-permute-start.22 = (bf16[128,1536]{1,0:T(8,128)(2,1)}, bf16[128,1536]{1,0:T(8,128)(2,1)S(1)}, u32[]{:S(2)}, u32[]{:S(2)}) collective-permute-start(bf16[128,1536]{1,0:T(8,128)(2,1)} %get-tuple-element.206.rest_0_.refs_0_.refs_5_.b_ref), channel_id=1, source_target_pairs={{0,2},{2,0},{4,6},{6,4},{1,3},{3,1},{5,7},{7,5},{8,10},{10,8},{12,... | collective-permute-start | bytes 1179656 | tf_op jit(solution)/shard_map/ppermute | solution.py:55
  122.6 28.7 %collective-permute-start.23 = (bf16[128,1536]{1,0:T(8,128)(2,1)}, bf16[128,1536]{1,0:T(8,128)(2,1)S(1)}, u32[]{:S(2)}, u32[]{:S(2)}) collective-permute-start(bf16[128,1536]{1,0:T(8,128)(2,1)} %get-tuple-element.206.rest_0_.refs_0_.refs_5_.b_ref), channel_id=1, source_target_pairs={{0,4},{2,6},{4,0},{6,2},{1,5},{3,7},{5,1},{7,3},{8,12},{10,14},{12... | collective-permute-start | bytes 1179656 | tf_op jit(solution)/shard_map/ppermute | solution.py:55
  124.7 35.6 %collective-permute-start.24 = (bf16[128,1536]{1,0:T(8,128)(2,1)}, bf16[128,1536]{1,0:T(8,128)(2,1)S(1)}, u32[]{:S(2)}, u32[]{:S(2)}) collective-permute-start(bf16[128,1536]{1,0:T(8,128)(2,1)} %get-tuple-element.206.rest_0_.refs_0_.refs_5_.b_ref), channel_id=1, source_target_pairs={{0,6},{2,4},{4,2},{6,0},{1,7},{3,5},{5,3},{7,1},{8,14},{10,12},{12... | collective-permute-start | bytes 1179656 | tf_op jit(solution)/shard_map/ppermute | solution.py:55
  135.5 29.3 %collective-permute-start.32 = (bf16[2,3,192,384]{3,2,1,0:T(8,128)(2,1)S(1)}, bf16[2,3,192,384]{3,2,1,0:T(8,128)(2,1)S(1)}, u32[]{:S(2)}, u32[]{:S(2)}) collective-permute-start(bf16[2,3,192,384]{3,2,1,0:T(8,128)(2,1)S(1)} %slice.230), channel_id=1, source_target_pairs={{0,16},{8,24},{16,0},{24,8},{1,17},{9,25},{17,1},{25,9},{2,18},{10... | collective-permute-start | bytes 2654216 | tf_op jit(solution)/shard_map/ppermute | solution.py:55
  141.7 23.2 %collective-permute-start.33 = (bf16[2,3,192,384]{3,2,1,0:T(8,128)(2,1)S(1)}, bf16[2,3,192,384]{3,2,1,0:T(8,128)(2,1)S(1)}, u32[]{:S(2)}, u32[]{:S(2)}) collective-permute-start(bf16[2,3,192,384]{3,2,1,0:T(8,128)(2,1)S(1)} %slice.231), channel_id=1, source_target_pairs={{0,8},{8,0},{16,24},{24,16},{1,9},{9,1},{17,25},{25,17},{2,10},{10... | collective-permute-start | bytes 2654216 | tf_op jit(solution)/shard_map/ppermute | solution.py:55
  160.3 2.8 collective-permute-start.28
  160.8 4.1 collective-permute-start.31
  192.0 3.9 collective-permute-start.34
  198.6 24.7 %collective-permute-start.38 = (bf16[512,1536]{1,0:T(8,128)(2,1)}, bf16[512,1536]{1,0:T(8,128)(2,1)}, u32[]{:S(2)}, u32[]{:S(2)}) collective-permute-start(bf16[512,1536]{1,0:T(8,128)(2,1)} %get-tuple-element.236), channel_id=1, source_target_pairs={{0,1},{1,0},{2,3},{3,2},{4,5},{5,4},{6,7},{7,6},{8,9},{9,8},{10,11... | collective-permute-start | bytes 4718600 | tf_op jit(solution)/shard_map/ppermute | solution.py:55
  198.7 19.3 %collective-permute-start.35 = (bf16[128,1664]{1,0:T(8,128)(2,1)}, bf16[128,1664]{1,0:T(8,128)(2,1)S(1)}, u32[]{:S(2)}, u32[]{:S(2)}) collective-permute-start(bf16[128,1664]{1,0:T(8,128)(2,1)} %get-tuple-element.362), channel_id=1, source_target_pairs={{0,2},{2,0},{4,6},{6,4},{1,3},{3,1},{5,7},{7,5},{8,10},{10,8},{12,... | collective-permute-start | bytes 1277960 | tf_op jit(solution)/shard_map/ppermute | solution.py:55
  198.7 22.4 %collective-permute-start.36 = (bf16[128,1664]{1,0:T(8,128)(2,1)S(1)}, bf16[128,1664]{1,0:T(8,128)(2,1)S(1)}, u32[]{:S(2)}, u32[]{:S(2)}) collective-permute-start(bf16[128,1664]{1,0:T(8,128)(2,1)S(1)} %get-tuple-element.361), channel_id=1, source_target_pairs={{0,4},{2,6},{4,0},{6,2},{1,5},{3,7},{5,1},{7,3},{8,12},{10,14},{12... | collective-permute-start | bytes 1277960 | tf_op jit(solution)/shard_map/ppermute | solution.py:55
  221.9 40.3 %collective-permute-start.42 = (bf16[2,2,3,192,384]{4,3,2,1,0:T(8,128)(2,1)}, bf16[2,2,3,192,384]{4,3,2,1,0:T(8,128)(2,1)}, u32[]{:S(2)}, u32[]{:S(2)}) collective-permute-start(bf16[2,2,3,192,384]{4,3,2,1,0:T(8,128)(2,1)} %get-tuple-element.255), channel_id=1, source_target_pairs={{0,16},{8,24},{16,0},{24,8},{1,17},{9,25},{17,1},{25,9},{2,18},{10... | collective-permute-start | bytes 5308424 | tf_op jit(solution)/shard_map/ppermute | solution.py:55
  222.2 40.0 %collective-permute-start.43 = (bf16[2,2,3,192,384]{4,3,2,1,0:T(8,128)(2,1)}, bf16[2,2,3,192,384]{4,3,2,1,0:T(8,128)(2,1)S(1)}, u32[]{:S(2)}, u32[]{:S(2)}) collective-permute-start(bf16[2,2,3,192,384]{4,3,2,1,0:T(8,128)(2,1)} %get-tuple-element.256), channel_id=1, source_target_pairs={{0,8},{8,0},{16,24},{24,16},{1,9},{9,1},{17,25},{25,17},{2,10},{10... | collective-permute-start | bytes 5308424 | tf_op jit(solution)/shard_map/ppermute | solution.py:55
  222.8 20.1 %collective-permute-start.37 = (bf16[128,1664]{1,0:T(8,128)(2,1)}, bf16[128,1664]{1,0:T(8,128)(2,1)}, u32[]{:S(2)}, u32[]{:S(2)}) collective-permute-start(bf16[128,1664]{1,0:T(8,128)(2,1)} %get-tuple-element.360), channel_id=1, source_target_pairs={{0,6},{2,4},{4,2},{6,0},{1,7},{3,5},{5,3},{7,1},{8,14},{10,12},{12... | collective-permute-start | bytes 1277960 | tf_op jit(solution)/shard_map/ppermute | solution.py:55
  247.2 1.9 collective-permute-start.39
  247.2 12.5 %collective-permute-start.40 = (bf16[128,1536]{1,0:T(8,128)(2,1)}, bf16[128,1536]{1,0:T(8,128)(2,1)}, u32[]{:S(2)}, u32[]{:S(2)}) collective-permute-start(bf16[128,1536]{1,0:T(8,128)(2,1)} %get-tuple-element.252), channel_id=1, source_target_pairs={{0,2},{2,0},{4,6},{6,4},{1,3},{3,1},{5,7},{7,5},{8,10},{10,8},{12,... | collective-permute-start | bytes 1179656 | tf_op jit(solution)/shard_map/ppermute | solution.py:55
  247.3 12.5 %collective-permute-start.41 = (bf16[128,1536]{1,0:T(8,128)(2,1)}, bf16[128,1536]{1,0:T(8,128)(2,1)}, u32[]{:S(2)}, u32[]{:S(2)}) collective-permute-start(bf16[128,1536]{1,0:T(8,128)(2,1)} %get-tuple-element.253), channel_id=1, source_target_pairs={{0,6},{2,4},{4,2},{6,0},{1,7},{3,5},{5,3},{7,1},{8,14},{10,12},{12... | collective-permute-start | bytes 1179656 | tf_op jit(solution)/shard_map/ppermute | solution.py:55
  263.7 22.2 %collective-permute-start.44 = (bf16[1,2,3,192,384]{4,3,2,1,0:T(8,128)(2,1)S(1)}, bf16[1,2,3,192,384]{4,3,2,1,0:T(8,128)(2,1)S(1)}, u32[]{:S(2)}, u32[]{:S(2)}) collective-permute-start(bf16[1,2,3,192,384]{4,3,2,1,0:T(8,128)(2,1)S(1)} %add_convert_fusion.4), channel_id=1, source_target_pairs={{0,8},{8,0},{16,24},{24,16},{1,9},{9,1},{17,25},{25,17},{2,10},{10... | collective-permute-start | bytes 2654216 | tf_op jit(solution)/shard_map/ppermute | solution.py:55
  266.1 21.5 %collective-permute-start.45 = (bf16[1,2,3,192,384]{4,3,2,1,0:T(8,128)(2,1)S(1)}, bf16[1,2,3,192,384]{4,3,2,1,0:T(8,128)(2,1)S(1)}, u32[]{:S(2)}, u32[]{:S(2)}) collective-permute-start(bf16[1,2,3,192,384]{4,3,2,1,0:T(8,128)(2,1)S(1)} %add_convert_fusion.1), channel_id=1, source_target_pairs={{0,16},{8,24},{16,0},{24,8},{1,17},{9,25},{17,1},{25,9},{2,18},{10... | collective-permute-start | bytes 2654216 | tf_op jit(solution)/shard_map/ppermute | solution.py:55
  267.2 22.9 %collective-permute-start.46 = (bf16[128,1536]{1,0:T(8,128)(2,1)}, bf16[128,1536]{1,0:T(8,128)(2,1)}, u32[]{:S(2)}, u32[]{:S(2)}) collective-permute-start(bf16[128,1536]{1,0:T(8,128)(2,1)} %get-tuple-element.267), channel_id=1, source_target_pairs={{0,4},{2,6},{4,0},{6,2},{1,5},{3,7},{5,1},{7,3},{8,12},{10,14},{12... | collective-permute-start | bytes 1179656 | tf_op jit(solution)/shard_map/ppermute | solution.py:55
  290.1 14.8 %collective-permute-start.48 = (bf16[2,512,256]{2,1,0:T(8,128)(2,1)S(1)}, bf16[2,512,256]{2,1,0:T(8,128)(2,1)S(1)}, u32[]{:S(2)}, u32[]{:S(2)}) collective-permute-start(bf16[2,512,256]{2,1,0:T(8,128)(2,1)S(1)} %copy-done.39), channel_id=1, source_target_pairs={{0,8},{8,0},{16,24},{24,16},{1,9},{9,1},{17,25},{25,17},{2,10},{10... | collective-permute-start | bytes 1572872 | tf_op jit(solution)/shard_map/ppermute | solution.py:55
  291.0 24.4 %collective-permute-start.49 = (bf16[2,512,256]{2,1,0:T(8,128)(2,1)S(1)}, bf16[2,512,256]{2,1,0:T(8,128)(2,1)S(1)}, u32[]{:S(2)}, u32[]{:S(2)}) collective-permute-start(bf16[2,512,256]{2,1,0:T(8,128)(2,1)S(1)} %copy-done.38), channel_id=1, source_target_pairs={{0,16},{8,24},{16,0},{24,8},{1,17},{9,25},{17,1},{25,9},{2,18},{10... | collective-permute-start | bytes 1572872 | tf_op jit(solution)/shard_map/ppermute | solution.py:55
  292.0 23.5 %collective-permute-start.50 = (bf16[2,512,256]{2,1,0:T(8,128)(2,1)S(1)}, bf16[2,512,256]{2,1,0:T(8,128)(2,1)S(1)}, u32[]{:S(2)}, u32[]{:S(2)}) collective-permute-start(bf16[2,512,256]{2,1,0:T(8,128)(2,1)S(1)} %copy-done.37), channel_id=1, source_target_pairs={{0,24},{8,16},{16,8},{24,0},{1,25},{9,17},{17,9},{25,1},{2,26},{10... | collective-permute-start | bytes 1572872 | tf_op jit(solution)/shard_map/ppermute | solution.py:55
  316.4 16.7 %collective-permute-start.51 = (bf16[2,128,256]{2,1,0:T(8,128)(2,1)S(1)}, bf16[2,128,256]{2,1,0:T(8,128)(2,1)S(1)}, u32[]{:S(2)}, u32[]{:S(2)}) collective-permute-start(bf16[2,128,256]{2,1,0:T(8,128)(2,1)S(1)} %get-tuple-element.391), channel_id=1, source_target_pairs={{0,2},{2,0},{4,6},{6,4},{1,3},{3,1},{5,7},{7,5},{8,10},{10,8},{12,... | collective-permute-start | bytes 393224 | tf_op jit(solution)/shard_map/ppermute | solution.py:55
  321.1 18.0 %collective-permute-start.52 = (bf16[2,128,256]{2,1,0:T(8,128)(2,1)S(1)}, bf16[2,128,256]{2,1,0:T(8,128)(2,1)S(1)}, u32[]{:S(2)}, u32[]{:S(2)}) collective-permute-start(bf16[2,128,256]{2,1,0:T(8,128)(2,1)S(1)} %get-tuple-element.390), channel_id=1, source_target_pairs={{0,4},{2,6},{4,0},{6,2},{1,5},{3,7},{5,1},{7,3},{8,12},{10,14},{12... | collective-permute-start | bytes 393224 | tf_op jit(solution)/shard_map/ppermute | solution.py:55
  322.1 27.6 %collective-permute-start.53 = (bf16[2,128,256]{2,1,0:T(8,128)(2,1)S(1)}, bf16[2,128,256]{2,1,0:T(8,128)(2,1)S(1)}, u32[]{:S(2)}, u32[]{:S(2)}) collective-permute-start(bf16[2,128,256]{2,1,0:T(8,128)(2,1)S(1)} %get-tuple-element.389), channel_id=1, source_target_pairs={{0,6},{2,4},{4,2},{6,0},{1,7},{3,5},{5,3},{7,1},{8,14},{10,12},{12... | collective-permute-start | bytes 393224 | tf_op jit(solution)/shard_map/ppermute | solution.py:55
  357.1 1.8 collective-permute-start.54
  368.4 32.5 %collective-permute-start.58 = (bf16[2,384,896]{2,1,0:T(8,128)(2,1)}, bf16[2,384,896]{2,1,0:T(8,128)(2,1)}, u32[]{:S(2)}, u32[]{:S(2)}) collective-permute-start(bf16[2,384,896]{2,1,0:T(8,128)(2,1)} %get-tuple-element.291), channel_id=1, source_target_pairs={{0,8},{8,0},{16,24},{24,16},{1,9},{9,1},{17,25},{25,17},{2,10},{10... | collective-permute-start | bytes 4128776 | tf_op jit(solution)/shard_map/ppermute | solution.py:55
  369.8 37.5 %collective-permute-start.56 = (bf16[2,384,1024]{2,1,0:T(8,128)(2,1)}, bf16[2,384,1024]{2,1,0:T(8,128)(2,1)S(1)}, u32[]{:S(2)}, u32[]{:S(2)}) collective-permute-start(bf16[2,384,1024]{2,1,0:T(8,128)(2,1)} %get-tuple-element.289), channel_id=1, source_target_pairs={{0,16},{8,24},{16,0},{24,8},{1,17},{9,25},{17,1},{25,9},{2,18},{10... | collective-permute-start | bytes 4718600 | tf_op jit(solution)/shard_map/ppermute | solution.py:55
  372.9 35.4 %collective-permute-start.47 = (bf16[128,1536]{1,0:T(8,128)(2,1)S(1)}, bf16[128,1536]{1,0:T(8,128)(2,1)S(1)}, u32[]{:S(2)}, u32[]{:S(2)}) collective-permute-start(bf16[128,1536]{1,0:T(8,128)(2,1)S(1)} %add_convert_fusion.17), channel_id=1, source_target_pairs={{0,1},{1,0},{2,3},{3,2},{4,5},{5,4},{6,7},{7,6},{8,9},{9,8},{10,11... | collective-permute-start | bytes 1179656 | tf_op jit(solution)/shard_map/ppermute | solution.py:55
  402.2 18.7 %collective-permute-start.59 = (bf16[1,384,896]{2,1,0:T(8,128)(2,1)S(1)}, bf16[1,384,896]{2,1,0:T(8,128)(2,1)S(1)}, u32[]{:S(2)}, u32[]{:S(2)}) collective-permute-start(bf16[1,384,896]{2,1,0:T(8,128)(2,1)S(1)} %add_convert_fusion.10), channel_id=1, source_target_pairs={{0,16},{8,24},{16,0},{24,8},{1,17},{9,25},{17,1},{25,9},{2,18},{10... | collective-permute-start | bytes 2064392 | tf_op jit(solution)/shard_map/ppermute | solution.py:55
  407.6 17.5 %collective-permute-start.57 = (bf16[1,384,1024]{2,1,0:T(8,128)(2,1)S(1)}, bf16[1,384,1024]{2,1,0:T(8,128)(2,1)S(1)}, u32[]{:S(2)}, u32[]{:S(2)}) collective-permute-start(bf16[1,384,1024]{2,1,0:T(8,128)(2,1)S(1)} %add_convert_fusion.7), channel_id=1, source_target_pairs={{0,8},{8,0},{16,24},{24,16},{1,9},{9,1},{17,25},{25,17},{2,10},{10... | collective-permute-start | bytes 2359304 | tf_op jit(solution)/shard_map/ppermute | solution.py:55
  408.4 56.3 %collective-permute-start.55 = (f32[128,1536]{1,0:T(8,128)S(1)}, f32[128,1536]{1,0:T(8,128)S(1)}, u32[]{:S(2)}, u32[]{:S(2)}) collective-permute-start(f32[128,1536]{1,0:T(8,128)S(1)} %copy-done.11), channel_id=1, source_target_pairs={{0,1},{1,0},{2,3},{3,2},{4,5},{5,4},{6,7},{7,6},{8,9},{9,8},{10,11... | collective-permute-start | bytes 2359304 | tf_op jit(solution)/shard_map/ppermute | solution.py:55
  425.6 18.1 %collective-permute-start.60 = (bf16[96,1920]{1,0:T(8,128)(2,1)S(1)}, bf16[96,1920]{1,0:T(8,128)(2,1)S(1)}, u32[]{:S(2)}, u32[]{:S(2)}) collective-permute-start(bf16[96,1920]{1,0:T(8,128)(2,1)S(1)} %get-tuple-element.374), channel_id=1, source_target_pairs={{0,2},{2,0},{4,6},{6,4},{1,3},{3,1},{5,7},{7,5},{8,10},{10,8},{12,... | collective-permute-start | bytes 1105928 | tf_op jit(solution)/shard_map/ppermute | solution.py:55
  425.7 29.2 %collective-permute-start.61 = (bf16[96,1920]{1,0:T(8,128)(2,1)S(1)}, bf16[96,1920]{1,0:T(8,128)(2,1)S(1)}, u32[]{:S(2)}, u32[]{:S(2)}) collective-permute-start(bf16[96,1920]{1,0:T(8,128)(2,1)S(1)} %get-tuple-element.375), channel_id=1, source_target_pairs={{0,4},{2,6},{4,0},{6,2},{1,5},{3,7},{5,1},{7,3},{8,12},{10,14},{12... | collective-permute-start | bytes 1105928 | tf_op jit(solution)/shard_map/ppermute | solution.py:55
  428.1 36.4 %collective-permute-start.62 = (bf16[96,1920]{1,0:T(8,128)(2,1)S(1)}, bf16[96,1920]{1,0:T(8,128)(2,1)S(1)}, u32[]{:S(2)}, u32[]{:S(2)}) collective-permute-start(bf16[96,1920]{1,0:T(8,128)(2,1)S(1)} %get-tuple-element.376), channel_id=1, source_target_pairs={{0,6},{2,4},{4,2},{6,0},{1,7},{3,5},{5,3},{7,1},{8,14},{10,12},{12... | collective-permute-start | bytes 1105928 | tf_op jit(solution)/shard_map/ppermute | solution.py:55
  466.0 15.2 %collective-permute-start.64 = (bf16[96,1920]{1,0:T(8,128)(2,1)S(1)}, bf16[96,1920]{1,0:T(8,128)(2,1)S(1)}, u32[]{:S(2)}, u32[]{:S(2)}) collective-permute-start(bf16[96,1920]{1,0:T(8,128)(2,1)S(1)} %pad_maximum_fusion.6.refs_0_), channel_id=1, source_target_pairs={{0,2},{2,0},{4,6},{6,4},{1,3},{3,1},{5,7},{7,5},{8,10},{10,8},{12,... | collective-permute-start | bytes 1105928 | tf_op jit(solution)/shard_map/ppermute | solution.py:55
  466.1 18.4 %collective-permute-start.65 = (bf16[96,1920]{1,0:T(8,128)(2,1)S(1)}, bf16[96,1920]{1,0:T(8,128)(2,1)S(1)}, u32[]{:S(2)}, u32[]{:S(2)}) collective-permute-start(bf16[96,1920]{1,0:T(8,128)(2,1)S(1)} %pad_maximum_fusion.6.refs_0_), channel_id=1, source_target_pairs={{0,4},{2,6},{4,0},{6,2},{1,5},{3,7},{5,1},{7,3},{8,12},{10,14},{12... | collective-permute-start | bytes 1105928 | tf_op jit(solution)/shard_map/ppermute | solution.py:55
  467.1 34.7 %collective-permute-start.66 = (bf16[96,1920]{1,0:T(8,128)(2,1)S(1)}, bf16[96,1920]{1,0:T(8,128)(2,1)}, u32[]{:S(2)}, u32[]{:S(2)}) collective-permute-start(bf16[96,1920]{1,0:T(8,128)(2,1)S(1)} %pad_maximum_fusion.6.refs_0_), channel_id=1, source_target_pairs={{0,6},{2,4},{4,2},{6,0},{1,7},{3,5},{5,3},{7,1},{8,14},{10,12},{12... | collective-permute-start | bytes 1105928 | tf_op jit(solution)/shard_map/ppermute | solution.py:55
  (54 other events, 579.5 us)
Sparse Core Ops, SparseCore 0:
  290.2 143.2 all-gather.2
